TPU v7x, 32 devices: a whole 2x2x4 slice. The times are simulated.
32 devices in a mesh: dp: 4 (over y, core), lat: 8 (over z, x).
Axes of the slice: x: 2, y: 2, z: 4, core: 2. Of those that a mesh axis runs over, the one named last changes fastest.
Arguments:
- inputs: bfloat16 [4, 96, 180, 768], P('dp', 'lat'), may hold values from -6 to 6
- cotangent: bfloat16 [4, 96, 180, 768], P('dp', 'lat'), may hold values from -6 to 6
- storm_weight: int32 [4], P('dp'), may hold values from 32 to 192
- norm_gain: float32 [768], replicated, may hold values from 0.5 to 1.5
- norm_shift: float32 [768], replicated, may hold values from -1 to 1
- inner_weight: bfloat16 [2, 8, 96, 96], replicated, may hold values from -0.4375 to 0.4375
- inner_bias: float32 [2, 8, 96], replicated, may hold values from -0.1 to 0.1
- outer_weight: bfloat16 [2, 8, 96, 96], replicated, may hold values from -0.4375 to 0.4375
- outer_bias: float32 [2, 8, 96], replicated, may hold values from -0.05 to 0.05
- post_gain: float32 [768], replicated, may hold values from 0.5 to 1.5
- post_shift: float32 [768], replicated, may hold values from -1 to 1
- expand_weight: bfloat16 [768, 3072], replicated, may hold values from -0.21875 to 0.21875
- expand_bias: float32 [3072], replicated, may hold values from -0.5 to 0.5
- reduce_weight: bfloat16 [3072, 768], replicated, may hold values from -0.109375 to 0.109375
- reduce_bias: float32 [768], replicated, may hold values from -0.5 to 0.5
Outputs:
- layer_out: bfloat16 [4, 96, 180, 768], P('dp', 'lat')
- input_grad: float32 [4, 96, 180, 768], P('dp', 'lat')
- norm_gain_grad: float32 [768], replicated
- norm_shift_grad: float32 [768], replicated
- inner_weight_grad: float32 [2, 8, 96, 96], replicated
- inner_bias_grad: float32 [2, 8, 96], replicated
- outer_weight_grad: float32 [2, 8, 96, 96], replicated
- outer_bias_grad: float32 [2, 8, 96], replicated
- post_gain_grad: float32 [768], replicated
- post_shift_grad: float32 [768], replicated
- expand_weight_grad: float32 [768, 3072], replicated
- expand_bias_grad: float32 [3072], replicated
- reduce_weight_grad: float32 [3072, 768], replicated
- reduce_bias_grad: float32 [768], replicated
All inputs are finite; a program needn't handle non-finite values.
Results may differ from a plain program's by a relative error of at most 0.017.
The roundings to bfloat16 on the way count: a program that leaves them out, or rounds other values in their place, can miss the bound.
Values may be sent and summed in bfloat16 or wider, within the bound.
A program may use at most 320 MiB of HBM per device.

v0:
```python
from functools import partial
import math

import jax
import jax.numpy as jnp
from jax import lax
from jax.sharding import PartitionSpec as P

BLOCKS = 8
LAT = 90
LON = 180
LAT_PAD = 96
LON_PAD = 96


shrink_level = 0.01
epsilon = 1e-06


def make_tables():
    mode_ids = jnp.arange(LON_PAD, dtype=jnp.int32)
    columns = jnp.arange(LON, dtype=jnp.int32)
    phases = (columns[:, None] * mode_ids[None, :] % LON).astype(jnp.float32) * (
        2.0 * math.pi / LON
    )
    kept_modes = (mode_ids < LON // 2 + 1).astype(jnp.float32)
    factor = (
        jnp.where((mode_ids == 0) | (mode_ids == LON // 2), 1.0, 2.0).astype(jnp.float32)
        * kept_modes
    )
    scaling = 1.0 / math.sqrt(LON)
    forward_lon = (
        jnp.stack([jnp.cos(phases) * kept_modes, -jnp.sin(phases) * kept_modes], axis=1) * scaling
    )
    inverse_lon = jnp.stack([jnp.cos(phases) * factor, -jnp.sin(phases) * factor], axis=1) * scaling
    row_ids = jnp.arange(LAT_PAD, dtype=jnp.int32)
    angles = (row_ids[:, None] * row_ids[None, :] % LAT).astype(jnp.float32) * (2.0 * math.pi / LAT)
    inside = ((row_ids[:, None] < LAT) & (row_ids[None, :] < LAT)).astype(jnp.float32) / math.sqrt(
        LAT
    )
    cosine = jnp.cos(angles) * inside
    sine_part = jnp.sin(angles) * inside
    forward_lat = jnp.stack(
        [jnp.stack([cosine, sine_part], axis=1), jnp.stack([-sine_part, cosine], axis=1)], axis=0
    )
    inverse_lat = jnp.stack(
        [jnp.stack([cosine, -sine_part], axis=1), jnp.stack([sine_part, cosine], axis=1)], axis=0
    )
    return (
        forward_lon.astype(jnp.bfloat16),
        inverse_lon.astype(jnp.bfloat16),
        forward_lat.astype(jnp.bfloat16),
        inverse_lat.astype(jnp.bfloat16),
    )


def layer_norm(values, gain, shift):
    center = jnp.mean(values, axis=-1, keepdims=True)
    spread = jnp.mean(jnp.square(values - center), axis=-1, keepdims=True)
    return (values - center) * lax.rsqrt(spread + epsilon) * gain + shift


def soft_shrink(values):
    return values - shrink_level * jnp.tanh(values / shrink_level)


def gelu_exact(values):
    return jax.nn.gelu(values, approximate=False)


def split_blocks(spectrum):
    samples, modes_k, _, modes_m, width = spectrum.shape
    block_shape = (samples, modes_k, modes_m, BLOCKS, width // BLOCKS)
    return (spectrum[:, :, 0].reshape(block_shape), spectrum[:, :, 1].reshape(block_shape))


def join_blocks(real, imag):
    samples, modes_k, modes_m, _, _ = real.shape
    flat_shape = (samples, modes_k, modes_m, real.shape[3] * real.shape[4])
    return jnp.stack([real.reshape(flat_shape), imag.reshape(flat_shape)], axis=2)


def complex_mix(real, imag, weight, bias):
    product = partial(jnp.einsum, "skmbi,bio->skmbo", preferred_element_type=jnp.float32)
    return (
        product(real, weight[0]) - product(imag, weight[1]) + bias[0],
        product(imag, weight[0]) + product(real, weight[1]) + bias[1],
    )


def mix_back(real, imag, weight, grad_re, grad_im):
    contract = partial(jnp.einsum, "skmbi,skmbo->bio", preferred_element_type=jnp.float32)
    weight_first = contract(real, grad_re) + contract(imag, grad_im)
    weight_second = contract(real, grad_im) - contract(imag, grad_re)
    bias_grad = jnp.stack(
        [
            jnp.sum(grad_re, axis=(0, 1, 2), dtype=jnp.float32),
            jnp.sum(grad_im, axis=(0, 1, 2), dtype=jnp.float32),
        ],
        axis=0,
    )
    backward = partial(jnp.einsum, "skmbo,bio->skmbi", preferred_element_type=jnp.float32)
    input_re = backward(grad_re, weight[0]) + backward(grad_im, weight[1])
    input_im = backward(grad_im, weight[0]) - backward(grad_re, weight[1])
    return (jnp.stack([weight_first, weight_second], axis=0), bias_grad, input_re, input_im)


def shards(
    inputs,
    cotangent,
    storm_weight,
    norm_gain,
    norm_shift,
    inner_weight,
    inner_bias,
    outer_weight,
    outer_bias,
    post_gain,
    post_shift,
    expand_weight,
    expand_bias,
    reduce_weight,
    reduce_bias,
):
    slab_rows = inputs.shape[1]
    width = inputs.shape[3]
    row_ids = lax.axis_index("lat") * slab_rows + jnp.arange(slab_rows, dtype=jnp.int32)
    row_keep = (row_ids < LAT).astype(jnp.float32)
    forward_lon, inverse_lon, forward_lat, inverse_lat = make_tables()
    values = inputs.astype(jnp.float32)
    first, norm_pull = jax.vjp(layer_norm, values, norm_gain, norm_shift)
    first_low = first.astype(jnp.bfloat16)
    lon_spec = jnp.einsum(
        "srwc,wqm->srqmc", first_low, forward_lon, preferred_element_type=jnp.float32
    ).astype(jnp.bfloat16)
    mode_slab = lax.all_to_all(lon_spec, "lat", split_axis=3, concat_axis=1, tiled=True)
    freq = jnp.einsum(
        "qkpr,srpmc->skqmc", forward_lat, mode_slab, preferred_element_type=jnp.float32
    ).astype(jnp.bfloat16)
    freq_re, freq_im = split_blocks(freq)
    inner_re, inner_im = complex_mix(freq_re, freq_im, inner_weight, inner_bias)
    hidden_re_full, inner_re_pull = jax.vjp(gelu_exact, inner_re)
    hidden_im_full, inner_im_pull = jax.vjp(gelu_exact, inner_im)
    hidden_re = hidden_re_full.astype(jnp.bfloat16)
    hidden_im = hidden_im_full.astype(jnp.bfloat16)
    outer_re, outer_im = complex_mix(hidden_re, hidden_im, outer_weight, outer_bias)
    shrunk_re, outer_re_pull = jax.vjp(soft_shrink, outer_re)
    shrunk_im, outer_im_pull = jax.vjp(soft_shrink, outer_im)
    shrunk = join_blocks(shrunk_re.astype(jnp.bfloat16), shrunk_im.astype(jnp.bfloat16))
    back_slab = jnp.einsum(
        "qrpk,skpmc->srqmc", inverse_lat, shrunk, preferred_element_type=jnp.float32
    ).astype(jnp.bfloat16)
    row_spec = lax.all_to_all(back_slab, "lat", split_axis=1, concat_axis=3, tiled=True)
    filtered = jnp.einsum(
        "wqm,srqmc->srwc", inverse_lon, row_spec, preferred_element_type=jnp.float32
    )
    mixed = filtered + first + values
    second, post_pull = jax.vjp(layer_norm, mixed, post_gain, post_shift)
    second_low = second.astype(jnp.bfloat16).reshape(-1, width)
    pre_act = jnp.dot(second_low, expand_weight, preferred_element_type=jnp.float32) + expand_bias
    activ, gelu_pull = jax.vjp(gelu_exact, pre_act)
    activ_low = activ.astype(jnp.bfloat16)
    branch = jnp.dot(activ_low, reduce_weight, preferred_element_type=jnp.float32) + reduce_bias
    total = mixed + branch.reshape(mixed.shape)
    layer_out = (total * row_keep[None, :, None, None]).astype(jnp.bfloat16)
    sample_scale = storm_weight.astype(jnp.float32) / 64.0
    upstream = (
        cotangent.astype(jnp.float32)
        * sample_scale[:, None, None, None]
        * row_keep[None, :, None, None]
    )
    up_low = upstream.astype(jnp.bfloat16).reshape(-1, width)
    reduce_bias_grad = jnp.sum(up_low, axis=0, dtype=jnp.float32)
    reduce_weight_grad = jnp.dot(activ_low.T, up_low, preferred_element_type=jnp.float32)
    activ_grad = jnp.dot(up_low, reduce_weight.T, preferred_element_type=jnp.float32)
    pre_grad = gelu_pull(activ_grad)[0].astype(jnp.bfloat16)
    expand_bias_grad = jnp.sum(pre_grad, axis=0, dtype=jnp.float32)
    expand_weight_grad = jnp.dot(second_low.T, pre_grad, preferred_element_type=jnp.float32)
    second_grad = jnp.dot(pre_grad, expand_weight.T, preferred_element_type=jnp.float32).reshape(
        mixed.shape
    )
    mixed_norm_grad, post_gain_grad, post_shift_grad = post_pull(second_grad)
    mixed_grad = upstream + mixed_norm_grad
    filt_low = mixed_grad.astype(jnp.bfloat16)
    row_grad = jnp.einsum(
        "wqm,srwc->srqmc", inverse_lon, filt_low, preferred_element_type=jnp.float32
    ).astype(jnp.bfloat16)
    mode_grad = lax.all_to_all(row_grad, "lat", split_axis=3, concat_axis=1, tiled=True)
    merged_grad = jnp.einsum(
        "qrpk,srqmc->skpmc", inverse_lat, mode_grad, preferred_element_type=jnp.float32
    )
    merged_re, merged_im = split_blocks(merged_grad)
    outer_re_grad = outer_re_pull(merged_re)[0].astype(jnp.bfloat16)
    outer_im_grad = outer_im_pull(merged_im)[0].astype(jnp.bfloat16)
    outer_weight_grad, outer_bias_grad, hidden_re_grad, hidden_im_grad = mix_back(
        hidden_re, hidden_im, outer_weight, outer_re_grad, outer_im_grad
    )
    inner_re_grad = inner_re_pull(hidden_re_grad)[0].astype(jnp.bfloat16)
    inner_im_grad = inner_im_pull(hidden_im_grad)[0].astype(jnp.bfloat16)
    inner_weight_grad, inner_bias_grad, freq_re_grad, freq_im_grad = mix_back(
        freq_re, freq_im, inner_weight, inner_re_grad, inner_im_grad
    )
    freq_grad = join_blocks(freq_re_grad.astype(jnp.bfloat16), freq_im_grad.astype(jnp.bfloat16))
    slab_grad = jnp.einsum(
        "qkpr,skqmc->srpmc", forward_lat, freq_grad, preferred_element_type=jnp.float32
    ).astype(jnp.bfloat16)
    lon_grad = lax.all_to_all(slab_grad, "lat", split_axis=1, concat_axis=3, tiled=True)
    first_grad = (
        jnp.einsum("wqm,srqmc->srwc", forward_lon, lon_grad, preferred_element_type=jnp.float32)
        + mixed_grad
    )
    values_grad, norm_gain_grad, norm_shift_grad = norm_pull(first_grad)
    input_grad = values_grad + mixed_grad
    grads = (
        norm_gain_grad,
        norm_shift_grad,
        inner_weight_grad,
        inner_bias_grad,
        outer_weight_grad,
        outer_bias_grad,
        post_gain_grad,
        post_shift_grad,
        expand_weight_grad,
        expand_bias_grad,
        reduce_weight_grad,
        reduce_bias_grad,
    )
    summed = lax.psum(
        (
            grads[0],
            grads[1],
            grads[2],
            grads[3],
            grads[4],
            grads[5],
            grads[6],
            grads[7],
            grads[8],
            grads[9],
            grads[10],
            grads[11],
        ),
        ("dp", "lat"),
    )
    return (
        layer_out,
        input_grad,
        summed[0],
        summed[1],
        summed[2],
        summed[3],
        summed[4],
        summed[5],
        summed[6],
        summed[7],
        summed[8],
        summed[9],
        summed[10],
        summed[11],
    )


def solution(mesh):
    return jax.shard_map(
        shards,
        mesh=mesh,
        in_specs=(
            P("dp", "lat", None, None),
            P("dp", "lat", None, None),
            P("dp"),
            P(),
            P(),
            P(),
            P(),
            P(),
            P(),
            P(),
            P(),
            P(),
            P(),
            P(),
            P(),
        ),
        out_specs=(
            P("dp", "lat", None, None),
            P("dp", "lat", None, None),
            P(),
            P(),
            P(),
            P(),
            P(),
            P(),
            P(),
            P(),
            P(),
            P(),
            P(),
            P(),
        ),
        check_vma=False,
    )
```

profile of v0, /device:TPU:0, one launch (start us, length us, event | category | flops | bytes accessed | tf_op | source)
XLA Modules:
  0.0 1046.4 jit_solution(9826930769798211330)
XLA Ops:
  19.7 7.5 all-to-all-start
  30.7 75.5 %all-to-all-done = bf16[1,12,2,96,768]{4,2,1,0,3:T(2,128)(2,1)S(1)} async-done(((bf16[1,12,2,96,768]{4,2,1,0,3:T(2,128)(2,1)}), bf16[1,12,2,96,768]{4,2,1,0,3:T(2,128)(2,1)S(1)}, u32[]{:S(2)}, u32[]{:S(2)}) %all-to-all-start) | async-done | bytes 3538976 | tf_op jit(solution)/shard_map/all_to_all | solution.py:136
  135.1 11.1 %fusion.115 = (bf16[96,12,8,96]{3,0,1,2:T(8,128)(2,1)S(1)}, f32[1,96,12,8,96]{4,1,2,3,0:T(8,128)}) fusion(f32[8,96,1,96,12]{1,3,4,0,2:T(8,128)S(1)} %bitcast_add_fusion.4), kind=kLoop, calls=%fused_computation.168 | loop fusion | flops 57507840 | bytes 8847360 | tf_op jit(solution)/shard_map/reshape.13
  147.2 11.1 %fusion.116 = (bf16[96,12,8,96]{3,0,1,2:T(8,128)(2,1)S(1)}, f32[1,96,12,8,96]{4,1,2,3,0:T(8,128)}) fusion(f32[8,96,1,96,12]{1,3,4,0,2:T(8,128)S(1)} %bitcast_add_fusion.3), kind=kLoop, calls=%fused_computation.169 | loop fusion | flops 57507840 | bytes 8847360 | tf_op jit(solution)/shard_map/reshape.34
  173.5 5.7 subtract_convert_fusion.1
  208.3 67.5 %all-to-all-done.1 = bf16[1,96,2,12,768]{4,2,3,0,1:T(2,128)(2,1)} async-done(((bf16[1,96,2,12,768]{4,2,3,0,1:T(2,128)(2,1)}), bf16[1,96,2,12,768]{4,2,3,0,1:T(2,128)(2,1)}, u32[]{:S(2)}, u32[]{:S(2)}) %all-to-all-start.1) | async-done | bytes 3538976 | tf_op jit(solution)/shard_map/all_to_all | solution.py:153
  295.9 71.0 %multiply_convert_fusion = (bf16[2160,3072]{1,0:T(8,128)(2,1)}, f32[2160,3072]{1,0:T(8,128)}, f32[2160,3072]{1,0:T(8,128)}) fusion(f32[3072]{0:T(1024)S(1)} %copy-done.78, bf16[2160,768]{1,0:T(8,128)(2,1)} %reshape.768, bf16[768,3072]{1,0:T(8,128)(2,1)} %param.26), kind=kOutput, calls=%fused_computation.4 | convolution fusion | flops 10630103040 | bytes 74403840 | tf_op jit(solution)/shard_map/dot_general | solution.py:160
  366.9 29.7 %convert_reduce_fusion = (f32[3072]{0:T(1024)}, bf16[2160,3072]{1,0:T(8,128)(2,1)}) fusion(f32[2160,3072]{1,0:T(8,128)} %get-tuple-element.97, bf16[2160,768]{1,0:T(8,128)(2,1)S(1)} %copy-done.27, bf16[3072,768]{1,0:T(8,128)(2,1)} %param.28, f32[2160,3072]{1,0:T(8,128)} %get-tuple-element.131, f32[3072]{0:T(1024)S(1)} %copy-done.78), kind=kOutput, calls=%fused_computation.2 | convolution fusion | flops 10304959488 | bytes 74416128 | tf_op jit(solution)/shard_map/dot_general | solution.py:175
  396.6 16.4 %fusion.285 = (f32[768]{0:T(1024)}, f32[2160]{0:T(1024)S(1)}, f32[2160,768]{1,0:T(8,128)}) fusion(f32[2160]{0:T(1024)S(1)} %copy-done.69, f32[768]{0:T(1024)S(1)} %copy-done.59, bf16[2160,3072]{1,0:T(8,128)(2,1)} %get-tuple-element.139, bf16[768,3072]{1,0:T(8,128)(2,1)S(1)} %copy-done.77), kind=kOutput, calls=%fused_computation.331 | convolution fusion | flops 10198791168 | bytes 24648576 | tf_op jit(solution)/shard_map/dot_general | solution.py:179
  413.0 7.3 reshape.771
  420.3 7.6 multiply_reduce_fusion
  429.4 16.7 %convolution_add_fusion = f32[2160,768]{1,0:T(8,128)} fusion(bf16[2160,3072]{1,0:T(8,128)(2,1)} %get-tuple-element.96, bf16[3072,768]{1,0:T(8,128)(2,1)} %param.28, f32[768]{0:T(1024)S(1)} %copy-done.79), kind=kOutput, calls=%fused_computation.55 | convolution fusion | flops 10193817600 | bytes 24628224 | tf_op jit(solution)/shard_map/dot_general | solution.py:163
  446.2 7.5 reshape.769
  453.7 9.9 add_add_fusion
  476.8 18.1 %fusion.293 = f32[768,3072]{1,0:T(8,128)} fusion(bf16[2160,768]{1,0:T(8,128)(2,1)} %reshape.768, bf16[2160,3072]{1,0:T(8,128)(2,1)} %get-tuple-element.139), kind=kOutput, calls=%fused_computation.335 | convolution fusion | flops 10192158720 | bytes 26025984 | tf_op jit(solution)/shard_map/dot_general | solution.py:178
  494.9 16.9 %fusion.294 = f32[3072,768]{1,0:T(8,128)} fusion(bf16[2160,3072]{1,0:T(8,128)(2,1)} %get-tuple-element.96, bf16[2160,768]{1,0:T(8,128)(2,1)S(1)} %copy-done.28), kind=kOutput, calls=%fused_computation.336 | convolution fusion | flops 10192158720 | bytes 26025984 | tf_op jit(solution)/shard_map/dot_general | solution.py:174
  511.8 44.3 %all-to-all-done.2 = bf16[1,12,2,96,768]{4,2,1,0,3:T(2,128)(2,1)S(1)} async-done(((bf16[1,12,2,96,768]{4,2,1,0,3:T(2,128)(2,1)}), bf16[1,12,2,96,768]{4,2,1,0,3:T(2,128)(2,1)S(1)}, u32[]{:S(2)}, u32[]{:S(2)}) %all-to-all-start.2) | async-done | bytes 3538976 | tf_op jit(solution)/shard_map/all_to_all | solution.py:188
  603.9 5.7 convert_reduce_fusion.5
  643.0 117.1 %all-to-all-done.3 = bf16[1,96,2,12,768]{4,2,3,0,1:T(2,128)(2,1)} async-done(((bf16[1,96,2,12,768]{4,2,3,0,1:T(2,128)(2,1)}), bf16[1,96,2,12,768]{4,2,3,0,1:T(2,128)(2,1)}, u32[]{:S(2)}, u32[]{:S(2)}) %all-to-all-start.3) | async-done | bytes 3538976 | tf_op jit(solution)/shard_map/all_to_all | solution.py:207
  765.2 7.1 fusion.19
  776.2 8.1 copy.168
  784.4 41.8 %all-reduce = (f32[768]{0:T(1024)}, f32[768]{0:T(1024)}, f32[2,8,96]{2,1,0:T(8,128)}, f32[2,8,96]{2,1,0:T(8,128)}, f32[768]{0:T(1024)}, /*index=5*/f32[768]{0:T(1024)}, f32[3072]{0:T(1024)}, f32[768]{0:T(1024)}) all-reduce(f32[768]{0:T(1024)S(1)} %get-tuple-element.72, ...), channel_id=1, replica_groups=mesh['dp'=4,'lat'=8] {'dp','lat'}, use_global_device_ids=true, to_apply=%region_11.12 | all-reduce | flops 9984 | bytes 79872 | tf_op jit(solution)/shard_map/psum | solution.py:228
  826.2 196.3 %all-reduce.4.cloned.1.call-done = (f32[2,8,96,96]{3,2,1,0:T(8,128)}, f32[2,8,96,96]{3,2,1,0:T(8,128)}, f32[768,3072]{1,0:T(8,128)}, f32[3072,768]{1,0:T(8,128)}) async-done(((f32[2,8,96,96]{3,2,1,0:T(8,128)}, f32[2,8,96,96]{3,2,1,0:T(8,128)}, f32[768,3072]{1,0:T(8,128)}, f32[3072,768]{1,0:T(8,128)}), (f32[2,8,96,96]{3,2,1,0:T(8,128)}, f32[2,8,96,96]{3,2,1,0:T(8,128)}, f32[768,3072]{1,0:T(8,128)}, ...) | async-done | bytes 20054032 | tf_op jit(solution)/shard_map/psum | solution.py:228
  1026.8 8.8 copy.240
  (285 shorter events, 221.5 us)
Async XLA Ops:
  10.2 270.7 %copy-start.33 = (f32[12,180]{1,0:T(8,128)}, f32[12,180]{1,0:T(8,128)S(1)}, u32[]{:S(2)}) copy-start(f32[12,180]{1,0:T(8,128)S(1)} %broadcast_multiply_fusion.1) | copy-start | bytes 25924
  19.7 86.5 %all-to-all-start = ((bf16[1,12,2,96,768]{4,2,1,0,3:T(2,128)(2,1)}), bf16[1,12,2,96,768]{4,2,1,0,3:T(2,128)(2,1)S(1)}, u32[]{:S(2)}, u32[]{:S(2)}) async-start(bf16[1,12,2,96,768]{4,2,1,0,3:T(2,128)(2,1)} %copy.128), calls=%async_computation | async-start | bytes 7077888 | tf_op jit(solution)/shard_map/all_to_all | solution.py:136
  121.3 24.9 %copy-start.1 = (bf16[96,12,8,96]{0,3,1,2:T(8,128)(2,1)}, bf16[96,12,8,96]{0,3,1,2:T(8,128)(2,1)S(1)}, u32[]{:S(2)}) copy-start(bf16[96,12,8,96]{0,3,1,2:T(8,128)(2,1)S(1)} %copy.160) | copy-start | bytes 5308420
  192.2 83.5 %all-to-all-start.1 = ((bf16[1,96,2,12,768]{4,2,3,0,1:T(2,128)(2,1)}), bf16[1,96,2,12,768]{4,2,3,0,1:T(2,128)(2,1)}, u32[]{:S(2)}, u32[]{:S(2)}) async-start(bf16[1,96,2,12,768]{4,2,3,0,1:T(2,128)(2,1)} %copy.140), calls=%async_computation.1 | async-start | bytes 7077888 | tf_op jit(solution)/shard_map/all_to_all | solution.py:153
  207.1 73.7 %copy-start.6 = (bf16[1,12,180,768]{3,2,1,0:T(8,128)(2,1)S(1)}, bf16[1,12,180,768]{3,2,1,0:T(8,128)(2,1)}, u32[]{:S(2)}) copy-start(bf16[1,12,180,768]{3,2,1,0:T(8,128)(2,1)} %param.15) | copy-start | bytes 9953284
  207.2 73.7 %copy-start.56 = (f32[12,180]{1,0:T(8,128)S(1)}, f32[12,180]{1,0:T(8,128)}, u32[]{:S(2)}) copy-start(f32[12,180]{1,0:T(8,128)} %copy-done.55) | copy-start | bytes 25924
  207.2 73.7 %copy-start.65 = (f32[768]{0:T(1024)S(1)}, f32[768]{0:T(1024)}, u32[]{:S(2)}) copy-start(f32[768]{0:T(1024)} %param.18) | copy-start | bytes 9220
  207.2 73.7 %copy-start.72 = (f32[768]{0:T(1024)S(1)}, f32[768]{0:T(1024)}, u32[]{:S(2)}) copy-start(f32[768]{0:T(1024)} %param.19) | copy-start | bytes 9220
  208.3 75.8 %copy-start.39 = (f32[180,1,96]{2,0,1:T(8,128)}, f32[180,1,96]{2,0,1:T(8,128)S(1)}, u32[]{:S(2)}) copy-start(f32[180,1,96]{2,0,1:T(8,128)S(1)} %get-tuple-element.118) | copy-start | bytes 207364
  295.9 71.0 %copy-start.27 = (bf16[2160,768]{1,0:T(8,128)(2,1)S(1)}, bf16[2160,768]{1,0:T(8,128)(2,1)}, u32[]{:S(2)}) copy-start(bf16[2160,768]{1,0:T(8,128)(2,1)} %reshape.770) | copy-start | bytes 9953284
  366.9 29.7 %copy-start.59 = (f32[768]{0:T(1024)S(1)}, f32[768]{0:T(1024)}, u32[]{:S(2)}) copy-start(f32[768]{0:T(1024)} %param.24) | copy-start | bytes 9220
  366.9 29.7 %copy-start.69 = (f32[2160]{0:T(1024)S(1)}, f32[2160]{0:T(1024)}, u32[]{:S(2)}) copy-start(f32[2160]{0:T(1024)} %rsqrt.26) | copy-start | bytes 25924
  366.9 29.7 %copy-start.77 = (bf16[768,3072]{1,0:T(8,128)(2,1)S(1)}, bf16[768,3072]{1,0:T(8,128)(2,1)}, u32[]{:S(2)}) copy-start(bf16[768,3072]{1,0:T(8,128)(2,1)} %param.26) | copy-start | bytes 14155780
  413.0 15.0 %slice-start = ((s8[6782976]{0:T(1024)(128)(4,1)}), s8[2588672]{0:T(1024)(128)(4,1)S(1)}, s32[]{:S(2)}) async-start(s8[6782976]{0:T(1024)(128)(4,1)} %bitcast.614), calls=%async_computation.5 | async-start | bytes 5177344
  473.1 82.9 %all-to-all-start.2 = ((bf16[1,12,2,96,768]{4,2,1,0,3:T(2,128)(2,1)}), bf16[1,12,2,96,768]{4,2,1,0,3:T(2,128)(2,1)S(1)}, u32[]{:S(2)}, u32[]{:S(2)}) async-start(bf16[1,12,2,96,768]{4,2,1,0,3:T(2,128)(2,1)} %copy.143), calls=%async_computation.2 | async-start | bytes 7077888 | tf_op jit(solution)/shard_map/all_to_all | solution.py:188
  476.8 545.7 %all-reduce.4.cloned.1.call-start = ((), (), s32[]{:S(2)}) async-start(), calls=%async_computation.4 | async-start | bytes 40894464 | tf_op jit(solution)/shard_map/psum | solution.py:228
  476.8 18.1 %copy-start.28 = (bf16[2160,768]{1,0:T(8,128)(2,1)S(1)}, bf16[2160,768]{1,0:T(8,128)(2,1)}, u32[]{:S(2)}) copy-start(bf16[2160,768]{1,0:T(8,128)(2,1)} %reshape.770) | copy-start | bytes 9953284
  596.4 15.4 %copy-start.8 = (bf16[1,96,12,8,96]{4,1,2,3,0:T(8,128)(2,1)}, bf16[1,96,12,8,96]{4,1,2,3,0:T(8,128)(2,1)S(1)}, u32[]{:S(2)}) copy-start(bf16[1,96,12,8,96]{4,1,2,3,0:T(8,128)(2,1)S(1)} %get-tuple-element.137) | copy-start | bytes 5308420
  638.4 121.7 %all-to-all-start.3 = ((bf16[1,96,2,12,768]{4,2,3,0,1:T(2,128)(2,1)}), bf16[1,96,2,12,768]{4,2,3,0,1:T(2,128)(2,1)}, u32[]{:S(2)}, u32[]{:S(2)}) async-start(bf16[1,96,2,12,768]{4,2,3,0,1:T(2,128)(2,1)} %copy.157), calls=%async_computation.3 | async-start | bytes 7077888 | tf_op jit(solution)/shard_map/all_to_all | solution.py:207
  642.9 122.3 %copy-start.7 = (bf16[1,12,180,768]{3,2,1,0:T(8,128)(2,1)S(1)}, bf16[1,12,180,768]{3,2,1,0:T(8,128)(2,1)}, u32[]{:S(2)}) copy-start(bf16[1,12,180,768]{3,2,1,0:T(8,128)(2,1)} %param.15) | copy-start | bytes 9953284
  642.9 122.3 %copy-start.34 = (f32[12,180]{1,0:T(8,128)S(1)}, f32[12,180]{1,0:T(8,128)}, u32[]{:S(2)}) copy-start(f32[12,180]{1,0:T(8,128)} %copy-done.33) | copy-start | bytes 25924
  642.9 122.3 %copy-start.36 = (f32[180,1,96]{2,0,1:T(8,128)S(1)}, f32[180,1,96]{2,0,1:T(8,128)}, u32[]{:S(2)}) copy-start(f32[180,1,96]{2,0,1:T(8,128)} %copy-done.35) | copy-start | bytes 207364
  642.9 122.3 %copy-start.57 = (f32[12,180]{1,0:T(8,128)S(1)}, f32[12,180]{1,0:T(8,128)}, u32[]{:S(2)}) copy-start(f32[12,180]{1,0:T(8,128)} %copy-done.55) | copy-start | bytes 25924
  642.9 122.3 %copy-start.66 = (f32[768]{0:T(1024)S(1)}, f32[768]{0:T(1024)}, u32[]{:S(2)}) copy-start(f32[768]{0:T(1024)} %param.18) | copy-start | bytes 9220
  (72 other events, 412.7 us)
Sparse Core Ops, SparseCore 0:
  622.8 399.6 all-reduce.3
where the time goes:
time: 1050 us
  waiting for transfers between devices  501 us (48%)
  matrix products  233 us (22%)
  local copies, waits for them, and re-layouts  162 us (15%)
  other arithmetic  72 us (7%)
  blocking collectives  41.8 us (4%)
  starting transfers between devices  20.6 us (2%)
  between operations  16.2 us (2%)
    psum x1, waiting for transfers between devices, shards(): lax.psum((grads[0], grads[1], grads[2], grads[3], grads[4], grads[5], gra...  196 us
    all_to_all x1, waiting for transfers between devices, shards(): lax.all_to_all(slab_grad, 'lat', split_axis=1, concat_axis=3, tiled=True)  117 us
    all_to_all x1, waiting for transfers between devices, shards(): lax.all_to_all(lon_spec, 'lat', split_axis=3, concat_axis=1, tiled=True)  75.5 us
    dot_general x1, matrix products, shards(): jnp.dot(second_low, expand_weight, preferred_element_type=jnp.float32)  71 us
    all_to_all x1, waiting for transfers between devices, shards(): lax.all_to_all(back_slab, 'lat', split_axis=1, concat_axis=3, tiled=True)  67.5 us
    all_to_all x1, waiting for transfers between devices, shards(): lax.all_to_all(row_grad, 'lat', split_axis=3, concat_axis=1, tiled=True)  44.3 us
    psum x1, blocking collectives, shards(): lax.psum((grads[0], grads[1], grads[2], grads[3], grads[4], grads[5], gra...  41.8 us
    unnamed x187, local copies, waits for them, and re-layouts  37.9 us
  transfers between devices with their start and end apart: 5, of which 5 were waited for; matrix products, arithmetic and copies ran while one was open for 8% of the time, Pallas kernels for 0%

commit v1 on v0

v1 whole, which is shorter than its diff:
```python
import functools
import math

import jax
import jax.numpy as jnp
import ml_dtypes
import numpy as np
from jax import lax
from jax.experimental import pallas as pl
from jax.experimental.pallas import tpu as pltpu
from jax.sharding import PartitionSpec as P

BLOCKS = 8
LAT = 90
LON = 180
LAT_PAD = 96
LON_PAD = 96
COLS = 192
GROUPS = 2
LANES = 128

SHRINK = 0.01
EPS = 1e-6
SQRT_HALF = 0.7071067811865476
PDF_SCALE = 0.3989422804014327

F32 = jnp.float32
BF16 = jnp.bfloat16
MESH = pl.DeviceIdType.MESH
VMEM_LIMIT = 62 * 2**20


def base_tables():
    f = np.float32
    modes = np.arange(LON_PAD)
    columns = np.arange(LON)
    phases = (columns[:, None] * modes[None, :] % LON).astype(f) * f(2.0 * math.pi / LON)
    kept = (modes < LON // 2 + 1).astype(f)
    factor = np.where((modes == 0) | (modes == LON // 2), f(1), f(2)) * kept
    scale = f(1.0 / math.sqrt(LON))
    forward_lon = np.stack([np.cos(phases) * kept, -np.sin(phases) * kept], axis=1) * scale
    inverse_lon = np.stack([np.cos(phases) * factor, -np.sin(phases) * factor], axis=1) * scale
    rows = np.arange(LAT_PAD)
    angles = (rows[:, None] * rows[None, :] % LAT).astype(f) * f(2.0 * math.pi / LAT)
    inside = ((rows[:, None] < LAT) & (rows[None, :] < LAT)).astype(f) / f(math.sqrt(LAT))
    cs = np.cos(angles) * inside
    sn = np.sin(angles) * inside
    forward_lat = np.stack([np.stack([cs, sn], 1), np.stack([-sn, cs], 1)], 0)
    inverse_lat = np.stack([np.stack([cs, -sn], 1), np.stack([sn, cs], 1)], 0)
    return forward_lon, inverse_lon, forward_lat, inverse_lat


def slab_rows(modes):
    return -(-2 * modes // 8) * 8


def lon_table(table, shards, modes):
    slab = slab_rows(modes)
    out = np.zeros((COLS, shards, slab), np.float32)
    split = table.reshape(LON, 2, shards, modes).transpose(0, 2, 3, 1)
    out[:LON, :, : 2 * modes] = split.reshape(LON, shards, 2 * modes)
    return out.reshape(COLS, shards * slab)


def make_tables(shards, modes):
    forward_lon, inverse_lon, forward_lat, inverse_lat = base_tables()
    low = lambda t: jnp.asarray(np.ascontiguousarray(t).astype(ml_dtypes.bfloat16))
    n = 2 * LAT_PAD
    fl = lon_table(forward_lon, shards, modes)
    il = lon_table(inverse_lon, shards, modes)
    fa = forward_lat.reshape(n, n)
    ia = inverse_lat.reshape(n, n)
    return dict(
        fl=low(fl), flt=low(fl.T), il=low(il), ilt=low(il.T),
        fa=low(fa), fat=low(fa.T), ia=low(ia), iat=low(ia.T),
    )


def dot(a, b):
    return jnp.dot(a, b, preferred_element_type=F32)


def dot_nt(a, b):
    return lax.dot_general(a, b, (((1,), (1,)), ((), ())), preferred_element_type=F32)


def dot_tn(a, b):
    return lax.dot_general(a, b, (((0,), (0,)), ((), ())), preferred_element_type=F32)


def gelu_both(v):
    cdf = 0.5 * (1.0 + lax.erf(v * SQRT_HALF))
    pdf = jnp.exp(-0.5 * v * v) * PDF_SCALE
    return v * cdf, cdf + v * pdf


def center_scale(v):
    inv = 1.0 / v.shape[-1]
    c = v - jnp.sum(v, -1, keepdims=True) * inv
    return c, lax.rsqrt(jnp.sum(c * c, -1, keepdims=True) * inv + EPS)


def pad_rows(v, n):
    return jnp.concatenate([v, jnp.zeros((n - v.shape[0], v.shape[1]), v.dtype)], 0)


def norm_back(grad, xhat, rs, gain):
    inv = 1.0 / grad.shape[-1]
    dx = grad * gain
    m1 = jnp.sum(dx, -1, keepdims=True) * inv
    m2 = jnp.sum(dx * xhat, -1, keepdims=True) * inv
    return rs * (dx - m1 - xhat * m2)


def full(a):
    return pl.BlockSpec(a.shape, lambda *_: (0,) * a.ndim, pipeline_mode=pl.Buffered(1))


def sds(shape, dtype):
    return jax.ShapeDtypeStruct(shape, dtype)


def params(**kw):
    return pltpu.CompilerParams(vmem_limit_bytes=VMEM_LIMIT, **kw)


def enter_kernel(x_ref, flt_ref, gain_ref, shift_ref, out_ref):
    shards, _, slab, width = out_ref.shape
    x = pad_rows(x_ref[0].astype(F32), COLS)
    c, rs = center_scale(x)
    first = (c * rs * gain_ref[...] + shift_ref[...]).astype(BF16)
    out_ref[:, 0] = dot(flt_ref[...], first).astype(BF16).reshape(shards, slab, width)


def enter(x, flt, gain, shift, shards, slab):
    rows, lon, width = x.shape
    return pl.pallas_call(
        enter_kernel,
        grid=(rows,),
        in_specs=[pl.BlockSpec((1, lon, width), lambda r: (r, 0, 0)), full(flt), full(gain), full(shift)],
        out_specs=pl.BlockSpec((shards, 1, slab, width), lambda r: (0, r, 0, 0)),
        out_shape=sds((shards, rows, slab, width), BF16),
        compiler_params=params(),
        name="enter",
    )(x, flt, gain, shift)


def exchange_kernel(src_ref, out_ref, send_sem, recv_sem, own_sem):
    shards = src_ref.shape[0]
    me = lax.axis_index("lat")
    dp = lax.axis_index("dp")
    barrier = pltpu.get_barrier_semaphore()
    for i in range(1, shards):
        peer = lax.rem(me + i, shards)
        pl.semaphore_signal(barrier, inc=1, device_id=(dp, peer), device_id_type=MESH)
    pl.semaphore_wait(barrier, shards - 1)
    own = pltpu.make_async_copy(src_ref.at[me], out_ref.at[me], own_sem)
    own.start()
    copies = []
    for i in range(1, shards):
        peer = lax.rem(me + i, shards)
        copy = pltpu.make_async_remote_copy(
            src_ref=src_ref.at[peer],
            dst_ref=out_ref.at[me],
            send_sem=send_sem.at[i],
            recv_sem=recv_sem.at[i],
            device_id=(dp, peer),
            device_id_type=MESH,
        )
        copy.start()
        copies.append(copy)
    own.wait()
    for copy in copies:
        copy.wait()


def exchange(x, collective_id):
    shards = x.shape[0]
    return pl.pallas_call(
        exchange_kernel,
        in_specs=[pl.BlockSpec(memory_space=pl.ANY)],
        out_specs=pl.BlockSpec(memory_space=pl.ANY),
        out_shape=sds(x.shape, x.dtype),
        scratch_shapes=[
            pltpu.SemaphoreType.DMA((shards,)),
            pltpu.SemaphoreType.DMA((shards,)),
            pltpu.SemaphoreType.DMA,
        ],
        compiler_params=pltpu.CompilerParams(collective_id=collective_id, has_side_effects=True),
        cost_estimate=pl.CostEstimate(flops=0, bytes_accessed=2 * x.size * 2, transcendentals=0),
        name="exchange",
    )(x)


def strided(ref, start, count, stride):
    return jnp.concatenate([ref[t, pl.ds(start, count, stride=stride), :] for t in range(ref.shape[0])], 1)


def put_rows(ref, start, value):
    n = value.shape[0]
    for t in range(ref.shape[0]):
        ref[t, pl.ds(pl.multiple_of(start, 8), n), :] = value[:, t * LANES : (t + 1) * LANES]


def load_mode(wide_ref, m, slab):
    re = strided(wide_ref, 2 * m, LAT_PAD, slab)
    im = strided(wide_ref, 2 * m + 1, LAT_PAD, slab)
    return jnp.concatenate([re, im], 0).astype(BF16)


def widen(recv_ref, wide_ref):
    shards, rows, slab, width = recv_ref.shape
    n = rows * slab

    def one(s, _):
        put_rows(wide_ref, s * n, recv_ref[s].astype(F32).reshape(n, width))
        return 0

    lax.fori_loop(0, shards, one, 0)


def store_mode(out_s, m, value):
    put_rows(out_s, 2 * m * LAT_PAD, value)


def emit_slabs(out_s, out_ref):
    shards, rows, slab, _ = out_ref.shape

    def one(i, _):
        out_ref[i // rows, lax.rem(i, rows)] = strided(out_s, i, slab, LAT_PAD).astype(BF16)
        return 0

    lax.fori_loop(0, shards * rows, one, 0)


def spectral_forward_kernel(
    recv_ref, fa_ref, ia_ref, wi_ref, bi_ref, wo_ref, bo_ref,
    out_ref, freq_ref, hid_ref, gp_ref, t2_ref, wide_s, out_s,
):
    slab, width = recv_ref.shape[2:]
    modes = freq_ref.shape[0]
    h = LAT_PAD
    widen(recv_ref, wide_s)
    if slab != 2 * modes:
        out_s[...] = jnp.zeros_like(out_s)

    def mix(v, w_ref, b_ref):
        a = dot(v, w_ref[0])
        re = a[:h, :width] - a[h:, width:] + b_ref[0:1]
        im = a[h:, :width] + a[:h, width:] + b_ref[1:2]
        return jnp.concatenate([re, im], 0)

    def one(m, _):
        fq = dot(fa_ref[...], load_mode(wide_s, m, slab)).astype(BF16)
        freq_ref[m] = fq
        hid, gp = gelu_both(mix(fq, wi_ref, bi_ref))
        hid = hid.astype(BF16)
        hid_ref[m] = hid
        gp_ref[m] = gp
        outer = mix(hid, wo_ref, bo_ref)
        t = jnp.tanh(outer * (1.0 / SHRINK))
        t2_ref[m] = t * t
        shrunk = (outer - SHRINK * t).astype(BF16)
        store_mode(out_s, m, dot(ia_ref[...], shrunk))
        return 0

    lax.fori_loop(0, modes, one, 0)
    emit_slabs(out_s, out_ref)


def group_specs(shards, rows, slab, modes, part):
    n = 2 * LAT_PAD
    slabs = pl.BlockSpec((shards, rows, slab, part), lambda g: (0, 0, 0, g))
    spec = pl.BlockSpec((modes, n, part), lambda g: (0, 0, g))
    weight = pl.BlockSpec((1, part, 2 * part), lambda g: (g, 0, 0))
    pair = pl.BlockSpec((2, part), lambda g: (0, g))
    return slabs, spec, weight, pair


def spectral_forward(recv, tb, wi, bi, wo, bo, modes):
    shards, rows, slab, width = recv.shape
    part = width // GROUPS
    n = 2 * LAT_PAD
    slabs, spec, weight, pair = group_specs(shards, rows, slab, modes, part)
    return pl.pallas_call(
        spectral_forward_kernel,
        grid=(GROUPS,),
        in_specs=[slabs, full(tb["fa"]), full(tb["ia"]), weight, pair, weight, pair],
        out_specs=[slabs, spec, spec, spec, spec],
        out_shape=[
            sds(recv.shape, BF16),
            sds((modes, n, width), BF16),
            sds((modes, n, width), BF16),
            sds((modes, n, width), F32),
            sds((modes, n, width), F32),
        ],
        scratch_shapes=[
            pltpu.VMEM((part // LANES, shards * rows * slab, LANES), F32),
            pltpu.VMEM((part // LANES, slab * LAT_PAD, LANES), F32),
        ],
        compiler_params=params(),
        name="spectral_forward",
    )(recv, tb["fa"], tb["ia"], wi, bi, wo, bo)


def spectral_backward_kernel(
    recv_ref, iat_ref, fat_ref, wo_ref, wi_ref, freq_ref, hid_ref, gp_ref, t2_ref,
    out_ref, dwo_ref, dbo_ref, dwi_ref, dbi_ref, wide_s, out_s,
):
    slab, width = recv_ref.shape[2:]
    modes = freq_ref.shape[0]
    h = LAT_PAD
    widen(recv_ref, wide_s)
    if slab != 2 * modes:
        out_s[...] = jnp.zeros_like(out_s)
    for ref in (dwo_ref, dbo_ref, dwi_ref, dbi_ref):
        ref[...] = jnp.zeros_like(ref)

    def grads(value, grad, dw_ref, db_ref):
        re, im = grad[:h], grad[h:]
        low_re, low_im = re.astype(BF16), im.astype(BF16)
        low = jnp.concatenate([low_re, low_im], 0)
        turned = jnp.concatenate([low_im, -low_re], 0)
        dw_ref[0] += dot_tn(value, jnp.concatenate([low, turned], 1))
        db_ref[0:1] += jnp.sum(low_re.astype(F32), 0, keepdims=True)
        db_ref[1:2] += jnp.sum(low_im.astype(F32), 0, keepdims=True)
        return low

    def pull(v, w_ref):
        a = dot(v, w_ref[0])
        re = a[:h, :width] + a[h:, width:]
        im = a[h:, :width] - a[:h, width:]
        return jnp.concatenate([re, im], 0)

    def one(m, _):
        merged = dot(iat_ref[...], load_mode(wide_s, m, slab))
        og = grads(hid_ref[m], merged * t2_ref[m], dwo_ref, dbo_ref)
        ig = grads(freq_ref[m], pull(og, wo_ref) * gp_ref[m], dwi_ref, dbi_ref)
        fg = pull(ig, wi_ref).astype(BF16)
        store_mode(out_s, m, dot(fat_ref[...], fg))
        return 0

    lax.fori_loop(0, modes, one, 0)
    emit_slabs(out_s, out_ref)


def spectral_backward(recv, tb, wo, wi, freq, hid, gp, t2):
    shards, rows, slab, width = recv.shape
    modes = freq.shape[0]
    part = width // GROUPS
    slabs, spec, weight, pair = group_specs(shards, rows, slab, modes, part)
    dw = sds((GROUPS, part, 2 * part), F32)
    db = sds((2, width), F32)
    return pl.pallas_call(
        spectral_backward_kernel,
        grid=(GROUPS,),
        in_specs=[slabs, full(tb["iat"]), full(tb["fat"]), weight, weight, spec, spec, spec, spec],
        out_specs=[slabs, weight, pair, weight, pair],
        out_shape=[sds(recv.shape, BF16), dw, db, dw, db],
        scratch_shapes=[
            pltpu.VMEM((part // LANES, shards * rows * slab, LANES), F32),
            pltpu.VMEM((part // LANES, slab * LAT_PAD, LANES), F32),
        ],
        compiler_params=params(),
        name="spectral_backward",
    )(recv, tb["iat"], tb["fat"], wo, wi, freq, hid, gp, t2)


def gather_row(r_ref, i):
    shards, _, slab, width = r_ref.shape
    return r_ref[:, i].astype(F32).reshape(shards * slab, width).astype(BF16)


def feed_kernel(
    per, chunk, scale_ref, x_ref, c_ref, r_ref, il_ref, ilt_ref, w1_ref, w2_ref, eb_ref, rb_ref,
    ng_ref, ns_ref, pg_ref, ps_ref,
    lo_ref, mg_ref, rg_ref, act_ref, pre_ref, sec_ref, up_ref, deb_ref, drb_ref, dpg_ref, dps_ref,
    mixed_s, xhat_s, rs_s, branch_s, grad_s,
):
    g = pl.program_id(0)
    lon, width = x_ref.shape[1:]
    hidden = w1_ref.shape[1]
    shards, _, slab, _ = r_ref.shape

    @pl.when(g == 0)
    def _():
        for ref in (deb_ref, drb_ref, dpg_ref, dps_ref):
            ref[...] = jnp.zeros_like(ref)

    for i in range(per):
        rows = pl.ds(i * COLS, COLS)
        x = pad_rows(x_ref[i].astype(F32), COLS)
        c, rs = center_scale(x)
        first = c * rs * ng_ref[...] + ns_ref[...]
        mixed = dot(il_ref[...], gather_row(r_ref, i)) + first + x
        c, rs = center_scale(mixed)
        xhat = c * rs
        mixed_s[rows, :] = mixed
        xhat_s[rows, :] = xhat
        rs_s[rows, :] = jnp.broadcast_to(rs, (COLS, 128))
        sec_ref[rows, :] = (xhat * pg_ref[...] + ps_ref[...]).astype(BF16)
        up = (pad_rows(c_ref[i].astype(F32), COLS) * scale_ref[0, g * per + i]).astype(BF16)
        up_ref[rows, :] = up
        drb_ref[...] += jnp.sum(up.astype(F32), 0, keepdims=True)
    branch_s[...] = jnp.broadcast_to(rb_ref[...], branch_s.shape)
    grad_s[...] = jnp.zeros_like(grad_s)

    def hidden_chunk(j, _):
        ds = pl.ds(pl.multiple_of(j * chunk, chunk), chunk)
        act, slope = gelu_both(dot(sec_ref[...], w1_ref[:, ds]) + eb_ref[:, ds])
        act = act.astype(BF16)
        act_ref[:, ds] = act
        pre = (dot_nt(up_ref[...], w2_ref[ds, :]) * slope).astype(BF16)
        pre_ref[:, ds] = pre
        deb_ref[:, ds] += jnp.sum(pre.astype(F32), 0, keepdims=True)
        branch_s[...] += dot(act, w2_ref[ds, :])
        grad_s[...] += dot_nt(pre, w1_ref[:, ds])
        return 0

    lax.fori_loop(0, hidden // chunk, hidden_chunk, 0)
    for i in range(per):
        rows = pl.ds(i * COLS, COLS)
        keep = scale_ref[1, g * per + i]
        lo_ref[i] = ((mixed_s[rows, :] + branch_s[rows, :]) * keep).astype(BF16)[:lon]
        grad = grad_s[rows, :]
        xhat = xhat_s[rows, :]
        dpg_ref[...] += jnp.sum(grad * xhat, 0, keepdims=True)
        dps_ref[...] += jnp.sum(grad, 0, keepdims=True)
        up = pad_rows(c_ref[i].astype(F32), COLS) * scale_ref[0, g * per + i]
        mg = up + norm_back(grad, xhat, rs_s[rows, 0:1], pg_ref[...])
        mg_ref[i] = mg[:lon]
        rg_ref[:, i] = dot(ilt_ref[...], mg.astype(BF16)).astype(BF16).reshape(shards, slab, width)


def feed(scale, x, cot, recv, tb, w1, w2, eb, rb, ng, ns, pg, ps):
    rows, lon, width = x.shape
    hidden = w1.shape[1]
    shards, _, slab, _ = recv.shape
    per = 3 if rows % 3 == 0 else 1
    row = pl.BlockSpec((per, lon, width), lambda g: (g, 0, 0))
    slabs = pl.BlockSpec((shards, per, slab, width), lambda g: (0, g, 0, 0))
    flat = lambda w: pl.BlockSpec((per * COLS, w), lambda g: (g, 0))
    vec = lambda w: pl.BlockSpec((1, w), lambda g: (0, 0))
    tall = per * COLS
    return pl.pallas_call(
        functools.partial(feed_kernel, per, 512),
        grid=(rows // per,),
        in_specs=[pl.BlockSpec(memory_space=pltpu.SMEM), row, row, slabs]
        + [full(a) for a in (tb["il"], tb["ilt"], w1, w2, eb, rb, ng, ns, pg, ps)],
        out_specs=[row, row, slabs, flat(hidden), flat(hidden), flat(width), flat(width)]
        + [vec(hidden), vec(width), vec(width), vec(width)],
        out_shape=[
            sds((rows, lon, width), BF16),
            sds((rows, lon, width), F32),
            sds(recv.shape, BF16),
            sds((rows * COLS, hidden), BF16),
            sds((rows * COLS, hidden), BF16),
            sds((rows * COLS, width), BF16),
            sds((rows * COLS, width), BF16),
            sds((1, hidden), F32),
            sds((1, width), F32),
            sds((1, width), F32),
            sds((1, width), F32),
        ],
        scratch_shapes=[
            pltpu.VMEM((tall, width), F32),
            pltpu.VMEM((tall, width), F32),
            pltpu.VMEM((tall, 128), F32),
            pltpu.VMEM((tall, width), F32),
            pltpu.VMEM((tall, width), F32),
        ],
        compiler_params=params(),
        name="feed",
    )(scale, x, cot, recv, tb["il"], tb["ilt"], w1, w2, eb, rb, ng, ns, pg, ps)


def leave_kernel(x_ref, r_ref, mg_ref, fl_ref, gain_ref, out_ref, dg_ref, db_ref):
    lon = x_ref.shape[1]

    @pl.when(pl.program_id(0) == 0)
    def _():
        dg_ref[...] = jnp.zeros_like(dg_ref)
        db_ref[...] = jnp.zeros_like(db_ref)

    x = pad_rows(x_ref[0].astype(F32), COLS)
    c, rs = center_scale(x)
    xhat = c * rs
    mg = pad_rows(mg_ref[0], COLS)
    grad = dot(fl_ref[...], gather_row(r_ref, 0)) + mg
    dg_ref[...] += jnp.sum(grad * xhat, 0, keepdims=True)
    db_ref[...] += jnp.sum(grad, 0, keepdims=True)
    out_ref[0] = (mg + norm_back(grad, xhat, rs, gain_ref[...]))[:lon]


def leave(x, recv, mg, fl, gain):
    rows, lon, width = x.shape
    shards, _, slab, _ = recv.shape
    row = pl.BlockSpec((1, lon, width), lambda r: (r, 0, 0))
    vec = pl.BlockSpec((1, width), lambda r: (0, 0))
    return pl.pallas_call(
        leave_kernel,
        grid=(rows,),
        in_specs=[row, pl.BlockSpec((shards, 1, slab, width), lambda r: (0, r, 0, 0)), row, full(fl), full(gain)],
        out_specs=[row, vec, vec],
        out_shape=[sds((rows, lon, width), F32), sds((1, width), F32), sds((1, width), F32)],
        compiler_params=params(),
        name="leave",
    )(x, recv, mg, fl, gain)


def dense_weights(weight):
    _, blocks, n, _ = weight.shape
    per = blocks // GROUPS
    w = weight.reshape(2, GROUPS, per, n, n)
    eye = jnp.eye(per, dtype=weight.dtype)
    side = per * n
    forward = jnp.einsum("pgbio,bd->gbipdo", w, eye).reshape(GROUPS, side, 2 * side)
    backward = jnp.einsum("pgbio,bd->gdopbi", w, eye).reshape(GROUPS, side, 2 * side)
    return forward, backward


def block_grads(dense):
    side = dense.shape[1]
    per = BLOCKS // GROUPS
    n = side // per
    d = dense.reshape(GROUPS, per, n, 2, per, n)
    picked = jnp.stack([d[:, b, :, :, b, :] for b in range(per)], 1)
    return picked.transpose(3, 0, 1, 2, 4).reshape(2, BLOCKS, n, n)


def shards_fn(
    shards, inputs, cotangent, storm_weight, norm_gain, norm_shift, inner_weight, inner_bias,
    outer_weight, outer_bias, post_gain, post_shift, expand_weight, expand_bias, reduce_weight, reduce_bias,
):
    _, rows, lon, width = inputs.shape
    modes = LON_PAD // shards
    slab = slab_rows(modes)
    tb = make_tables(shards, modes)
    row_ids = lax.axis_index("lat") * rows + jnp.arange(rows, dtype=jnp.int32)
    keep = (row_ids < LAT).astype(F32)
    scale = jnp.stack([keep * (storm_weight[0].astype(F32) / 64.0), keep])
    x = inputs[0]
    cot = cotangent[0]
    line = lambda v: v.reshape(1, -1)
    ng, ns, pg, ps = line(norm_gain), line(norm_shift), line(post_gain), line(post_shift)
    eb, rb = line(expand_bias), line(reduce_bias)
    bi, bo = inner_bias.reshape(2, width), outer_bias.reshape(2, width)
    wi, wi_back = dense_weights(inner_weight)
    wo, wo_back = dense_weights(outer_weight)

    spec = exchange(enter(x, tb["flt"], ng, ns, shards, slab), 0)
    back, freq, hid, gp, t2 = spectral_forward(spec, tb, wi, bi, wo, bo, modes)
    row_spec = exchange(back, 1)
    (layer_out, mixed_grad, row_grad, act, pre, second, up, deb, drb, dpg, dps) = feed(
        scale, x, cot, row_spec, tb, expand_weight, reduce_weight, eb, rb, ng, ns, pg, ps
    )
    dw2 = dot_tn(act, up)
    dw1 = dot_tn(second, pre)
    dw1, dw2 = lax.psum((dw1, dw2), ("dp", "lat"))
    mode_grad = exchange(row_grad, 2)
    slab_grad, dwo, dbo, dwi, dbi = spectral_backward(mode_grad, tb, wo_back, wi_back, freq, hid, gp, t2)
    lon_grad = exchange(slab_grad, 3)
    input_grad, dng, dns = leave(x, lon_grad, mixed_grad, tb["fl"], ng)
    small = lax.psum(
        (dng, dns, block_grads(dwi), dbi, block_grads(dwo), dbo, dpg, dps, deb, drb), ("dp", "lat")
    )
    dng, dns, dwi, dbi, dwo, dbo, dpg, dps, deb, drb = small
    flat = lambda v: v.reshape(-1)
    return (
        layer_out[None], input_grad[None], flat(dng), flat(dns),
        dwi, dbi.reshape(inner_bias.shape), dwo, dbo.reshape(outer_bias.shape),
        flat(dpg), flat(dps), dw1, flat(deb), dw2, flat(drb),
    )


def solution(mesh):
    split = P("dp", "lat", None, None)
    return jax.shard_map(
        functools.partial(shards_fn, mesh.shape["lat"]),
        mesh=mesh,
        in_specs=(split, split, P("dp")) + (P(),) * 12,
        out_specs=(split, split) + (P(),) * 12,
        check_vma=False,
    )
```

time: 1050 us -> 913 us (0.87)
  Pallas kernels: 0 us -> 520 us
  waiting for transfers between devices: 501 us -> 211 us
  matrix products: 233 us -> 31.4 us
  local copies, waits for them, and re-layouts: 162 us -> 57.3 us
  other arithmetic: 72 us -> 6.12 us
  blocking collectives: 41.8 us -> 70.2 us
  starting transfers between devices: 20.6 us -> 0.04 us
    pallas_call x0 -> x9, Pallas kernels: none -> 520 us  [the longest x4 331 us: exchange(): pl.pallas_call(exchange_kernel, in_specs=[pl.BlockSpec(memory_space=pl.AN...]
    all_to_all x4 -> x0, waiting for transfers between devices: 304 us -> none  [the longest x1 117 us: shards(): lax.all_to_all(slab_grad, 'lat', split_axis=1, concat_axis=3, tiled=True)]
    dot_general x38 -> x2, matrix products: 233 us -> 31.4 us  [dot_tn(): lax.dot_general(a, b, (((0,), (0,)), ((), ())), preferred_element_type=F32)]
    another operation x10 -> x0, local copies, waits for them, and re-layouts: 42.1 us -> none
    convert_element_type x8 -> x0, local copies, waits for them, and re-layouts: 30.6 us -> none  [the longest x1 5.43 us: shards(): slab_grad = jnp.einsum('qkpr,skqmc->srpmc', forward_lat, freq_grad, prefe...]
    reduce_sum x9 -> x0, other arithmetic: 29.1 us -> none  [the longest x1 7.64 us: layer_norm(): return (values - center) * lax.rsqrt(spread + epsilon) * gain + shift]
    psum x1, blocking collectives: 41.8 us -> 70.2 us  [shards_fn(): lax.psum((dng, dns, block_grads(dwi), dbi, block_grads(dwo), dbo, dpg, dp...]
    another operation x6 -> x2, other arithmetic: 25.5 us -> 0.57 us  [the longest x1 0.57 us: shards_fn(): scale = jnp.stack([keep * (storm_weight[0].astype(F32) / 64.0), keep])]
  transfers between devices with their start and end apart: 5 -> 1, of which waited for: 5 -> 1; matrix products, arithmetic and copies ran while one was open for 8% -> 1% of each run, Pallas kernels for 0% -> 13%
where the time goes in v1:
time: 913 us; the launch traced here: 912 us
  Pallas kernels  520 us (57%)
  waiting for transfers between devices  211 us (23%)
  blocking collectives  70.2 us (8%)
  local copies, waits for them, and re-layouts  57.3 us (6%)
  matrix products  31.4 us (3%)
  between operations  15.1 us (2%)
    pallas_call x4, Pallas kernels, exchange(): pl.pallas_call(exchange_kernel, in_specs=[pl.BlockSpec(memory_space=pl.AN...  331 us
    psum x1, waiting for transfers between devices, shards_fn(): lax.psum((dng, dns, block_grads(dwi), dbi, block_grads(dwo), dbo, dpg, dp...  211 us
    pallas_call x1, Pallas kernels, feed(): pl.pallas_call(functools.partial(feed_kernel, per, 512), grid=(rows // pe...  72.7 us
    psum x1, blocking collectives, shards_fn(): lax.psum((dng, dns, block_grads(dwi), dbi, block_grads(dwo), dbo, dpg, dp...  70.2 us
    pallas_call x1, Pallas kernels, spectral_backward(): pl.pallas_call(spectral_backward_kernel, grid=(GROUPS,), in_specs=[slabs,...  50.9 us
    pallas_call x1, Pallas kernels, spectral_forward(): pl.pallas_call(spectral_forward_kernel, grid=(GROUPS,), in_specs=[slabs,...  41.7 us
    dot_general x2, matrix products, dot_tn(): lax.dot_general(a, b, (((0,), (0,)), ((), ())), preferred_element_type=F32)  31.4 us
    unnamed x53, local copies, waits for them, and re-layouts  26 us
  transfers between devices with their start and end apart: 1, of which 1 were waited for; matrix products, arithmetic and copies ran while one was open for 1% of the time, Pallas kernels for 13%

profile of v1, /device:TPU:0, one launch (start us, length us, event | category | flops | bytes accessed | tf_op | source)
XLA Modules:
  0.0 911.5 jit_solution(15664922951051982599)
XLA Ops:
  9.8 10.6 %enter.1.src_ref = bf16[8,12,24,768]{3,2,1,0:T(8,128)(2,1)} custom-call(bf16[12,180,768]{2,1,0:T(8,128)(2,1)} %bitcast.51, bf16[192,192]{1,0:T(8,128)(2,1)} %constant.27.clone.flt_ref, f32[1,768]{1,0:T(1,128)} %reshape.130.gain_ref.ng_ref, f32[1,768]{1,0:T(1,128)} %reshape.131.shift_ref.ns_ref), custom_call_target="tpu_custom_call" | custom-call | tf_op jit(solution)/shard_map/enter/pallas_call | solution.py:137
  20.4 63.3 %exchange.4.recv_ref = bf16[8,12,24,768]{3,2,1,0:T(8,128)(2,1)} custom-call(bf16[8,12,24,768]{3,2,1,0:T(8,128)(2,1)} %enter.1.src_ref), custom_call_target="tpu_custom_call" | custom-call | bytes 7077888 | tf_op jit(solution)/shard_map/exchange/pallas_call | solution.py:179
  84.2 3.3 multiply_bitcast_fusion.2
  87.5 3.2 copy.38
  90.7 2.1 reshape.134.wi_ref
  94.9 2.1 reshape.138.wo_ref
  98.4 41.7 %spectral_forward.1 = (bf16[8,12,24,768]{3,2,1,0:T(8,128)(2,1)}, bf16[12,192,768]{2,1,0:T(8,128)(2,1)}, bf16[12,192,768]{2,1,0:T(8,128)(2,1)}, f32[12,192,768]{2,1,0:T(8,128)}, f32[12,192,768]{2,1,0:T(8,128)}) custom-call(bf16[8,12,24,768]{3,2,1,0:T(8,128)(2,1)} %exchange.4.recv_ref, bf16[192,192]{1,0:T(8,128)(2,1)} %constant.30.clone.fa_ref.iat_ref, ...), custom_call_target="tpu_custom_call" | custom-call | tf_op jit(solution)/shard_map/spectral_forward/pallas_call | solution.py:285
  140.2 79.7 %exchange.5.r_ref = bf16[8,12,24,768]{3,2,1,0:T(8,128)(2,1)} custom-call(bf16[8,12,24,768]{3,2,1,0:T(8,128)(2,1)} %get-tuple-element.38.src_ref), custom_call_target="tpu_custom_call" | custom-call | bytes 7077888 | tf_op jit(solution)/shard_map/exchange/pallas_call | solution.py:179
  222.9 72.7 %feed.1 = (bf16[12,180,768]{2,1,0:T(8,128)(2,1)}, f32[12,180,768]{2,1,0:T(8,128)}, bf16[8,12,24,768]{3,2,1,0:T(8,128)(2,1)}, bf16[2304,3072]{1,0:T(8,128)(2,1)},...) custom-call(f32[2,12]{1,0:T(2,128)} %pad_maximum_fusion.scale_ref, ...), custom_call_target="tpu_custom_call" | custom-call | tf_op jit(solution)/shard_map/feed/pallas_call | solution.py:445
  295.6 78.8 %exchange.6.recv_ref = bf16[8,12,24,768]{3,2,1,0:T(8,128)(2,1)} custom-call(bf16[8,12,24,768]{3,2,1,0:T(8,128)(2,1)} %get-tuple-element.40.src_ref), custom_call_target="tpu_custom_call" | custom-call | bytes 7077888 | tf_op jit(solution)/shard_map/exchange/pallas_call | solution.py:179
  374.4 2.2 reshape.144.wo_ref
  378.7 50.9 %spectral_backward.1 = (bf16[8,12,24,768]{3,2,1,0:T(8,128)(2,1)}, f32[2,384,768]{2,1,0:T(8,128)}, f32[2,768]{1,0:T(2,128)}, f32[2,384,768]{2,1,0:T(8,128)}, f32[2,768]{1,0:T(2,128)}) custom-call(bf16[8,12,24,768]{3,2,1,0:T(8,128)(2,1)} %exchange.6.recv_ref, bf16[192,192]{1,0:T(8,128)(2,1)} %constant.30.clone.fa_ref.iat_ref, ...), custom_call_target="tpu_custom_call" | custom-call | tf_op jit(solution)/shard_map/spectral_backward/pallas_call | solution.py:354
  429.6 3.8 reshape.151
  435.6 3.8 reshape.148
  441.6 17.6 %fusion.4 = f32[3072,768]{1,0:T(8,128)} fusion(bf16[2304,3072]{1,0:T(8,128)(2,1)} %get-tuple-element.59, bf16[2304,768]{1,0:T(8,128)(2,1)S(1)} %copy-done.16), kind=kOutput, calls=%fused_computation.15 | convolution fusion | flops 10871635968 | bytes 27131904 | tf_op jit(solution)/shard_map/dot_general | solution.py:88
  459.2 13.8 %fusion.3 = f32[768,3072]{1,0:T(8,128)} fusion(bf16[2304,768]{1,0:T(8,128)(2,1)S(1)} %copy-done.15, bf16[2304,3072]{1,0:T(8,128)(2,1)S(1)} %bitcast.73), kind=kOutput, calls=%fused_computation.14 | convolution fusion | flops 10871635968 | bytes 27131904 | tf_op jit(solution)/shard_map/dot_general | solution.py:88
  473.0 109.2 %exchange.7.r_ref = bf16[8,12,24,768]{3,2,1,0:T(8,128)(2,1)} custom-call(bf16[8,12,24,768]{3,2,1,0:T(8,128)(2,1)} %get-tuple-element.45.src_ref), custom_call_target="tpu_custom_call" | custom-call | bytes 7077888 | tf_op jit(solution)/shard_map/exchange/pallas_call | solution.py:179
  582.3 13.4 %leave.1 = (f32[12,180,768]{2,1,0:T(8,128)}, f32[1,768]{1,0:T(1,128)}, f32[1,768]{1,0:T(1,128)}) custom-call(bf16[12,180,768]{2,1,0:T(8,128)(2,1)} %bitcast.53, bf16[8,12,24,768]{3,2,1,0:T(8,128)(2,1)} %exchange.7.r_ref, f32[12,180,768]{2,1,0:T(8,128)} %get-tuple-element.46.mg_ref, bf16[192,192]{1,0:T(8,128)(2,1)} %constant.26.clone.fl_ref, ...), custom_call_target="tpu_custom_call" | custom-call | tf_op jit(solution)/shard_map/leave/pallas_call | solution.py:500
  597.4 9.1 %copy.49 = f32[1,12,180,768]{3,0,2,1:T(1,128)} copy(f32[1,12,180,768]{3,2,1,0:T(8,128)} %bitcast.56) | data formatting | bytes 13271040
  606.5 70.2 %all-reduce = (f32[768]{0:T(1024)}, f32[768]{0:T(1024)}, f32[2,8,96]{2,1,0:T(8,128)}, f32[2,8,96]{2,1,0:T(8,128)}, f32[768]{0:T(1024)}, /*index=5*/f32[768]{0:T(1024)}, f32[3072]{0:T(1024)}, f32[768]{0:T(1024)}) all-reduce(f32[768]{0:T(1024)S(1)} %reduce, f32[768]{0:T(1024)S(1)} %reduce.1, ...), channel_id=1, replica_groups=mesh['dp'=4,'lat'=8] {'dp','lat'}, use_global_device_ids=true, to_apply=%region_0.0 | all-reduce | flops 9984 | bytes 79872 | tf_op jit(solution)/shard_map/psum | solution.py:564
  676.7 211.2 %all-reduce.4.cloned.1.call-done = (f32[2,8,96,96]{3,2,1,0:T(8,128)}, f32[2,8,96,96]{3,2,1,0:T(8,128)}, f32[768,3072]{1,0:T(8,128)}, f32[3072,768]{1,0:T(8,128)}) async-done(((f32[2,8,96,96]{3,2,1,0:T(8,128)}, f32[2,8,96,96]{3,2,1,0:T(8,128)}, f32[768,3072]{1,0:T(8,128)}, f32[3072,768]{1,0:T(8,128)}), (f32[2,8,96,96]{3,2,1,0:T(8,128)}, f32[2,8,96,96]{3,2,1,0:T(8,128)}, f32[768,3072]{1,0:T(8,128)}, ...) | async-done | bytes 20054032 | tf_op jit(solution)/shard_map/psum | solution.py:564
  889.9 2.2 copy.62
  892.1 8.8 copy.63
  900.9 3.7 copy.64
  (81 shorter events, 19.1 us)
Async XLA Ops:
  7.2 880.7 %all-reduce.4.cloned.1.call-start = ((), (), s32[]{:S(2)}) async-start(), calls=%async_computation | async-start | bytes 40894464 | tf_op jit(solution)/shard_map/psum | solution.py:564
  20.4 63.3 %copy-start.2 = (bf16[2,8,96,96]{3,2,1,0:T(8,128)(2,1)S(1)}, bf16[2,8,96,96]{3,2,1,0:T(8,128)(2,1)}, u32[]{:S(2)}) copy-start(bf16[2,8,96,96]{3,2,1,0:T(8,128)(2,1)} %param.28) | copy-start | bytes 884740
  20.4 63.6 %copy-start.3 = (bf16[2,8,96,96]{3,2,1,0:T(8,128)(2,1)S(1)}, bf16[2,8,96,96]{3,2,1,0:T(8,128)(2,1)}, u32[]{:S(2)}) copy-start(bf16[2,8,96,96]{3,2,1,0:T(8,128)(2,1)} %param.30) | copy-start | bytes 884740
  92.9 4.2 copy-start.5
  92.9 4.9 copy-start.6
  140.1 80.4 %copy-start.9 = (f32[768]{0:T(1024)S(1)}, f32[768]{0:T(1024)}, u32[]{:S(2)}) copy-start(f32[768]{0:T(1024)} %param.37) | copy-start | bytes 9220
  140.1 81.0 %copy-start.10 = (f32[768]{0:T(1024)S(1)}, f32[768]{0:T(1024)}, u32[]{:S(2)}) copy-start(f32[768]{0:T(1024)} %param.32) | copy-start | bytes 9220
  140.2 81.6 %copy-start.11 = (f32[768]{0:T(1024)S(1)}, f32[768]{0:T(1024)}, u32[]{:S(2)}) copy-start(f32[768]{0:T(1024)} %param.33) | copy-start | bytes 9220
  295.6 78.8 %copy-start.1 = (bf16[2,4,96,2,4,96]{5,4,3,2,1,0:T(4,128)(2,1)S(1)}, bf16[2,4,96,2,4,96]{5,4,3,2,1,0:T(4,128)(2,1)}, u32[]{:S(2)}) copy-start(bf16[2,4,96,2,4,96]{5,4,3,2,1,0:T(4,128)(2,1)} %get-tuple-element.101) | copy-start | bytes 3538948
  295.6 81.0 %copy-start = (bf16[2,4,96,2,4,96]{5,4,3,2,1,0:T(4,128)(2,1)S(1)}, bf16[2,4,96,2,4,96]{5,4,3,2,1,0:T(4,128)(2,1)}, u32[]{:S(2)}) copy-start(bf16[2,4,96,2,4,96]{5,4,3,2,1,0:T(4,128)(2,1)} %get-tuple-element.96) | copy-start | bytes 3538948
  440.6 18.6 %slice-start.3 = ((s8[14155776]{0:T(1024)(128)(4,1)}), s8[4194304]{0:T(1024)(128)(4,1)S(1)}, s32[]{:S(2)}) async-start(s8[14155776]{0:T(1024)(128)(4,1)} %bitcast.72), calls=%async_computation.4 | async-start | bytes 8388608
  441.6 17.6 %slice-start.4 = ((s8[14155776]{0:T(1024)(128)(4,1)}), s8[4194304]{0:T(1024)(128)(4,1)S(1)}, s32[]{:S(2)}) async-start(s8[14155776]{0:T(1024)(128)(4,1)} %bitcast.72), calls=%async_computation.5 | async-start | bytes 8388608
  441.6 17.6 %slice-start.5 = ((s8[14155776]{0:T(1024)(128)(4,1)}), s8[4194304]{0:T(1024)(128)(4,1)S(1)}, s32[]{:S(2)}) async-start(s8[14155776]{0:T(1024)(128)(4,1)} %bitcast.72), calls=%async_computation.6 | async-start | bytes 8388608
  441.6 17.6 %slice-start.6 = ((s8[14155776]{0:T(1024)(128)(4,1)}), s8[1572864]{0:T(1024)(128)(4,1)S(1)}, s32[]{:S(2)}) async-start(s8[14155776]{0:T(1024)(128)(4,1)} %bitcast.72), calls=%async_computation.7 | async-start | bytes 3145728
  441.6 17.6 %copy-start.15 = (bf16[2304,768]{1,0:T(8,128)(2,1)S(1)}, bf16[2304,768]{1,0:T(8,128)(2,1)}, u32[]{:S(2)}) copy-start(bf16[2304,768]{1,0:T(8,128)(2,1)} %get-tuple-element.56) | copy-start | bytes 10616836
  582.3 14.8 %copy-start.8 = (f32[2,768]{1,0:T(2,128)S(1)}, f32[2,768]{1,0:T(2,128)}, u32[]{:S(2)}) copy-start(f32[2,768]{1,0:T(2,128)} %get-tuple-element.51) | copy-start | bytes 18436
  582.3 14.9 %copy-start.7 = (f32[2,768]{1,0:T(2,128)S(1)}, f32[2,768]{1,0:T(2,128)}, u32[]{:S(2)}) copy-start(f32[2,768]{1,0:T(2,128)} %get-tuple-element.53) | copy-start | bytes 18436
  582.3 15.0 %copy-start.14 = (f32[1,768]{1,0:T(1,128)S(1)}, f32[1,768]{1,0:T(1,128)}, u32[]{:S(2)}) copy-start(f32[1,768]{1,0:T(1,128)} %get-tuple-element.54) | copy-start | bytes 9220
  582.3 15.0 %copy-start.13 = (f32[1,768]{1,0:T(1,128)S(1)}, f32[1,768]{1,0:T(1,128)}, u32[]{:S(2)}) copy-start(f32[1,768]{1,0:T(1,128)} %get-tuple-element.55) | copy-start | bytes 9220
  582.3 15.0 %copy-start.12 = (f32[1,768]{1,0:T(1,128)S(1)}, f32[1,768]{1,0:T(1,128)}, u32[]{:S(2)}) copy-start(f32[1,768]{1,0:T(1,128)} %get-tuple-element.61) | copy-start | bytes 9220
  597.3 9.2 %copy-start.4 = (f32[1,3072]{1,0:T(1,128)S(1)}, f32[1,3072]{1,0:T(1,128)}, u32[]{:S(2)}) copy-start(f32[1,3072]{1,0:T(1,128)} %get-tuple-element.58) | copy-start | bytes 36868
  889.9 11.0 %slice-start = ((s8[9437184]{0:T(1024)(128)(4,1)}), s8[4194304]{0:T(1024)(128)(4,1)S(1)}, s32[]{:S(2)}) async-start(s8[9437184]{0:T(1024)(128)(4,1)} %bitcast.54), calls=%async_computation.1 | async-start | bytes 8388608
  892.1 8.8 slice-start.1
  892.1 8.8 slice-start.2
  (1 other events, 2.2 us)
Sparse Core Ops, SparseCore 0:
  473.2 414.6 all-reduce.3

commit v2 on v1

--- a/solution.py
+++ b/solution.py
@@ -15,6 +15,7 @@
 LON = 180
 LAT_PAD = 96
 LON_PAD = 96
+KEPT = LON // 2 + 1
 COLS = 192
 GROUPS = 2
 LANES = 128
@@ -145,39 +146,88 @@
     )(x, flt, gain, shift)
 
 
-def exchange_kernel(src_ref, out_ref, send_sem, recv_sem, own_sem):
-    shards = src_ref.shape[0]
+def up8(n):
+    return -(-n // 8) * 8
+
+
+def slab_sizes(index, modes, slab):
+    sizes = [(index < KEPT // modes, slab)]
+    if KEPT % modes:
+        sizes.append((index == KEPT // modes, up8(2 * (KEPT % modes))))
+    return sizes
+
+
+def row_sizes(index, rows):
+    sizes = [(index < LAT // rows, rows)]
+    if LAT % rows:
+        sizes.append((index == LAT // rows, LAT % rows))
+    return sizes
+
+
+def each_size(row_options, slab_options, fn):
+    for row_ok, nr in row_options:
+        for slab_ok, ns in slab_options:
+            pl.when(row_ok & slab_ok)(functools.partial(fn, nr, ns))
+
+
+def greet(shards, me, dp):
+    barrier = pltpu.get_barrier_semaphore()
+
+    def one(i, _):
+        peer = lax.rem(me + i, shards)
+        pl.semaphore_signal(barrier, inc=1, device_id=(dp, peer), device_id_type=MESH)
+        return 0
+
+    lax.fori_loop(1, shards, one, 0)
+    pl.semaphore_wait(barrier, shards - 1)
+
+
+def send(src, dst, send_sem, recv_sem, dp, peer):
+    return pltpu.make_async_remote_copy(
+        src_ref=src, dst_ref=dst, send_sem=send_sem, recv_sem=recv_sem,
+        device_id=(dp, peer), device_id_type=MESH,
+    )
+
+
+def exchange_kernel(from_rows, modes, src_ref, out_ref, send_sem, recv_sem, own_sem):
+    shards, rows, slab, _ = src_ref.shape
     me = lax.axis_index("lat")
     dp = lax.axis_index("dp")
-    barrier = pltpu.get_barrier_semaphore()
-    for i in range(1, shards):
-        peer = lax.rem(me + i, shards)
-        pl.semaphore_signal(barrier, inc=1, device_id=(dp, peer), device_id_type=MESH)
-    pl.semaphore_wait(barrier, shards - 1)
+    greet(shards, me, dp)
     own = pltpu.make_async_copy(src_ref.at[me], out_ref.at[me], own_sem)
     own.start()
-    copies = []
-    for i in range(1, shards):
-        peer = lax.rem(me + i, shards)
-        copy = pltpu.make_async_remote_copy(
-            src_ref=src_ref.at[peer],
-            dst_ref=out_ref.at[me],
-            send_sem=send_sem.at[i],
-            recv_sem=recv_sem.at[i],
-            device_id=(dp, peer),
-            device_id_type=MESH,
-        )
-        copy.start()
-        copies.append(copy)
+
+    def go(i, sender, receiver, act):
+        row_owner, mode_owner = (sender, receiver) if from_rows else (receiver, sender)
+
+        def piece(nr, ns):
+            part = (pl.ds(0, nr), pl.ds(0, ns))
+            copy = send(
+                src_ref.at[(receiver,) + part], out_ref.at[(sender,) + part],
+                send_sem.at[i], recv_sem.at[i], dp, receiver,
+            )
+            act(copy)
+
+        each_size(row_sizes(row_owner, rows), slab_sizes(mode_owner, modes, slab), piece)
+
+    def start(i, _):
+        go(i, me, lax.rem(me + i, shards), lambda copy: copy.start())
+        return 0
+
+    def finish(i, _):
+        go(i, me, lax.rem(me + i, shards), lambda copy: copy.wait_send())
+        go(i, lax.rem(me + shards - i, shards), me, lambda copy: copy.wait_recv())
+        return 0
+
+    lax.fori_loop(1, shards, start, 0)
     own.wait()
-    for copy in copies:
-        copy.wait()
-
-
-def exchange(x, collective_id):
+    lax.fori_loop(1, shards, finish, 0)
+
+
+def exchange(x, from_rows, modes, collective_id):
     shards = x.shape[0]
     return pl.pallas_call(
-        exchange_kernel,
+        functools.partial(exchange_kernel, from_rows, modes),
         in_specs=[pl.BlockSpec(memory_space=pl.ANY)],
         out_specs=pl.BlockSpec(memory_space=pl.ANY),
         out_shape=sds(x.shape, x.dtype),
@@ -202,10 +252,12 @@
         ref[t, pl.ds(pl.multiple_of(start, 8), n), :] = value[:, t * LANES : (t + 1) * LANES]
 
 
-def load_mode(wide_ref, m, slab):
+def load_mode(wide_ref, m, slab, modes):
     re = strided(wide_ref, 2 * m, LAT_PAD, slab)
     im = strided(wide_ref, 2 * m + 1, LAT_PAD, slab)
-    return jnp.concatenate([re, im], 0).astype(BF16)
+    live = lax.axis_index("lat") * modes + m < KEPT
+    value = jnp.concatenate([re, im], 0)
+    return jnp.where(live, value, jnp.zeros_like(value)).astype(BF16)
 
 
 def widen(recv_ref, wide_ref):
@@ -217,6 +269,12 @@
         return 0
 
     lax.fori_loop(0, shards, one, 0)
+    if LAT % rows:
+        first = LAT * slab
+        last = (LAT // rows + 1) * n
+        put_rows(wide_ref, first, jnp.zeros((last - first, width), F32))
+    for s in range(-(-LAT // rows), shards):
+        put_rows(wide_ref, s * n, jnp.zeros((n, width), F32))
 
 
 def store_mode(out_s, m, value):
@@ -251,7 +309,7 @@
         return jnp.concatenate([re, im], 0)
 
     def one(m, _):
-        fq = dot(fa_ref[...], load_mode(wide_s, m, slab)).astype(BF16)
+        fq = dot(fa_ref[...], load_mode(wide_s, m, slab, modes)).astype(BF16)
         freq_ref[m] = fq
         hid, gp = gelu_both(mix(fq, wi_ref, bi_ref))
         hid = hid.astype(BF16)
@@ -333,7 +391,7 @@
         return jnp.concatenate([re, im], 0)
 
     def one(m, _):
-        merged = dot(iat_ref[...], load_mode(wide_s, m, slab))
+        merged = dot(iat_ref[...], load_mode(wide_s, m, slab, modes))
         og = grads(hid_ref[m], merged * t2_ref[m], dwo_ref, dbo_ref)
         ig = grads(freq_ref[m], pull(og, wo_ref) * gp_ref[m], dwi_ref, dbi_ref)
         fg = pull(ig, wi_ref).astype(BF16)
@@ -366,41 +424,111 @@
     )(recv, tb["iat"], tb["fat"], wo, wi, freq, hid, gp, t2)
 
 
-def gather_row(r_ref, i):
+def gather_row(r_ref, row, modes):
     shards, _, slab, width = r_ref.shape
-    return r_ref[:, i].astype(F32).reshape(shards * slab, width).astype(BF16)
+    whole = KEPT // modes
+    parts = [r_ref[:whole, row].astype(F32).reshape(whole * slab, width)]
+    rest = (shards - whole) * slab
+    if KEPT % modes:
+        n = up8(2 * (KEPT % modes))
+        parts.append(r_ref[whole, row].astype(F32)[:n])
+        rest -= n
+    if rest:
+        parts.append(jnp.zeros((rest, width), F32))
+    return jnp.concatenate(parts, 0).astype(BF16)
 
 
 def feed_kernel(
-    per, chunk, scale_ref, x_ref, c_ref, r_ref, il_ref, ilt_ref, w1_ref, w2_ref, eb_ref, rb_ref,
+    per, chunk, modes, scale_ref, x_ref, c_ref, back_ref, il_ref, ilt_ref, w1_ref, w2_ref, eb_ref, rb_ref,
     ng_ref, ns_ref, pg_ref, ps_ref,
-    lo_ref, mg_ref, rg_ref, act_ref, pre_ref, sec_ref, up_ref, deb_ref, drb_ref, dpg_ref, dps_ref,
-    mixed_s, xhat_s, rs_s, branch_s, grad_s,
+    lo_ref, mg_ref, out_ref, act_ref, pre_ref, sec_ref, up_ref, deb_ref, drb_ref, dpg_ref, dps_ref,
+    recv_s, stage_s, mixed_s, xhat_s, rs_s, branch_s, grad_s,
+    in_send, in_recv, in_own, out_send, out_recv, out_own,
 ):
     g = pl.program_id(0)
+    steps = pl.num_programs(0)
     lon, width = x_ref.shape[1:]
     hidden = w1_ref.shape[1]
-    shards, _, slab, _ = r_ref.shape
+    shards, rows, slab, _ = recv_s.shape
+    me = lax.axis_index("lat")
+    dp = lax.axis_index("dp")
+
+    def incoming(step, i, sender, receiver, act):
+        part = pl.ds(step * per, per)
+
+        def piece(nr, ns):
+            act(send(
+                back_ref.at[receiver, part, pl.ds(0, ns)], recv_s.at[sender, part, pl.ds(0, ns)],
+                in_send.at[step, i], in_recv.at[step, i], dp, receiver,
+            ))
+
+        live = receiver * rows + step * per < LAT
+        each_size([(live, per)], slab_sizes(sender, modes, slab), piece)
+
+    def outgoing(step, i, sender, receiver, act):
+        part = pl.ds(step * per, per)
+
+        def piece(nr, ns):
+            act(send(
+                stage_s.at[receiver, part, pl.ds(0, ns)], out_ref.at[sender, part, pl.ds(0, ns)],
+                out_send.at[step, i], out_recv.at[step, i], dp, receiver,
+            ))
+
+        live = sender * rows + step * per < LAT
+        each_size([(live, per)], slab_sizes(receiver, modes, slab), piece)
+
+    def own_in(step):
+        part = pl.ds(step * per, per)
+        return pltpu.make_async_copy(back_ref.at[me, part], recv_s.at[me, part], in_own.at[step])
+
+    def own_out(step):
+        part = pl.ds(step * per, per)
+        return pltpu.make_async_copy(stage_s.at[me, part], out_ref.at[me, part], out_own.at[step])
+
+    def to(i):
+        return lax.rem(me + i, shards)
+
+    def source(i):
+        return lax.rem(me + shards - i, shards)
+
+    def peers(fn):
+        def one(i, _):
+            fn(i)
+            return 0
+
+        lax.fori_loop(1, shards, one, 0)
 
     @pl.when(g == 0)
     def _():
+        greet(shards, me, dp)
+
+        def one(step, _):
+            own_in(step).start()
+            peers(lambda i: incoming(step, i, me, to(i), lambda c: c.start()))
+            return 0
+
+        lax.fori_loop(0, steps, one, 0)
         for ref in (deb_ref, drb_ref, dpg_ref, dps_ref):
             ref[...] = jnp.zeros_like(ref)
 
+    own_in(g).wait()
+    peers(lambda i: incoming(g, i, source(i), me, lambda c: c.wait_recv()))
     for i in range(per):
-        rows = pl.ds(i * COLS, COLS)
+        rows_i = pl.ds(i * COLS, COLS)
         x = pad_rows(x_ref[i].astype(F32), COLS)
         c, rs = center_scale(x)
         first = c * rs * ng_ref[...] + ns_ref[...]
-        mixed = dot(il_ref[...], gather_row(r_ref, i)) + first + x
+        filtered = dot(il_ref[...], gather_row(recv_s, g * per + i, modes))
+        live = me * rows + g * per + i < LAT
+        mixed = jnp.where(live, filtered, jnp.zeros_like(filtered)) + first + x
         c, rs = center_scale(mixed)
         xhat = c * rs
-        mixed_s[rows, :] = mixed
-        xhat_s[rows, :] = xhat
-        rs_s[rows, :] = jnp.broadcast_to(rs, (COLS, 128))
-        sec_ref[rows, :] = (xhat * pg_ref[...] + ps_ref[...]).astype(BF16)
+        mixed_s[rows_i, :] = mixed
+        xhat_s[rows_i, :] = xhat
+        rs_s[rows_i, :] = jnp.broadcast_to(rs, (COLS, LANES))
+        sec_ref[rows_i, :] = (xhat * pg_ref[...] + ps_ref[...]).astype(BF16)
         up = (pad_rows(c_ref[i].astype(F32), COLS) * scale_ref[0, g * per + i]).astype(BF16)
-        up_ref[rows, :] = up
+        up_ref[rows_i, :] = up
         drb_ref[...] += jnp.sum(up.astype(F32), 0, keepdims=True)
     branch_s[...] = jnp.broadcast_to(rb_ref[...], branch_s.shape)
     grad_s[...] = jnp.zeros_like(grad_s)
@@ -419,40 +547,63 @@
 
     lax.fori_loop(0, hidden // chunk, hidden_chunk, 0)
     for i in range(per):
-        rows = pl.ds(i * COLS, COLS)
+        rows_i = pl.ds(i * COLS, COLS)
+        grad = grad_s[rows_i, :]
+        xhat = xhat_s[rows_i, :]
+        up = pad_rows(c_ref[i].astype(F32), COLS) * scale_ref[0, g * per + i]
+        mg = up + norm_back(grad, xhat, rs_s[rows_i, 0:1], pg_ref[...])
+        mg_ref[i] = mg[:lon]
+        rg = dot(ilt_ref[...], mg.astype(BF16)).astype(BF16)
+        stage_s[:, g * per + i] = rg.reshape(shards, slab, width)
+    own_out(g).start()
+    peers(lambda i: outgoing(g, i, me, to(i), lambda c: c.start()))
+    for i in range(per):
+        rows_i = pl.ds(i * COLS, COLS)
         keep = scale_ref[1, g * per + i]
-        lo_ref[i] = ((mixed_s[rows, :] + branch_s[rows, :]) * keep).astype(BF16)[:lon]
-        grad = grad_s[rows, :]
-        xhat = xhat_s[rows, :]
-        dpg_ref[...] += jnp.sum(grad * xhat, 0, keepdims=True)
+        lo_ref[i] = ((mixed_s[rows_i, :] + branch_s[rows_i, :]) * keep).astype(BF16)[:lon]
+        grad = grad_s[rows_i, :]
+        dpg_ref[...] += jnp.sum(grad * xhat_s[rows_i, :], 0, keepdims=True)
         dps_ref[...] += jnp.sum(grad, 0, keepdims=True)
-        up = pad_rows(c_ref[i].astype(F32), COLS) * scale_ref[0, g * per + i]
-        mg = up + norm_back(grad, xhat, rs_s[rows, 0:1], pg_ref[...])
-        mg_ref[i] = mg[:lon]
-        rg_ref[:, i] = dot(ilt_ref[...], mg.astype(BF16)).astype(BF16).reshape(shards, slab, width)
-
-
-def feed(scale, x, cot, recv, tb, w1, w2, eb, rb, ng, ns, pg, ps):
+
+    @pl.when(g == steps - 1)
+    def _():
+        def one(step, _):
+            own_out(step).wait()
+
+            def wait_all(i):
+                incoming(step, i, me, to(i), lambda c: c.wait_send())
+                outgoing(step, i, me, to(i), lambda c: c.wait_send())
+                outgoing(step, i, source(i), me, lambda c: c.wait_recv())
+
+            peers(wait_all)
+            return 0
+
+        lax.fori_loop(0, steps, one, 0)
+
+
+def feed(scale, x, cot, back, tb, w1, w2, eb, rb, ng, ns, pg, ps, modes, collective_id):
     rows, lon, width = x.shape
     hidden = w1.shape[1]
-    shards, _, slab, _ = recv.shape
+    shards, _, slab, _ = back.shape
     per = 3 if rows % 3 == 0 else 1
+    steps = rows // per
     row = pl.BlockSpec((per, lon, width), lambda g: (g, 0, 0))
-    slabs = pl.BlockSpec((shards, per, slab, width), lambda g: (0, g, 0, 0))
+    any_ = pl.BlockSpec(memory_space=pl.ANY)
     flat = lambda w: pl.BlockSpec((per * COLS, w), lambda g: (g, 0))
     vec = lambda w: pl.BlockSpec((1, w), lambda g: (0, 0))
     tall = per * COLS
+    dma = pltpu.SemaphoreType.DMA
     return pl.pallas_call(
-        functools.partial(feed_kernel, per, 512),
-        grid=(rows // per,),
-        in_specs=[pl.BlockSpec(memory_space=pltpu.SMEM), row, row, slabs]
+        functools.partial(feed_kernel, per, 512, modes),
+        grid=(steps,),
+        in_specs=[pl.BlockSpec(memory_space=pltpu.SMEM), row, row, any_]
         + [full(a) for a in (tb["il"], tb["ilt"], w1, w2, eb, rb, ng, ns, pg, ps)],
-        out_specs=[row, row, slabs, flat(hidden), flat(hidden), flat(width), flat(width)]
+        out_specs=[row, row, any_, flat(hidden), flat(hidden), flat(width), flat(width)]
         + [vec(hidden), vec(width), vec(width), vec(width)],
         out_shape=[
             sds((rows, lon, width), BF16),
             sds((rows, lon, width), F32),
-            sds(recv.shape, BF16),
+            sds(back.shape, BF16),
             sds((rows * COLS, hidden), BF16),
             sds((rows * COLS, hidden), BF16),
             sds((rows * COLS, width), BF16),
@@ -463,18 +614,22 @@
             sds((1, width), F32),
         ],
         scratch_shapes=[
+            pltpu.VMEM(back.shape, BF16),
+            pltpu.VMEM(back.shape, BF16),
             pltpu.VMEM((tall, width), F32),
             pltpu.VMEM((tall, width), F32),
-            pltpu.VMEM((tall, 128), F32),
+            pltpu.VMEM((tall, LANES), F32),
             pltpu.VMEM((tall, width), F32),
             pltpu.VMEM((tall, width), F32),
+            dma((steps, shards)), dma((steps, shards)), dma((steps,)),
+            dma((steps, shards)), dma((steps, shards)), dma((steps,)),
         ],
-        compiler_params=params(),
+        compiler_params=params(collective_id=collective_id, has_side_effects=True),
         name="feed",
-    )(scale, x, cot, recv, tb["il"], tb["ilt"], w1, w2, eb, rb, ng, ns, pg, ps)
-
-
-def leave_kernel(x_ref, r_ref, mg_ref, fl_ref, gain_ref, out_ref, dg_ref, db_ref):
+    )(scale, x, cot, back, tb["il"], tb["ilt"], w1, w2, eb, rb, ng, ns, pg, ps)
+
+
+def leave_kernel(modes, x_ref, r_ref, mg_ref, fl_ref, gain_ref, out_ref, dg_ref, db_ref):
     lon = x_ref.shape[1]
 
     @pl.when(pl.program_id(0) == 0)
@@ -486,19 +641,21 @@
     c, rs = center_scale(x)
     xhat = c * rs
     mg = pad_rows(mg_ref[0], COLS)
-    grad = dot(fl_ref[...], gather_row(r_ref, 0)) + mg
+    live = lax.axis_index("lat") * pl.num_programs(0) + pl.program_id(0) < LAT
+    spread = dot(fl_ref[...], gather_row(r_ref, 0, modes))
+    grad = jnp.where(live, spread, jnp.zeros_like(spread)) + mg
     dg_ref[...] += jnp.sum(grad * xhat, 0, keepdims=True)
     db_ref[...] += jnp.sum(grad, 0, keepdims=True)
     out_ref[0] = (mg + norm_back(grad, xhat, rs, gain_ref[...]))[:lon]
 
 
-def leave(x, recv, mg, fl, gain):
+def leave(x, recv, mg, fl, gain, modes):
     rows, lon, width = x.shape
     shards, _, slab, _ = recv.shape
     row = pl.BlockSpec((1, lon, width), lambda r: (r, 0, 0))
     vec = pl.BlockSpec((1, width), lambda r: (0, 0))
     return pl.pallas_call(
-        leave_kernel,
+        functools.partial(leave_kernel, modes),
         grid=(rows,),
         in_specs=[row, pl.BlockSpec((shards, 1, slab, width), lambda r: (0, r, 0, 0)), row, full(fl), full(gain)],
         out_specs=[row, vec, vec],
@@ -548,19 +705,18 @@
     wi, wi_back = dense_weights(inner_weight)
     wo, wo_back = dense_weights(outer_weight)
 
-    spec = exchange(enter(x, tb["flt"], ng, ns, shards, slab), 0)
+    spec = exchange(enter(x, tb["flt"], ng, ns, shards, slab), True, modes, 0)
     back, freq, hid, gp, t2 = spectral_forward(spec, tb, wi, bi, wo, bo, modes)
-    row_spec = exchange(back, 1)
-    (layer_out, mixed_grad, row_grad, act, pre, second, up, deb, drb, dpg, dps) = feed(
-        scale, x, cot, row_spec, tb, expand_weight, reduce_weight, eb, rb, ng, ns, pg, ps
+    (layer_out, mixed_grad, mode_grad, act, pre, second, up, deb, drb, dpg, dps) = feed(
+        scale, x, cot, back, tb, expand_weight, reduce_weight, eb, rb, ng, ns, pg, ps, modes, 1
     )
-    dw2 = dot_tn(act, up)
-    dw1 = dot_tn(second, pre)
+    dw2 = dot_tn(act, up).astype(BF16)
+    dw1 = dot_tn(second, pre).astype(BF16)
     dw1, dw2 = lax.psum((dw1, dw2), ("dp", "lat"))
-    mode_grad = exchange(row_grad, 2)
+    dw1, dw2 = dw1.astype(F32), dw2.astype(F32)
     slab_grad, dwo, dbo, dwi, dbi = spectral_backward(mode_grad, tb, wo_back, wi_back, freq, hid, gp, t2)
-    lon_grad = exchange(slab_grad, 3)
-    input_grad, dng, dns = leave(x, lon_grad, mixed_grad, tb["fl"], ng)
+    lon_grad = exchange(slab_grad, False, modes, 2)
+    input_grad, dng, dns = leave(x, lon_grad, mixed_grad, tb["fl"], ng, modes)
     small = lax.psum(
         (dng, dns, block_grads(dwi), dbi, block_grads(dwo), dbo, dpg, dps, deb, drb), ("dp", "lat")
     )

time: 913 us -> 758 us (0.83)
  Pallas kernels: 520 us -> 424 us
  waiting for transfers between devices: 211 us -> 152 us
  other arithmetic: 6.12 us -> 16.8 us
    pallas_call x6 -> x4, Pallas kernels: 417 us -> 319 us  [the longest x1 182 us: feed(): pl.pallas_call(functools.partial(feed_kernel, per, 512, modes), grid=(ste...]
    psum x1, waiting for transfers between devices: 211 us -> 127 us  [shards_fn(): lax.psum((dng, dns, block_grads(dwi), dbi, block_grads(dwo), dbo, dpg, dp...]
    psum x0 -> x1, waiting for transfers between devices: none -> 24.7 us  [shards_fn(): dw1, dw2 = lax.psum((dw1, dw2), ('dp', 'lat'))]
    unnamed x53 -> x36, local copies, waits for them, and re-layouts: 26 us -> 13.8 us
    convert_element_type x0 -> x2, other arithmetic: none -> 12 us  [shards_fn(): dw1, dw2 = (dw1.astype(F32), dw2.astype(F32))]
  transfers between devices with their start and end apart: 1 -> 2, of which waited for: 1 -> 2; matrix products, arithmetic and copies ran while one was open for 1% -> 5% of each run, Pallas kernels for 13% -> 17%
where the time goes in v2:
time: 758 us; the launch traced here: 757 us
  Pallas kernels  424 us (56%)
  waiting for transfers between devices  152 us (20%)
  blocking collectives  68.8 us (9%)
  local copies, waits for them, and re-layouts  50.4 us (7%)
  matrix products  30.2 us (4%)
  other arithmetic  16.8 us (2%)
  between operations  15 us (2%)
    pallas_call x1, Pallas kernels, feed(): pl.pallas_call(functools.partial(feed_kernel, per, 512, modes), grid=(ste...  182 us
    psum x1, waiting for transfers between devices, shards_fn(): lax.psum((dng, dns, block_grads(dwi), dbi, block_grads(dwo), dbo, dpg, dp...  127 us
    pallas_call x2, Pallas kernels, exchange(): pl.pallas_call(functools.partial(exchange_kernel, from_rows, modes), in_s...  124 us
    psum x1, blocking collectives, shards_fn(): lax.psum((dng, dns, block_grads(dwi), dbi, block_grads(dwo), dbo, dpg, dp...  68.8 us
    pallas_call x1, Pallas kernels, spectral_backward(): pl.pallas_call(spectral_backward_kernel, grid=(GROUPS,), in_specs=[slabs,...  52.2 us
    pallas_call x1, Pallas kernels, spectral_forward(): pl.pallas_call(spectral_forward_kernel, grid=(GROUPS,), in_specs=[slabs,...  41.7 us
    dot_general x2, matrix products, dot_tn(): lax.dot_general(a, b, (((0,), (0,)), ((), ())), preferred_element_type=F32)  30.2 us
    psum x1, waiting for transfers between devices, shards_fn(): dw1, dw2 = lax.psum((dw1, dw2), ('dp', 'lat'))  24.7 us
  transfers between devices with their start and end apart: 2, of which 2 were waited for; matrix products, arithmetic and copies ran while one was open for 5% of the time, Pallas kernels for 17%

profile of v2, /device:TPU:0, one launch (start us, length us, event | category | flops | bytes accessed | tf_op | source)
XLA Modules:
  0.0 756.8 jit_solution(2148973310143219235)
XLA Ops:
  19.5 10.6 %enter.1.src_ref = bf16[8,12,24,768]{3,2,1,0:T(8,128)(2,1)} custom-call(bf16[12,180,768]{2,1,0:T(8,128)(2,1)} %bitcast.51, bf16[192,192]{1,0:T(8,128)(2,1)} %constant.27.clone.flt_ref, f32[1,768]{1,0:T(1,128)} %reshape.130.gain_ref.ng_ref, f32[1,768]{1,0:T(1,128)} %reshape.131.shift_ref.ns_ref), custom_call_target="tpu_custom_call" | custom-call | tf_op jit(solution)/shard_map/enter/pallas_call | solution.py:138
  30.1 60.2 %exchange.2.recv_ref = bf16[8,12,24,768]{3,2,1,0:T(8,128)(2,1)} custom-call(bf16[8,12,24,768]{3,2,1,0:T(8,128)(2,1)} %enter.1.src_ref), custom_call_target="tpu_custom_call" | custom-call | bytes 7077888 | tf_op jit(solution)/shard_map/exchange/pallas_call | solution.py:229
  90.2 3.3 multiply_bitcast_fusion.2
  93.5 3.2 copy.38
  96.8 2.2 reshape.134.wi_ref
  98.9 2.0 copy.40
  101.0 2.2 reshape.138.wo_ref
  103.7 41.7 %spectral_forward.1 = (bf16[8,12,24,768]{3,2,1,0:T(8,128)(2,1)}, bf16[12,192,768]{2,1,0:T(8,128)(2,1)}, bf16[12,192,768]{2,1,0:T(8,128)(2,1)}, f32[12,192,768]{2,1,0:T(8,128)}, f32[12,192,768]{2,1,0:T(8,128)}) custom-call(bf16[8,12,24,768]{3,2,1,0:T(8,128)(2,1)} %exchange.2.recv_ref, bf16[192,192]{1,0:T(8,128)(2,1)} %constant.30.clone.fa_ref.iat_ref, ...), custom_call_target="tpu_custom_call" | custom-call | tf_op jit(solution)/shard_map/spectral_forward/pallas_call | solution.py:343
  145.4 182.3 %feed.1 = (bf16[12,180,768]{2,1,0:T(8,128)(2,1)}, f32[12,180,768]{2,1,0:T(8,128)}, bf16[8,12,24,768]{3,2,1,0:T(8,128)(2,1)}, bf16[2304,3072]{1,0:T(8,128)(2,1)},...) custom-call(f32[2,12]{1,0:T(2,128)} %pad_maximum_fusion.scale_ref, ...), custom_call_target="tpu_custom_call" | custom-call | tf_op jit(solution)/shard_map/feed/pallas_call | solution.py:596
  327.8 17.2 %convolution_convert_fusion = bf16[768,3072]{1,0:T(8,128)(2,1)} fusion(bf16[2304,768]{1,0:T(8,128)(2,1)} %get-tuple-element.56, bf16[2304,3072]{1,0:T(8,128)(2,1)} %get-tuple-element.57), kind=kOutput, calls=%fused_computation | convolution fusion | flops 10873995264 | bytes 22413312 | tf_op jit(solution)/shard_map/dot_general | solution.py:89
  345.0 13.0 %convolution_convert_fusion.1 = bf16[3072,768]{1,0:T(8,128)(2,1)} fusion(bf16[2304,3072]{1,0:T(8,128)(2,1)S(1)} %copy-done.14, bf16[2304,768]{1,0:T(8,128)(2,1)S(1)} %copy-done.15), kind=kOutput, calls=%fused_computation.1 | convolution fusion | flops 10873995264 | bytes 22413312 | tf_op jit(solution)/shard_map/dot_general | solution.py:89
  359.4 2.1 reshape.145.wi_ref
  361.5 2.1 reshape.144.wo_ref
  363.7 52.2 %spectral_backward.1 = (bf16[8,12,24,768]{3,2,1,0:T(8,128)(2,1)}, f32[2,384,768]{2,1,0:T(8,128)}, f32[2,768]{1,0:T(2,128)}, f32[2,384,768]{2,1,0:T(8,128)}, f32[2,768]{1,0:T(2,128)}) custom-call(bf16[8,12,24,768]{3,2,1,0:T(8,128)(2,1)} %get-tuple-element.40.recv_ref, bf16[192,192]{1,0:T(8,128)(2,1)} %constant.30.clone.fa_ref.iat_ref, ...), custom_call_target="tpu_custom_call" | custom-call | tf_op jit(solution)/shard_map/spectral_backward/pallas_call | solution.py:412
  415.9 3.8 reshape.148
  421.8 3.8 reshape.151
  427.8 63.5 %exchange.3.r_ref = bf16[8,12,24,768]{3,2,1,0:T(8,128)(2,1)} custom-call(bf16[8,12,24,768]{3,2,1,0:T(8,128)(2,1)} %get-tuple-element.45.src_ref), custom_call_target="tpu_custom_call" | custom-call | bytes 7077888 | tf_op jit(solution)/shard_map/exchange/pallas_call | solution.py:229
  491.3 13.3 %leave.1 = (f32[12,180,768]{2,1,0:T(8,128)}, f32[1,768]{1,0:T(1,128)}, f32[1,768]{1,0:T(1,128)}) custom-call(bf16[12,180,768]{2,1,0:T(8,128)(2,1)} %bitcast.53, bf16[8,12,24,768]{3,2,1,0:T(8,128)(2,1)} %exchange.3.r_ref, f32[12,180,768]{2,1,0:T(8,128)} %get-tuple-element.46.mg_ref, bf16[192,192]{1,0:T(8,128)(2,1)} %constant.26.clone.fl_ref, ...), custom_call_target="tpu_custom_call" | custom-call | tf_op jit(solution)/shard_map/leave/pallas_call | solution.py:657
  504.7 8.9 %copy.49 = f32[1,12,180,768]{3,0,2,1:T(1,128)} copy(f32[1,12,180,768]{3,2,1,0:T(8,128)} %bitcast.54) | data formatting | bytes 13271040
  513.9 68.8 %all-reduce = (f32[768]{0:T(1024)}, f32[768]{0:T(1024)}, f32[2,8,96]{2,1,0:T(8,128)}, f32[2,8,96]{2,1,0:T(8,128)}, f32[768]{0:T(1024)}, /*index=5*/f32[768]{0:T(1024)}, f32[3072]{0:T(1024)}, f32[768]{0:T(1024)}) all-reduce(f32[768]{0:T(1024)S(1)} %reduce, f32[768]{0:T(1024)S(1)} %reduce.1, ...), channel_id=1, replica_groups=mesh['dp'=4,'lat'=8] {'dp','lat'}, use_global_device_ids=true, to_apply=%region_0.0 | all-reduce | flops 9984 | bytes 79872 | tf_op jit(solution)/shard_map/psum | solution.py:720
  582.7 24.7 %all-reduce.8.cloned.1.call-done = (bf16[768,3072]{1,0:T(8,128)(2,1)}, bf16[3072,768]{1,0:T(8,128)(2,1)}) async-done(((bf16[768,3072]{1,0:T(8,128)(2,1)}, bf16[3072,768]{1,0:T(8,128)(2,1)}), (bf16[768,3072]{1,0:T(8,128)(2,1)}, bf16[3072,768]{1,0:T(8,128)(2,1)})) %all-reduce.8.cloned.1.call-update) | async-done | bytes 9437200 | tf_op jit(solution)/shard_map/psum | solution.py:715
  607.4 7.5 convert_element_type.31
  614.9 4.5 convert_element_type.33
  619.4 127.0 %all-reduce.6.cloned.1.call-done = (f32[2,8,96,96]{3,2,1,0:T(8,128)}, f32[2,8,96,96]{3,2,1,0:T(8,128)}) async-done(((f32[2,8,96,96]{3,2,1,0:T(8,128)}, f32[2,8,96,96]{3,2,1,0:T(8,128)}), (f32[2,8,96,96]{3,2,1,0:T(8,128)}, f32[2,8,96,96]{3,2,1,0:T(8,128)})) %all-reduce.6.cloned.1.call-update) | async-done | bytes 1179664 | tf_op jit(solution)/shard_map/psum | solution.py:720
  (65 shorter events, 21.7 us)
Async XLA Ops:
  7.2 600.2 %all-reduce.8.cloned.1.call-start = ((), (), s32[]{:S(2)}) async-start(), calls=%async_computation.1 | async-start | bytes 18874368 | tf_op jit(solution)/shard_map/psum | solution.py:715
  327.8 17.3 %copy-start.14 = (bf16[2304,3072]{1,0:T(8,128)(2,1)S(1)}, bf16[2304,3072]{1,0:T(8,128)(2,1)}, u32[]{:S(2)}) copy-start(bf16[2304,3072]{1,0:T(8,128)(2,1)} %get-tuple-element.59) | copy-start | bytes 42467332
  327.8 17.3 %copy-start.15 = (bf16[2304,768]{1,0:T(8,128)(2,1)S(1)}, bf16[2304,768]{1,0:T(8,128)(2,1)}, u32[]{:S(2)}) copy-start(bf16[2304,768]{1,0:T(8,128)(2,1)} %get-tuple-element.60) | copy-start | bytes 10616836
  358.0 1.4 copy-start.1
  358.0 3.5 copy-start
  358.0 388.4 %all-reduce.6.cloned.1.call-start = ((), (), s32[]{:S(2)}) async-start(), calls=%async_computation | async-start | bytes 3145728 | tf_op jit(solution)/shard_map/psum | solution.py:720
  504.7 9.0 %copy-start.13 = (f32[1,768]{1,0:T(1,128)S(1)}, f32[1,768]{1,0:T(1,128)}, u32[]{:S(2)}) copy-start(f32[1,768]{1,0:T(1,128)} %get-tuple-element.48) | copy-start | bytes 9220
  504.7 9.0 %copy-start.12 = (f32[1,768]{1,0:T(1,128)S(1)}, f32[1,768]{1,0:T(1,128)}, u32[]{:S(2)}) copy-start(f32[1,768]{1,0:T(1,128)} %get-tuple-element.49) | copy-start | bytes 9220
  504.7 9.0 %copy-start.11 = (f32[1,768]{1,0:T(1,128)S(1)}, f32[1,768]{1,0:T(1,128)}, u32[]{:S(2)}) copy-start(f32[1,768]{1,0:T(1,128)} %get-tuple-element.54) | copy-start | bytes 9220
  504.7 9.0 %copy-start.10 = (f32[1,768]{1,0:T(1,128)S(1)}, f32[1,768]{1,0:T(1,128)}, u32[]{:S(2)}) copy-start(f32[1,768]{1,0:T(1,128)} %get-tuple-element.55) | copy-start | bytes 9220
  504.7 9.1 %copy-start.9 = (f32[1,768]{1,0:T(1,128)S(1)}, f32[1,768]{1,0:T(1,128)}, u32[]{:S(2)}) copy-start(f32[1,768]{1,0:T(1,128)} %get-tuple-element.61) | copy-start | bytes 9220
  504.7 9.1 %copy-start.8 = (f32[2,768]{1,0:T(2,128)S(1)}, f32[2,768]{1,0:T(2,128)}, u32[]{:S(2)}) copy-start(f32[2,768]{1,0:T(2,128)} %get-tuple-element.51) | copy-start | bytes 18436
  504.7 9.2 %copy-start.7 = (f32[2,768]{1,0:T(2,128)S(1)}, f32[2,768]{1,0:T(2,128)}, u32[]{:S(2)}) copy-start(f32[2,768]{1,0:T(2,128)} %get-tuple-element.53) | copy-start | bytes 18436
  504.7 9.2 %copy-start.6 = (f32[1,3072]{1,0:T(1,128)S(1)}, f32[1,3072]{1,0:T(1,128)}, u32[]{:S(2)}) copy-start(f32[1,3072]{1,0:T(1,128)} %get-tuple-element.58) | copy-start | bytes 36868
  607.4 7.5 copy-start.2
  614.9 131.5 %copy-start.3 = (bf16[12,180,768]{2,1,0:T(8,128)(2,1)S(1)}, bf16[12,180,768]{2,1,0:T(8,128)(2,1)}, u32[]{:S(2)}) copy-start(bf16[12,180,768]{2,1,0:T(8,128)(2,1)} %get-tuple-element.39) | copy-start | bytes 9953284
  746.4 1.8 copy-start.5
  746.4 2.6 copy-start.4
Sparse Core Ops, SparseCore 0:
  358.1 249.2 all-reduce.7
  614.4 132.0 all-reduce.5

commit v3 on v2

v3 whole, which is shorter than its diff:
```python
import functools
import math

import jax
import jax.numpy as jnp
import ml_dtypes
import numpy as np
from jax import lax
from jax.experimental import pallas as pl
from jax.experimental.pallas import tpu as pltpu
from jax.sharding import PartitionSpec as P

BLOCKS = 8
LAT = 90
LON = 180
LAT_PAD = 96
LON_PAD = 96
KEPT = LON // 2 + 1
COLS = 192
GROUPS = 2
LANES = 128
LOW_ROWS = 16
NORM_G, NORM_S, POST_G, POST_S, REDUCE_B, INNER_B, OUTER_B, EXPAND_B = 0, 1, 2, 3, 4, 5, 7, 9

SHRINK = 0.01
EPS = 1e-6
SQRT_HALF = 0.7071067811865476
PDF_SCALE = 0.3989422804014327

F32 = jnp.float32
BF16 = jnp.bfloat16
MESH = pl.DeviceIdType.MESH
VMEM_LIMIT = 62 * 2**20


def base_tables():
    f = np.float32
    modes = np.arange(LON_PAD)
    columns = np.arange(LON)
    phases = (columns[:, None] * modes[None, :] % LON).astype(f) * f(2.0 * math.pi / LON)
    kept = (modes < LON // 2 + 1).astype(f)
    factor = np.where((modes == 0) | (modes == LON // 2), f(1), f(2)) * kept
    scale = f(1.0 / math.sqrt(LON))
    forward_lon = np.stack([np.cos(phases) * kept, -np.sin(phases) * kept], axis=1) * scale
    inverse_lon = np.stack([np.cos(phases) * factor, -np.sin(phases) * factor], axis=1) * scale
    rows = np.arange(LAT_PAD)
    angles = (rows[:, None] * rows[None, :] % LAT).astype(f) * f(2.0 * math.pi / LAT)
    inside = ((rows[:, None] < LAT) & (rows[None, :] < LAT)).astype(f) / f(math.sqrt(LAT))
    cs = np.cos(angles) * inside
    sn = np.sin(angles) * inside
    forward_lat = np.stack([np.stack([cs, sn], 1), np.stack([-sn, cs], 1)], 0)
    inverse_lat = np.stack([np.stack([cs, -sn], 1), np.stack([sn, cs], 1)], 0)
    return forward_lon, inverse_lon, forward_lat, inverse_lat


def slab_rows(modes):
    return -(-2 * modes // 8) * 8


def lon_table(table, shards, modes):
    slab = slab_rows(modes)
    out = np.zeros((COLS, shards, slab), np.float32)
    split = table.reshape(LON, 2, shards, modes).transpose(0, 2, 3, 1)
    out[:LON, :, : 2 * modes] = split.reshape(LON, shards, 2 * modes)
    return out.reshape(COLS, shards * slab)


def make_tables(shards, modes):
    forward_lon, inverse_lon, forward_lat, inverse_lat = base_tables()
    low = lambda t: jnp.asarray(np.ascontiguousarray(t).astype(ml_dtypes.bfloat16))
    n = 2 * LAT_PAD
    fl = lon_table(forward_lon, shards, modes)
    il = lon_table(inverse_lon, shards, modes)
    fa = forward_lat.reshape(n, n)
    ia = inverse_lat.reshape(n, n)
    return dict(
        fl=low(fl), flt=low(fl.T), il=low(il), ilt=low(il.T),
        fa=low(fa), fat=low(fa.T), ia=low(ia), iat=low(ia.T),
    )


def dot(a, b):
    return jnp.dot(a, b, preferred_element_type=F32)


def dot_nt(a, b):
    return lax.dot_general(a, b, (((1,), (1,)), ((), ())), preferred_element_type=F32)


def dot_tn(a, b):
    return lax.dot_general(a, b, (((0,), (0,)), ((), ())), preferred_element_type=F32)


def gelu_both(v):
    cdf = 0.5 * (1.0 + lax.erf(v * SQRT_HALF))
    pdf = jnp.exp(-0.5 * v * v) * PDF_SCALE
    return v * cdf, cdf + v * pdf


def center_scale(v):
    inv = 1.0 / v.shape[-1]
    c = v - jnp.sum(v, -1, keepdims=True) * inv
    return c, lax.rsqrt(jnp.sum(c * c, -1, keepdims=True) * inv + EPS)


def pad_rows(v, n):
    return jnp.concatenate([v, jnp.zeros((n - v.shape[0], v.shape[1]), v.dtype)], 0)


def norm_back(grad, xhat, rs, gain):
    inv = 1.0 / grad.shape[-1]
    dx = grad * gain
    m1 = jnp.sum(dx, -1, keepdims=True) * inv
    m2 = jnp.sum(dx * xhat, -1, keepdims=True) * inv
    return rs * (dx - m1 - xhat * m2)


def full(a):
    return pl.BlockSpec(a.shape, lambda *_: (0,) * a.ndim, pipeline_mode=pl.Buffered(1))


def sds(shape, dtype):
    return jax.ShapeDtypeStruct(shape, dtype)


def params(**kw):
    return pltpu.CompilerParams(vmem_limit_bytes=VMEM_LIMIT, **kw)


def vector(v_ref, row):
    return v_ref[row : row + 1, :]


def enter_kernel(x_ref, flt_ref, v_ref, out_ref):
    shards, _, slab, width = out_ref.shape
    x = pad_rows(x_ref[0].astype(F32), COLS)
    c, rs = center_scale(x)
    first = (c * rs * vector(v_ref, NORM_G) + vector(v_ref, NORM_S)).astype(BF16)
    out_ref[:, 0] = dot(flt_ref[...], first).astype(BF16).reshape(shards, slab, width)


def enter(x, flt, vectors, shards, slab):
    rows, lon, width = x.shape
    return pl.pallas_call(
        enter_kernel,
        grid=(rows,),
        in_specs=[pl.BlockSpec((1, lon, width), lambda r: (r, 0, 0)), full(flt), full(vectors)],
        out_specs=pl.BlockSpec((shards, 1, slab, width), lambda r: (0, r, 0, 0)),
        out_shape=sds((shards, rows, slab, width), BF16),
        compiler_params=params(),
        name="enter",
    )(x, flt, vectors)


def up8(n):
    return -(-n // 8) * 8


def slab_sizes(index, modes, slab):
    sizes = [(index < KEPT // modes, slab)]
    if KEPT % modes:
        sizes.append((index == KEPT // modes, up8(2 * (KEPT % modes))))
    return sizes


def row_sizes(index, rows):
    sizes = [(index < LAT // rows, rows)]
    if LAT % rows:
        sizes.append((index == LAT // rows, LAT % rows))
    return sizes


def each_size(row_options, slab_options, fn):
    for row_ok, nr in row_options:
        for slab_ok, ns in slab_options:
            pl.when(row_ok & slab_ok)(functools.partial(fn, nr, ns))


def greet(shards, me, dp):
    barrier = pltpu.get_barrier_semaphore()

    def one(i, _):
        peer = lax.rem(me + i, shards)
        pl.semaphore_signal(barrier, inc=1, device_id=(dp, peer), device_id_type=MESH)
        return 0

    lax.fori_loop(1, shards, one, 0)
    pl.semaphore_wait(barrier, shards - 1)


def send(src, dst, send_sem, recv_sem, dp, peer):
    return pltpu.make_async_remote_copy(
        src_ref=src, dst_ref=dst, send_sem=send_sem, recv_sem=recv_sem,
        device_id=(dp, peer), device_id_type=MESH,
    )


def exchange_kernel(from_rows, modes, src_ref, out_ref, send_sem, recv_sem, own_sem):
    shards, rows, slab, _ = src_ref.shape
    me = lax.axis_index("lat")
    dp = lax.axis_index("dp")
    greet(shards, me, dp)
    own = pltpu.make_async_copy(src_ref.at[me], out_ref.at[me], own_sem)
    own.start()

    def go(i, sender, receiver, act):
        row_owner, mode_owner = (sender, receiver) if from_rows else (receiver, sender)

        def piece(nr, ns):
            part = (pl.ds(0, nr), pl.ds(0, ns))
            copy = send(
                src_ref.at[(receiver,) + part], out_ref.at[(sender,) + part],
                send_sem.at[i], recv_sem.at[i], dp, receiver,
            )
            act(copy)

        each_size(row_sizes(row_owner, rows), slab_sizes(mode_owner, modes, slab), piece)

    def start(i, _):
        go(i, me, lax.rem(me + i, shards), lambda copy: copy.start())
        return 0

    def finish(i, _):
        go(i, me, lax.rem(me + i, shards), lambda copy: copy.wait_send())
        go(i, lax.rem(me + shards - i, shards), me, lambda copy: copy.wait_recv())
        return 0

    lax.fori_loop(1, shards, start, 0)
    own.wait()
    lax.fori_loop(1, shards, finish, 0)


def exchange(x, from_rows, modes, collective_id):
    shards = x.shape[0]
    return pl.pallas_call(
        functools.partial(exchange_kernel, from_rows, modes),
        in_specs=[pl.BlockSpec(memory_space=pl.ANY)],
        out_specs=pl.BlockSpec(memory_space=pl.ANY),
        out_shape=sds(x.shape, x.dtype),
        scratch_shapes=[
            pltpu.SemaphoreType.DMA((shards,)),
            pltpu.SemaphoreType.DMA((shards,)),
            pltpu.SemaphoreType.DMA,
        ],
        compiler_params=pltpu.CompilerParams(collective_id=collective_id, has_side_effects=True),
        cost_estimate=pl.CostEstimate(flops=0, bytes_accessed=2 * x.size * 2, transcendentals=0),
        name="exchange",
    )(x)


def halving_plan(groups, shards, n, turn):
    dp_bits = [("dp", b) for b in range(groups.bit_length() - 1)]
    lat_bits = [("lat", b) for b in range(shards.bit_length() - 1)]
    middle = dp_bits[1:2] + lat_bits[:2]
    turn = turn % len(middle)
    order = dp_bits[:1] + middle[turn:] + middle[:turn] + dp_bits[2:] + lat_bits[2:]
    plan = []
    for axis, bit in order:
        halved = n % (2 * LOW_ROWS) == 0
        plan.append((axis, bit, n, halved))
        n = n // 2 if halved else n
    return plan, n


def halving_plans(groups, shards, sizes):
    return [
        (k, t * size // 3) + halving_plan(groups, shards, size // 3, t)
        for k, size in enumerate(sizes)
        for t in range(3)
    ]


def halving_walk(first, plan, dp, me):
    offsets, bits, peers = [first], [], []
    for axis, bit, n, halved in plan:
        index = dp if axis == "dp" else me
        b = lax.rem(index // 2**bit, 2)
        other = index + 2**bit * (1 - 2 * b)
        peers.append((other, me) if axis == "dp" else (dp, other))
        bits.append(b)
        offsets.append(offsets[-1] + b * (n // 2) if halved else offsets[-1])
    return offsets, bits, peers


def sorted_peers(groups, shards, dp, me):
    out = []
    for axis, count in (("dp", groups), ("lat", shards)):
        index = dp if axis == "dp" else me
        for bit in range(count.bit_length() - 1):
            other = index + 2**bit * (1 - 2 * lax.rem(index // 2**bit, 2))
            out.append((other, me) if axis == "dp" else (dp, other))
    return out


def rows_at(start, n, unit=8):
    return pl.ds(pl.multiple_of(start, unit), n)


def low_rows_at(start, n):
    return rows_at(start, n, LOW_ROWS)


def signal_all(devices):
    barrier = pltpu.get_barrier_semaphore()
    for device in devices:
        pl.semaphore_signal(barrier, inc=1, device_id=device, device_id_type=MESH)
    pl.semaphore_wait(barrier, len(devices))


def received(plan):
    return sum(n // 2 if halved else n for _, _, n, halved in plan)


class Halving:
    def __init__(self, plans, accs, recvs, send_sems, recv_sems, dp, me):
        self.plans, self.accs, self.recvs = plans, accs, recvs
        self.send_sems, self.recv_sems = send_sems, recv_sems
        self.walks = [halving_walk(first, plan, dp, me) for _, first, plan, _ in plans]
        self.stages = len(plans[0][2])

    def base(self, j, stage):
        k, _, plan, _ = self.plans[j]
        before = sum(received(p) for which, _, p, _ in self.plans[:j] if which == k)
        return before + received(plan[:stage])

    def copy(self, j, stage):
        k = self.plans[j][0]
        _, _, n, halved = self.plans[j][2][stage]
        offsets, bits, peers = self.walks[j]
        count = n // 2 if halved else n
        start = offsets[stage] + (1 - bits[stage]) * count if halved else offsets[stage]
        return pltpu.make_async_remote_copy(
            src_ref=self.accs[k].at[low_rows_at(start, count)],
            dst_ref=self.recvs[k].at[pl.ds(self.base(j, stage), count)],
            send_sem=self.send_sems.at[j, stage], recv_sem=self.recv_sems.at[j, stage],
            device_id=peers[stage], device_id_type=MESH,
        )

    def start(self, stage):
        for j in range(len(self.plans)):
            self.copy(j, stage).start()

    def finish(self, stage):
        for j in range(len(self.plans)):
            self.copy(j, stage).wait()
            k = self.plans[j][0]
            _, _, n, halved = self.plans[j][2][stage]
            count = n // 2 if halved else n
            first = self.walks[j][0][stage + 1]
            base = self.base(j, stage)
            acc, recv = self.accs[k], self.recvs[k]
            most = 98304 // acc.shape[1]
            step = max(c for c in range(LOW_ROWS, most + 1, LOW_ROWS) if count % c == 0)

            def add(i, _):
                mine = low_rows_at(first + i * step, step)
                other = low_rows_at(base + i * step, step)
                acc[mine, :] = (acc[mine, :].astype(F32) + recv[other, :].astype(F32)).astype(BF16)
                return 0

            lax.fori_loop(0, count // step, add, 0)

    def tick(self, stage):
        self.finish(stage)
        if stage + 1 < self.stages:
            self.start(stage + 1)

    def keep(self, refs):
        at = [0] * len(refs)
        for j, (k, _, _, n) in enumerate(self.plans):
            refs[k][at[k] : at[k] + n, :] = self.accs[k][low_rows_at(self.walks[j][0][-1], n), :]
            at[k] += n


def strided(ref, start, count, stride):
    return jnp.concatenate([ref[t, pl.ds(start, count, stride=stride), :] for t in range(ref.shape[0])], 1)


def put_rows(ref, start, value):
    n = value.shape[0]
    for t in range(ref.shape[0]):
        ref[t, pl.ds(pl.multiple_of(start, 8), n), :] = value[:, t * LANES : (t + 1) * LANES]


def load_mode(wide_ref, m, slab, modes):
    re = strided(wide_ref, 2 * m, LAT_PAD, slab)
    im = strided(wide_ref, 2 * m + 1, LAT_PAD, slab)
    live = lax.axis_index("lat") * modes + m < KEPT
    value = jnp.concatenate([re, im], 0)
    return jnp.where(live, value, jnp.zeros_like(value)).astype(BF16)


def widen(recv_ref, wide_ref):
    shards, rows, slab, width = recv_ref.shape
    n = rows * slab

    def one(s, _):
        put_rows(wide_ref, s * n, recv_ref[s].astype(F32).reshape(n, width))
        return 0

    lax.fori_loop(0, shards, one, 0)
    if LAT % rows:
        first = LAT * slab
        last = (LAT // rows + 1) * n
        put_rows(wide_ref, first, jnp.zeros((last - first, width), F32))
    for s in range(-(-LAT // rows), shards):
        put_rows(wide_ref, s * n, jnp.zeros((n, width), F32))


def store_mode(out_s, m, value):
    put_rows(out_s, 2 * m * LAT_PAD, value)


def emit_slabs(out_s, out_ref):
    shards, rows, slab, _ = out_ref.shape

    def one(s, _):
        for r in range(rows):
            out_ref[s, r] = strided(out_s, s * rows + r, slab, LAT_PAD).astype(BF16)
        return 0

    lax.fori_loop(0, shards, one, 0)


def each_mode(modes, fn, between=None):
    few = next(n for n in (3, 2, 1) if modes % n == 0)

    def some(j, _):
        if between is not None:
            between(j * few)
        for u in range(few):
            fn(j * few + u)
        return 0

    lax.fori_loop(0, modes // few, some, 0)


def spread_blocks(w_ref, dense_s):
    _, blocks, n, _ = w_ref.shape
    dense_s[...] = jnp.zeros_like(dense_s)
    for p in range(2):
        for b in range(blocks):
            at = (p * blocks + b) * n
            dense_s[b * n : (b + 1) * n, at : at + n] = w_ref[p, b]


def pick_blocks(dense_ref, out_ref):
    _, blocks, n, lanes = out_ref.shape
    for p in range(2):
        for b in range(blocks):
            at = (p * blocks + b) * n
            block = dense_ref[b * n : (b + 1) * n, at : at + n]
            out_ref[p, b] = jnp.concatenate([block, jnp.zeros((n, lanes - n), F32)], 1)


def spectral_forward_kernel(
    recv_ref, fa_ref, ia_ref, wi_ref, wo_ref, v_ref,
    out_ref, freq_ref, hid_ref, gp_ref, t2_ref, wide_s, out_s, wi_s, wo_s,
):
    slab, width = recv_ref.shape[2:]
    modes = freq_ref.shape[0]
    h = LAT_PAD
    widen(recv_ref, wide_s)
    spread_blocks(wi_ref, wi_s)
    spread_blocks(wo_ref, wo_s)
    if slab != 2 * modes:
        out_s[...] = jnp.zeros_like(out_s)

    def mix(v, w_ref, bias):
        a = dot(v, w_ref[...])
        re = a[:h, :width] - a[h:, width:] + vector(v_ref, bias)
        im = a[h:, :width] + a[:h, width:] + vector(v_ref, bias + 1)
        return jnp.concatenate([re, im], 0)

    def one(m):
        fq = dot(fa_ref[...], load_mode(wide_s, m, slab, modes)).astype(BF16)
        freq_ref[m] = fq
        hid, gp = gelu_both(mix(fq, wi_s, INNER_B))
        hid = hid.astype(BF16)
        hid_ref[m] = hid
        gp_ref[m] = gp
        outer = mix(hid, wo_s, OUTER_B)
        t = jnp.tanh(outer * (1.0 / SHRINK))
        t2_ref[m] = t * t
        shrunk = (outer - SHRINK * t).astype(BF16)
        store_mode(out_s, m, dot(ia_ref[...], shrunk))

    each_mode(modes, one)
    emit_slabs(out_s, out_ref)


def group_specs(shards, rows, slab, modes, part):
    n = 2 * LAT_PAD
    slabs = pl.BlockSpec((shards, rows, slab, part), lambda g: (0, 0, 0, g))
    spec = pl.BlockSpec((modes, n, part), lambda g: (0, 0, g))
    pair = pl.BlockSpec((2, part), lambda g: (0, g))
    return slabs, spec, pair


def weight_spec(weight, lanes=None):
    _, blocks, n, _ = weight.shape
    return pl.BlockSpec((2, blocks // GROUPS, n, lanes or n), lambda g: (0, g, 0, 0))


def spectral_forward(recv, tb, wi, wo, vectors, modes):
    shards, rows, slab, width = recv.shape
    part = width // GROUPS
    n = 2 * LAT_PAD
    slabs, spec, _ = group_specs(shards, rows, slab, modes, part)
    lines = pl.BlockSpec((vectors.shape[0], part), lambda g: (0, g))
    return pl.pallas_call(
        spectral_forward_kernel,
        grid=(GROUPS,),
        in_specs=[slabs, full(tb["fa"]), full(tb["ia"]), weight_spec(wi), weight_spec(wo), lines],
        out_specs=[slabs, spec, spec, spec, spec],
        out_shape=[
            sds(recv.shape, BF16),
            sds((modes, n, width), BF16),
            sds((modes, n, width), BF16),
            sds((modes, n, width), F32),
            sds((modes, n, width), F32),
        ],
        scratch_shapes=[
            pltpu.VMEM((part // LANES, shards * rows * slab, LANES), F32),
            pltpu.VMEM((part // LANES, slab * LAT_PAD, LANES), F32),
            pltpu.VMEM((part, 2 * part), BF16),
            pltpu.VMEM((part, 2 * part), BF16),
        ],
        compiler_params=params(),
        name="spectral_forward",
    )(recv, tb["fa"], tb["ia"], wi, wo, vectors)


def spectral_backward_kernel(
    groups, plans, recv_ref, iat_ref, fat_ref, wo_ref, wi_ref, freq_ref, hid_ref, gp_ref, t2_ref, dw1_ref, dw2_ref,
    out_ref, dwo_ref, dbo_ref, dwi_ref, dbi_ref, part1_ref, part2_ref,
    wide_s, out_s, wo_s, wi_s, dwo_s, dwi_s, acc1_s, acc2_s, recv1_s, recv2_s, load_sem, send_sems, recv_sems,
):
    shards = recv_ref.shape[0]
    slab, width = recv_ref.shape[2:]
    modes = freq_ref.shape[0]
    h = LAT_PAD
    g = pl.program_id(0)
    me = lax.axis_index("lat")
    dp = lax.axis_index("dp")
    halving = Halving(plans, (acc1_s, acc2_s), (recv1_s, recv2_s), send_sems, recv_sems, dp, me)
    loads = [
        pltpu.make_async_copy(dw1_ref, acc1_s, load_sem.at[0]),
        pltpu.make_async_copy(dw2_ref, acc2_s, load_sem.at[1]),
    ]

    @pl.when(g == 0)
    def _():
        for copy in loads:
            copy.start()
        signal_all(sorted_peers(groups, shards, dp, me))
        for copy in loads:
            copy.wait()
        halving.start(0)

    whole = GROUPS * modes
    early = [whole * n // 8 // 3 * 3 for n in (1, 4, 6, 7)]

    widen(recv_ref, wide_s)
    spread_blocks(wo_ref, wo_s)
    spread_blocks(wi_ref, wi_s)
    if slab != 2 * modes:
        out_s[...] = jnp.zeros_like(out_s)
    for ref in (dwo_s, dbo_ref, dwi_s, dbi_ref):
        ref[...] = jnp.zeros_like(ref)

    def grads(value, grad, dw_ref, db_ref):
        re, im = grad[:h], grad[h:]
        low_re, low_im = re.astype(BF16), im.astype(BF16)
        low = jnp.concatenate([low_re, low_im], 0)
        turned = jnp.concatenate([low_im, -low_re], 0)
        dw_ref[...] += dot_tn(value, jnp.concatenate([low, turned], 1))
        db_ref[0:1] += jnp.sum(low_re.astype(F32), 0, keepdims=True)
        db_ref[1:2] += jnp.sum(low_im.astype(F32), 0, keepdims=True)
        return low

    def pull(v, w_ref):
        a = dot_nt(v, w_ref[:, :width])
        b = dot_nt(v, w_ref[:, width:])
        return jnp.concatenate([a[:h] + b[h:], a[h:] - b[:h]], 0)

    def between(m):
        for stage, when in enumerate(early):
            pl.when(g * modes + m == when)(functools.partial(halving.tick, stage))

    def one(m):
        merged = dot(iat_ref[...], load_mode(wide_s, m, slab, modes))
        og = grads(hid_ref[m], merged * t2_ref[m], dwo_s, dbo_ref)
        ig = grads(freq_ref[m], pull(og, wo_s) * gp_ref[m], dwi_s, dbi_ref)
        fg = pull(ig, wi_s).astype(BF16)
        store_mode(out_s, m, dot(fat_ref[...], fg))

    each_mode(modes, one, between)
    pick_blocks(dwo_s, dwo_ref)
    pick_blocks(dwi_s, dwi_ref)
    emit_slabs(out_s, out_ref)

    @pl.when(g == GROUPS - 1)
    def _():
        for stage in range(len(early), halving.stages):
            halving.tick(stage)
        halving.keep((part1_ref, part2_ref))


def spectral_backward(recv, tb, wo, wi, freq, hid, gp, t2, dw1, dw2, groups, plans, collective_id):
    shards, rows, slab, width = recv.shape
    modes = freq.shape[0]
    part = width // GROUPS
    slabs, spec, pair = group_specs(shards, rows, slab, modes, part)
    dw = sds(wo.shape[:3] + (LANES,), F32)
    grad = weight_spec(wo, LANES)
    db = sds((2, width), F32)
    any_ = pl.BlockSpec(memory_space=pl.ANY)
    whole = lambda n, w: pl.BlockSpec((n, w), lambda g: (0, 0))
    n1, n2 = (sum(n for k, _, _, n in plans if k == which) for which in range(2))
    stages = len(plans[0][2])
    dma = pltpu.SemaphoreType.DMA
    return pl.pallas_call(
        functools.partial(spectral_backward_kernel, groups, plans),
        grid=(GROUPS,),
        in_specs=[slabs, full(tb["iat"]), full(tb["fat"]), weight_spec(wo), weight_spec(wi), spec, spec, spec, spec]
        + [any_, any_],
        out_specs=[slabs, grad, pair, grad, pair, whole(n1, dw1.shape[1]), whole(n2, dw2.shape[1])],
        out_shape=[
            sds(recv.shape, BF16), dw, db, dw, db,
            sds((n1, dw1.shape[1]), BF16), sds((n2, dw2.shape[1]), BF16),
        ],
        scratch_shapes=[
            pltpu.VMEM((part // LANES, shards * rows * slab, LANES), F32),
            pltpu.VMEM((part // LANES, slab * LAT_PAD, LANES), F32),
            pltpu.VMEM((part, 2 * part), BF16),
            pltpu.VMEM((part, 2 * part), BF16),
            pltpu.VMEM((part, 2 * part), F32),
            pltpu.VMEM((part, 2 * part), F32),
            pltpu.VMEM(dw1.shape, BF16),
            pltpu.VMEM(dw2.shape, BF16),
            pltpu.VMEM((sum(received(p) for k, _, p, _ in plans if k == 0), dw1.shape[1]), BF16),
            pltpu.VMEM((sum(received(p) for k, _, p, _ in plans if k == 1), dw2.shape[1]), BF16),
            dma((2,)), dma((len(plans), stages)), dma((len(plans), stages)),
        ],
        compiler_params=params(collective_id=collective_id, has_side_effects=True),
        name="spectral_backward",
    )(recv, tb["iat"], tb["fat"], wo, wi, freq, hid, gp, t2, dw1, dw2)


def gather_row(r_ref, row, modes):
    shards, _, slab, width = r_ref.shape
    whole = KEPT // modes
    parts = [r_ref[:whole, row].astype(F32).reshape(whole * slab, width)]
    rest = (shards - whole) * slab
    if KEPT % modes:
        n = up8(2 * (KEPT % modes))
        parts.append(r_ref[whole, row].astype(F32)[:n])
        rest -= n
    if rest:
        parts.append(jnp.zeros((rest, width), F32))
    return jnp.concatenate(parts, 0).astype(BF16)


def feed_kernel(
    per, chunk, hops, modes, scale_ref, x_ref, c_ref, back_ref, il_ref, ilt_ref, w1_ref, w2_ref, v_ref,
    lo_ref, mg_ref, out_ref, dw1_ref, dw2_ref, deb_ref, drb_ref, dpg_ref, dps_ref,
    slab_s, w1_s, w2_s, act_s, pre_s, sec_s, sect_s, up_s, mixed_s, xhat_s, rs_s, branch_s, grad_s,
    w_sem, dw_sem, in_send, in_recv, in_own, out_send, out_recv, out_own,
):
    g = pl.program_id(0)
    steps = pl.num_programs(0)
    lon, width = x_ref.shape[1:]
    hidden = w1_s.shape[1]
    shards, rows, slab, _ = slab_s.shape
    hop = rows // hops
    every = steps // hops
    tall = per * COLS
    me = lax.axis_index("lat")
    dp = lax.axis_index("dp")

    def transfer(src, dst, sems, h, i, sender, receiver, row_owner, mode_owner, act):
        part = pl.ds(h * hop, hop)

        def piece(nr, ns):
            act(send(
                src.at[receiver, part, pl.ds(0, ns)], dst.at[sender, part, pl.ds(0, ns)],
                sems[0].at[h, i], sems[1].at[h, i], dp, receiver,
            ))

        live = row_owner * rows + h * hop < LAT
        each_size([(live, hop)], slab_sizes(mode_owner, modes, slab), piece)

    def incoming(h, i, sender, receiver, act):
        transfer(back_ref, slab_s, (in_send, in_recv), h, i, sender, receiver, receiver, sender, act)

    def outgoing(h, i, sender, receiver, act):
        transfer(slab_s, out_ref, (out_send, out_recv), h, i, sender, receiver, sender, receiver, act)

    def own_in(h):
        part = pl.ds(h * hop, hop)
        return pltpu.make_async_copy(back_ref.at[me, part], slab_s.at[me, part], in_own.at[h])

    def own_out(h):
        part = pl.ds(h * hop, hop)
        return pltpu.make_async_copy(slab_s.at[me, part], out_ref.at[me, part], out_own.at[h])

    def to(i):
        return lax.rem(me + i, shards)

    def source(i):
        return lax.rem(me + shards - i, shards)

    def peers(fn):
        def one(i, _):
            fn(i)
            return 0

        lax.fori_loop(1, shards, one, 0)

    def fetch(h):
        own_in(h).start()
        peers(lambda i: incoming(h, i, me, to(i), lambda c: c.start()))

    weights = [
        pltpu.make_async_copy(w1_ref, w1_s, w_sem.at[0]),
        pltpu.make_async_copy(w2_ref, w2_s, w_sem.at[1]),
    ]

    @pl.when(g == 0)
    def _():
        for copy in weights:
            copy.start()
        greet(shards, me, dp)
        fetch(0)
        for ref in (deb_ref, drb_ref, dpg_ref, dps_ref):
            ref[...] = jnp.zeros_like(ref)

    @pl.when(lax.rem(g, every) == 0)
    def _():
        h = g // every
        own_in(h).wait()
        peers(lambda i: incoming(h, i, source(i), me, lambda c: c.wait_recv()))

        @pl.when(h + 1 < hops)
        def _():
            fetch(h + 1)

    at = pl.ds(0 if rows == per else pl.multiple_of(g * tall, tall), tall)
    for i in range(per):
        rows_i = pl.ds(i * COLS, COLS)
        x = pad_rows(x_ref[i].astype(F32), COLS)
        c, rs = center_scale(x)
        first = c * rs * vector(v_ref, NORM_G) + vector(v_ref, NORM_S)
        filtered = dot(il_ref[...], gather_row(slab_s, g * per + i, modes))
        live = me * rows + g * per + i < LAT
        mixed = jnp.where(live, filtered, jnp.zeros_like(filtered)) + first + x
        c, rs = center_scale(mixed)
        xhat = c * rs
        mixed_s[rows_i, :] = mixed
        xhat_s[rows_i, :] = xhat
        rs_s[rows_i, :] = jnp.broadcast_to(rs, (COLS, LANES))
        sec_s[rows_i, :] = (xhat * vector(v_ref, POST_G) + vector(v_ref, POST_S)).astype(BF16)
        up = (pad_rows(c_ref[i].astype(F32), COLS) * scale_ref[0, g * per + i]).astype(BF16)
        up_s[pl.ds(pl.multiple_of(g * tall + i * COLS, COLS), COLS), :] = up
        drb_ref[...] += jnp.sum(up.astype(F32), 0, keepdims=True)
    sect_s[:, at] = sec_s[...].T
    branch_s[...] = jnp.broadcast_to(vector(v_ref, REDUCE_B), branch_s.shape)
    grad_s[...] = jnp.zeros_like(grad_s)

    @pl.when(g == 0)
    def _():
        for copy in weights:
            copy.wait()

    def hidden_chunk(j, _):
        ds = pl.ds(pl.multiple_of(j * chunk, chunk), chunk)
        act, slope = gelu_both(dot(sec_s[...], w1_s[:, ds]) + v_ref[pl.ds(EXPAND_B + j, 1), :])
        act = act.astype(BF16)
        act_s[at, ds] = act
        pre = (dot_nt(up_s[at, :], w2_s[ds, :]) * slope).astype(BF16)
        pre_s[at, ds] = pre
        deb_ref[pl.ds(j, 1), :] += jnp.sum(pre.astype(F32), 0, keepdims=True)
        branch_s[...] += dot(act, w2_s[ds, :])
        grad_s[...] += dot_nt(pre, w1_s[:, ds])
        return 0

    lax.fori_loop(0, hidden // chunk, hidden_chunk, 0)
    for i in range(per):
        rows_i = pl.ds(i * COLS, COLS)
        grad = grad_s[rows_i, :]
        xhat = xhat_s[rows_i, :]
        up = pad_rows(c_ref[i].astype(F32), COLS) * scale_ref[0, g * per + i]
        mg = up + norm_back(grad, xhat, rs_s[rows_i, 0:1], vector(v_ref, POST_G))
        mg_ref[i] = mg[:lon]
        rg = dot(ilt_ref[...], mg.astype(BF16)).astype(BF16)
        slab_s[:, g * per + i] = rg.reshape(shards, slab, width)

    @pl.when(lax.rem(g, every) == every - 1)
    def _():
        h = g // every
        own_out(h).start()
        peers(lambda i: outgoing(h, i, me, to(i), lambda c: c.start()))

    for i in range(per):
        rows_i = pl.ds(i * COLS, COLS)
        keep = scale_ref[1, g * per + i]
        lo_ref[i] = ((mixed_s[rows_i, :] + branch_s[rows_i, :]) * keep).astype(BF16)[:lon]
        grad = grad_s[rows_i, :]
        dpg_ref[...] += jnp.sum(grad * xhat_s[rows_i, :], 0, keepdims=True)
        dps_ref[...] += jnp.sum(grad, 0, keepdims=True)

    def gradients(j):
        ds = pl.ds(pl.multiple_of(j * chunk, chunk), chunk)
        side = dw1_ref.shape[1] // chunk
        place = (
            pl.ds(pl.multiple_of(j // side * width, width), width),
            pl.ds(pl.multiple_of(lax.rem(j, side) * chunk, chunk), chunk),
        )
        return (
            pltpu.make_async_copy(w1_s.at[:, ds], dw1_ref.at[place], dw_sem.at[0, j]),
            pltpu.make_async_copy(w2_s.at[ds, :], dw2_ref.at[ds, :], dw_sem.at[1, j]),
        )

    @pl.when(g == steps - 1)
    def _():
        def weight_chunk(j, _):
            ds = pl.ds(pl.multiple_of(j * chunk, chunk), chunk)
            w1_s[:, ds] = dot(sect_s[...], pre_s[:, ds]).astype(BF16)
            w2_s[ds, :] = dot_tn(act_s[:, ds], up_s[...]).astype(BF16)
            for copy in gradients(j):
                copy.start()
            return 0

        lax.fori_loop(0, hidden // chunk, weight_chunk, 0)

        def one(h, _):
            own_out(h).wait()

            def wait_all(i):
                incoming(h, i, me, to(i), lambda c: c.wait_send())
                outgoing(h, i, me, to(i), lambda c: c.wait_send())
                outgoing(h, i, source(i), me, lambda c: c.wait_recv())

            peers(wait_all)
            return 0

        lax.fori_loop(0, hops, one, 0)

        def finish(j, _):
            for copy in gradients(j):
                copy.wait()
            return 0

        lax.fori_loop(0, hidden // chunk, finish, 0)


def feed(scale, x, cot, back, tb, w1, w2, vectors, modes, collective_id):
    rows, lon, width = x.shape
    hidden = w1.shape[1]
    shards, _, slab, _ = back.shape
    per = next(n for n in (2, 3, 1) if rows % n == 0)
    steps = rows // per
    hops = 2 if steps % 2 == 0 else 1
    chunk = width
    row = pl.BlockSpec((per, lon, width), lambda g: (g, 0, 0))
    any_ = pl.BlockSpec(memory_space=pl.ANY)
    vec = lambda n: pl.BlockSpec((n, width), lambda g: (0, 0))
    tall = per * COLS
    total = rows * COLS
    dma = pltpu.SemaphoreType.DMA
    return pl.pallas_call(
        functools.partial(feed_kernel, per, chunk, hops, modes),
        grid=(steps,),
        in_specs=[
            pl.BlockSpec(memory_space=pltpu.SMEM), row, row, any_, full(tb["il"]), full(tb["ilt"]), any_, any_,
            full(vectors),
        ],
        out_specs=[row, row, any_, any_, any_, vec(hidden // width), vec(1), vec(1), vec(1)],
        out_shape=[
            sds((rows, lon, width), BF16),
            sds((rows, lon, width), F32),
            sds(back.shape, BF16),
            sds((2 * width, hidden // 2), BF16),
            sds(w2.shape, BF16),
            sds((hidden // width, width), F32),
            sds((1, width), F32),
            sds((1, width), F32),
            sds((1, width), F32),
        ],
        scratch_shapes=[
            pltpu.VMEM(back.shape, BF16),
            pltpu.VMEM(w1.shape, BF16),
            pltpu.VMEM(w2.shape, BF16),
            pltpu.VMEM((total, hidden), BF16),
            pltpu.VMEM((total, hidden), BF16),
            pltpu.VMEM((tall, width), BF16),
            pltpu.VMEM((width, total), BF16),
            pltpu.VMEM((total, width), BF16),
            pltpu.VMEM((tall, width), F32),
            pltpu.VMEM((tall, width), F32),
            pltpu.VMEM((tall, LANES), F32),
            pltpu.VMEM((tall, width), F32),
            pltpu.VMEM((tall, width), F32),
            dma((2,)), dma((2, hidden // chunk)),
            dma((hops, shards)), dma((hops, shards)), dma((hops,)),
            dma((hops, shards)), dma((hops, shards)), dma((hops,)),
        ],
        compiler_params=pltpu.CompilerParams(
            vmem_limit_bytes=63 * 2**20, collective_id=collective_id, has_side_effects=True
        ),
        name="feed",
    )(scale, x, cot, back, tb["il"], tb["ilt"], w1, w2, vectors)


def leave_kernel(
    groups, hops, modes, plans, x_ref, back_ref, mg_ref, fl_ref, v_ref, *refs,
):
    weight_refs, line_refs, refs = refs[:2], refs[2:8], refs[8:]
    (
        part1_ref, part2_ref, out_ref, sums_ref, norm_ref, dw1_ref, dw2_ref,
        slab_s, line_s, mine_s, from_dp, part_s, from_lat, all_s, norm_lat, norm_dp,
        in_send, in_recv, in_own, wide_send, wide_recv, own_sem, small_sems,
    ) = refs
    g = pl.program_id(0)
    steps = pl.num_programs(0)
    lon = x_ref.shape[1]
    shards, rows, slab, _ = slab_s.shape
    n = from_lat.shape[1]
    hop = rows // hops
    me = lax.axis_index("lat")
    dp = lax.axis_index("dp")
    lat_peers = [lax.rem(me + i, shards) for i in range(1, shards)]
    dp_peers = [lax.rem(dp + i, groups) for i in range(1, groups)]

    def incoming(h, i, sender, receiver, act):
        part = pl.ds(h * hop, hop)

        def piece(nr, ns):
            act(send(
                back_ref.at[receiver, part, pl.ds(0, ns)], slab_s.at[sender, part, pl.ds(0, ns)],
                in_send.at[h, i], in_recv.at[h, i], dp, receiver,
            ))

        live = receiver * rows + h * hop < LAT
        each_size([(live, hop)], slab_sizes(sender, modes, slab), piece)

    def own_in(h):
        part = pl.ds(h * hop, hop)
        return pltpu.make_async_copy(back_ref.at[me, part], slab_s.at[me, part], in_own.at[h])

    def peers(fn):
        def one(i, _):
            fn(i)
            return 0

        lax.fori_loop(1, shards, one, 0)

    def fetch(h):
        own_in(h).start()
        peers(lambda i: incoming(h, i, me, lax.rem(me + i, shards), lambda c: c.start()))

    def arrived(h):
        own_in(h).wait()
        peers(lambda i: incoming(h, i, lax.rem(me + shards - i, shards), me, lambda c: c.wait_recv()))

    walks = [halving_walk(first, plan, dp, me) for _, first, plan, _ in plans]
    outs = (dw1_ref, dw2_ref)
    parts = (part1_ref, part2_ref)
    stages = len(plans[0][2])
    count = len(plans)

    def part(j):
        k, _, _, n = plans[j]
        at = sum(rest for which, _, _, rest in plans[:j] if which == k)
        return parts[k].at[pl.ds(at, n)]

    def own_part(j):
        k, _, _, n = plans[j]
        return pltpu.make_async_copy(part(j), outs[k].at[low_rows_at(walks[j][0][-1], n)], own_sem.at[j])

    def spread(j, stage):
        k, _, plan, _ = plans[j]
        _, _, n, halved = plan[stage]
        if not halved:
            return None
        where = low_rows_at(walks[j][0][stage + 1], n // 2)
        first = not any(later[3] for later in plan[stage + 1 :])
        return pltpu.make_async_remote_copy(
            src_ref=part(j) if first else outs[k].at[where], dst_ref=outs[k].at[where],
            send_sem=wide_send.at[j, stage], recv_sem=wide_recv.at[j, stage],
            device_id=walks[j][2][stage], device_id_type=MESH,
        )

    def spread_all(stage, act):
        for j in range(count):
            copy = spread(j, stage)
            if copy is not None:
                act(copy)

    def tick(i):
        stage = stages - 1 - i
        spread_all(stage, lambda c: c.wait())
        if i == 0:
            for j in range(count):
                own_part(j).wait()
        if stage:
            spread_all(stage - 1, lambda c: c.start())


    def remote(src, dst, stage, i, to):
        return pltpu.make_async_remote_copy(
            src_ref=src, dst_ref=dst, send_sem=small_sems.at[stage, 0, i], recv_sem=small_sems.at[stage, 1, i],
            device_id=to, device_id_type=MESH,
        )

    def over(peers_, axis):
        return [(i, p, (p, me) if axis == "dp" else (dp, p)) for i, p in enumerate(peers_)]

    block = shards * n
    mine = rows_at((dp * shards + me) * n, n)
    mine_dp = rows_at(dp * block, block)
    tiles = line_s.shape[1] // LANES

    def small(stage):
        if stage == 0:
            return [
                remote(mine_s.at[rows_at(p * block, block)], from_dp.at[i], 0, i, to)
                for i, p, to in over(dp_peers, "dp")
            ]
        if stage == 1:
            return [
                remote(part_s.at[rows_at(p * n, n)], from_lat.at[i], 1, i, to)
                for i, p, to in over(lat_peers, "lat")
            ]
        if stage == 2:
            return [remote(all_s.at[mine], all_s.at[mine], 2, i, to) for i, p, to in over(lat_peers, "lat")]
        if stage == 3:
            return [remote(all_s.at[mine_dp], all_s.at[mine_dp], 3, i, to) for i, p, to in over(dp_peers, "dp")]
        if stage == 4:
            return [remote(norm_lat.at[me], norm_lat.at[me], 4, i, to) for i, p, to in over(lat_peers, "lat")]
        return [remote(norm_dp.at[dp], norm_dp.at[dp], 5, i, to) for i, p, to in over(dp_peers, "dp")]

    def begin(stage):
        for copy in small(stage):
            copy.start()

    def end(stage):
        for copy in small(stage):
            copy.wait()
        if stage == 0:
            part_s[...] = mine_s[mine_dp, :] + jnp.sum(from_dp[...], 0)
        if stage == 1:
            all_s[mine, :] = part_s[rows_at(me * n, n), :] + jnp.sum(from_lat[...], 0)

    def small_tick(stage):
        end(stage)
        begin(stage + 1)

    @pl.when(g == 0)
    def _():
        at = 0
        for ref in weight_refs:
            value = ref[...].reshape(-1, LANES)
            mine_s[at : at + value.shape[0], :] = value
            at += value.shape[0]
        mine_s[at:, :] = jnp.zeros((mine_s.shape[0] - at, LANES), F32)
        for ref in line_refs:
            for row in range(ref.shape[0]):
                for t in range(tiles):
                    mine_s[at : at + 1, :] = ref[row : row + 1, t * LANES : (t + 1) * LANES]
                    at += 1
        signal_all([(dp, p) for p in lat_peers] + [(p, me) for p in dp_peers])
        for j in range(count):
            own_part(j).start()
        spread_all(stages - 1, lambda c: c.start())
        begin(0)
        fetch(0)
        line_s[...] = jnp.zeros_like(line_s)
        tick(0)
        small_tick(0)
        arrived(0)
        tick(1)
        small_tick(1)
        if hops > 1:
            fetch(1)

    for h in range(1, hops):
        pl.when(g == h * hop)(functools.partial(arrived, h))

    x = pad_rows(x_ref[0].astype(F32), COLS)
    c, rs = center_scale(x)
    xhat = c * rs
    mg = pad_rows(mg_ref[0], COLS)
    live = me * rows + g < LAT
    spectrum = dot(fl_ref[...], gather_row(slab_s, g, modes))
    grad = jnp.where(live, spectrum, jnp.zeros_like(spectrum)) + mg
    line_s[0:1] += jnp.sum(grad * xhat, 0, keepdims=True)
    line_s[1:2] += jnp.sum(grad, 0, keepdims=True)
    out_ref[0] = (mg + norm_back(grad, xhat, rs, vector(v_ref, NORM_G)))[:lon]

    @pl.when(g == hop - 1)
    def _():
        tick(2)
        small_tick(2)

    @pl.when(g == steps - 1)
    def _():
        norm_lat[me] = line_s[...]
        begin(4)
        for i in range(3, stages):
            tick(i)
        end(4)
        norm_dp[dp] = jnp.sum(norm_lat[...], 0)
        begin(5)
        end(3)
        sums_ref[...] = all_s[...]
        for h in range(hops):
            peers(lambda i: incoming(h, i, me, lax.rem(me + i, shards), lambda c: c.wait_send()))
        end(5)
        norm_ref[...] = jnp.sum(norm_dp[...], 0)


def leave(x, back, mg, fl, vectors, small, part1, part2, shapes, groups, plans, modes, collective_id):
    rows, lon, width = x.shape
    shards, _, slab, _ = back.shape
    hops = 2 if rows % 2 == 0 else 1
    stages = len(plans[0][2])
    unit = 8 * groups * shards
    total = -(-sum(v.size // LANES for v in small) // unit) * unit
    n = total // (groups * shards)
    row = pl.BlockSpec((1, lon, width), lambda r: (r, 0, 0))
    any_ = pl.BlockSpec(memory_space=pl.ANY)
    whole = lambda *shape: pl.BlockSpec(shape, lambda r: (0,) * len(shape))
    dma = pltpu.SemaphoreType.DMA
    return pl.pallas_call(
        functools.partial(leave_kernel, groups, hops, modes, plans),
        grid=(rows,),
        in_specs=[row, any_, row, full(fl), full(vectors)] + [full(v) for v in small] + [any_, any_],
        out_specs=[row, whole(total, LANES), whole(2, width), any_, any_],
        out_shape=[sds((rows, lon, width), F32), sds((total, LANES), F32), sds((2, width), F32)]
        + [sds(shape, BF16) for shape in shapes],
        scratch_shapes=[
            pltpu.VMEM(back.shape, BF16),
            pltpu.VMEM((2, width), F32),
            pltpu.VMEM((total, LANES), F32),
            pltpu.VMEM((groups - 1, shards * n, LANES), F32),
            pltpu.VMEM((shards * n, LANES), F32),
            pltpu.VMEM((shards - 1, n, LANES), F32),
            pltpu.VMEM((total, LANES), F32),
            pltpu.VMEM((shards, 2, width), F32),
            pltpu.VMEM((groups, 2, width), F32),
            dma((hops, shards)), dma((hops, shards)), dma((hops,)),
            dma((len(plans), stages)), dma((len(plans), stages)), dma((len(plans),)),
            dma((6, 2, max(groups, shards) - 1)),
        ],
        compiler_params=params(collective_id=collective_id, has_side_effects=True),
        name="leave",
    )(x, back, mg, fl, vectors, *small, part1, part2)


def shards_fn(
    groups, shards, inputs, cotangent, storm_weight, norm_gain, norm_shift, inner_weight, inner_bias,
    outer_weight, outer_bias, post_gain, post_shift, expand_weight, expand_bias, reduce_weight, reduce_bias,
):
    _, rows, lon, width = inputs.shape
    modes = LON_PAD // shards
    slab = slab_rows(modes)
    tb = make_tables(shards, modes)
    row_ids = lax.axis_index("lat") * rows + jnp.arange(rows, dtype=jnp.int32)
    keep = (row_ids < LAT).astype(F32)
    scale = jnp.stack([keep * (storm_weight[0].astype(F32) / 64.0), keep])
    x = inputs[0]
    cot = cotangent[0]
    vectors = jnp.concatenate([
        norm_gain, norm_shift, post_gain, post_shift, reduce_bias,
        inner_bias.reshape(-1), outer_bias.reshape(-1), expand_bias,
    ]).reshape(-1, width)

    spec = exchange(enter(x, tb["flt"], vectors, shards, slab), True, modes, 0)
    back, freq, hid, gp, t2 = spectral_forward(spec, tb, inner_weight, outer_weight, vectors, modes)
    (layer_out, mixed_grad, mode_grad, dw1, dw2, deb, drb, dpg, dps) = feed(
        scale, x, cot, back, tb, expand_weight, reduce_weight, vectors, modes, 1
    )
    plans = halving_plans(groups, shards, (dw1.shape[0], dw2.shape[0]))
    slab_grad, dwo, dbo, dwi, dbi, part1, part2 = spectral_backward(
        mode_grad, tb, outer_weight, inner_weight, freq, hid, gp, t2, dw1, dw2, groups, plans, 2
    )
    small = (dwi, dwo, dbi, dbo, dpg, dps, deb, drb)
    input_grad, sums, norm, dw1, dw2 = leave(
        x, slab_grad, mixed_grad, tb["fl"], vectors, small, part1, part2,
        (dw1.shape, dw2.shape), groups, plans, modes, 3
    )
    dw1 = jnp.concatenate([dw1[:width], dw1[width:]], 1).astype(F32)
    dw2 = dw2.astype(F32)
    ends = np.cumsum([v.size // LANES for v in small])
    dwi, dwo, dbi, dbo, dpg, dps, deb, drb = [
        sums[e - v.size // LANES : e] for v, e in zip(small, ends)
    ]
    block = inner_weight.shape[-1]
    weight = lambda v: v.reshape(inner_weight.shape[:3] + (LANES,))[..., :block]
    line = lambda v: v.reshape(-1)
    return (
        layer_out[None], input_grad[None], norm[0], norm[1],
        weight(dwi), dbi.reshape(inner_bias.shape), weight(dwo), dbo.reshape(outer_bias.shape),
        line(dpg), line(dps), dw1, line(deb), dw2, line(drb),
    )


def solution(mesh):
    split = P("dp", "lat", None, None)
    return jax.shard_map(
        functools.partial(shards_fn, mesh.shape["dp"], mesh.shape["lat"]),
        mesh=mesh,
        in_specs=(split, split, P("dp")) + (P(),) * 12,
        out_specs=(split, split) + (P(),) * 12,
        check_vma=False,
    )
```

time: 758 us -> 538 us (0.71)
  waiting for transfers between devices: 152 us -> 0 us
  Pallas kernels: 424 us -> 501 us
  blocking collectives: 68.8 us -> 0 us
  matrix products: 30.2 us -> 0 us
  local copies, waits for them, and re-layouts: 50.4 us -> 24.4 us
  between operations: 15 us -> 1.39 us
    psum x2 -> x0, waiting for transfers between devices: 152 us -> none  [the longest x1 127 us: shards_fn(): lax.psum((dng, dns, block_grads(dwi), dbi, block_grads(dwo), dbo, dpg, dp...]
    pallas_call x3, Pallas kernels: 248 us -> 395 us  [the longest x1 169 us: feed(): pl.pallas_call(functools.partial(feed_kernel, per, chunk, hops, modes), g...]
    psum x1 -> x0, blocking collectives: 68.8 us -> none  [shards_fn(): lax.psum((dng, dns, block_grads(dwi), dbi, block_grads(dwo), dbo, dpg, dp...]
    pallas_call x2 -> x1, Pallas kernels: 124 us -> 60.2 us  [exchange(): pl.pallas_call(functools.partial(exchange_kernel, from_rows, modes), in_s...]
    dot_general x2 -> x0, matrix products: 30.2 us -> none  [dot_tn(): lax.dot_general(a, b, (((0,), (0,)), ((), ())), preferred_element_type=F32)]
    reshape x15 -> x5, local copies, waits for them, and re-layouts: 27.6 us -> 3.37 us  [the longest x2 1.21 us: shards_fn(): line = lambda v: v.reshape(-1)]
  transfers between devices with their start and end apart: 2 -> 0, of which waited for: 2 -> 0; matrix products, arithmetic and copies ran while one was open for 5% -> 0% of each run, Pallas kernels for 17% -> 0%
where the time goes in v3:
time: 538 us; the launch traced here: 537 us
  Pallas kernels  501 us (93%)
  local copies, waits for them, and re-layouts  24.4 us (5%)
  other arithmetic  10.1 us (2%)
    pallas_call x1, Pallas kernels, feed(): pl.pallas_call(functools.partial(feed_kernel, per, chunk, hops, modes), g...  169 us
    pallas_call x1, Pallas kernels, leave(): pl.pallas_call(functools.partial(leave_kernel, groups, hops, modes, plans...  135 us
    pallas_call x1, Pallas kernels, spectral_backward(): pl.pallas_call(functools.partial(spectral_backward_kernel, groups, plans)...  91 us
    pallas_call x1, Pallas kernels, exchange(): pl.pallas_call(functools.partial(exchange_kernel, from_rows, modes), in_s...  60.2 us
    pallas_call x1, Pallas kernels, spectral_forward(): pl.pallas_call(spectral_forward_kernel, grid=(GROUPS,), in_specs=[slabs,...  35 us
    unnamed x19, local copies, waits for them, and re-layouts  14.3 us

profile of v3, /device:TPU:0, one launch (start us, length us, event | category | flops | bytes accessed | tf_op | source)
XLA Modules:
  0.0 536.6 jit_solution(13839240179628020907)
XLA Ops:
  1.9 0.8 reshape.81
  2.7 0.8 reshape.82
  3.4 0.7 constant_dynamic-update-slice_fusion.7
  4.1 0.7 constant_dynamic-update-slice_fusion.6
  4.8 0.7 constant_dynamic-update-slice_fusion.5
  5.5 0.7 constant_dynamic-update-slice_fusion.4
  6.2 0.7 constant_dynamic-update-slice_fusion.3
  6.9 0.7 constant_dynamic-update-slice_fusion
  7.6 0.6 reshape.83.v_ref
  8.3 10.6 %enter.1.src_ref = bf16[8,12,24,768]{3,2,1,0:T(8,128)(2,1)} custom-call(bf16[12,180,768]{2,1,0:T(8,128)(2,1)} %bitcast.17, bf16[192,192]{1,0:T(8,128)(2,1)} %constant.27.clone.flt_ref, f32[13,768]{1,0:T(8,128)} %reshape.83.v_ref), custom_call_target="tpu_custom_call" | custom-call | tf_op jit(solution)/shard_map/enter/pallas_call | solution.py:144
  18.8 60.2 %exchange.1.recv_ref = bf16[8,12,24,768]{3,2,1,0:T(8,128)(2,1)} custom-call(bf16[8,12,24,768]{3,2,1,0:T(8,128)(2,1)} %enter.1.src_ref), custom_call_target="tpu_custom_call" | custom-call | bytes 7077888 | tf_op jit(solution)/shard_map/exchange/pallas_call | solution.py:235
  79.0 35.0 %spectral_forward.1 = (bf16[8,12,24,768]{3,2,1,0:T(8,128)(2,1)}, bf16[12,192,768]{2,1,0:T(8,128)(2,1)}, bf16[12,192,768]{2,1,0:T(8,128)(2,1)}, f32[12,192,768]{2,1,0:T(8,128)}, f32[12,192,768]{2,1,0:T(8,128)}) custom-call(bf16[8,12,24,768]{3,2,1,0:T(8,128)(2,1)} %exchange.1.recv_ref, bf16[192,192]{1,0:T(8,128)(2,1)} %constant.30.clone.fa_ref.iat_ref, ...), custom_call_target="tpu_custom_call" | custom-call | tf_op jit(solution)/shard_map/spectral_forward/pallas_call | solution.py:511
  114.0 169.4 %feed.1 = (bf16[12,180,768]{2,1,0:T(8,128)(2,1)}, f32[12,180,768]{2,1,0:T(8,128)}, bf16[8,12,24,768]{3,2,1,0:T(8,128)(2,1)}, bf16[1536,1536]{1,0:T(8,128)(2,1)},...) custom-call(f32[2,12]{1,0:T(2,128)} %pad_maximum_fusion.scale_ref, ...), custom_call_target="tpu_custom_call" | custom-call | tf_op jit(solution)/shard_map/feed/pallas_call | solution.py:872
  283.4 91.0 %spectral_backward.1 = (bf16[8,12,24,768]{3,2,1,0:T(8,128)(2,1)}, f32[2,8,96,128]{3,2,1,0:T(8,128)}, f32[2,768]{1,0:T(2,128)}, f32[2,8,96,128]{3,2,1,0:T(8,128)}...) custom-call(bf16[8,12,24,768]{3,2,1,0:T(8,128)(2,1)} %get-tuple-element.42.recv_ref, ...), custom_call_target="tpu_custom_call" | custom-call | tf_op jit(solution)/shard_map/spectral_backward/pallas_call | solution.py:623
  374.5 134.6 %leave.1 = (f32[12,180,768]{2,1,0:T(8,128)}, f32[3328,128]{1,0:T(8,128)}, f32[2,768]{1,0:T(2,128)}, bf16[1536,1536]{1,0:T(8,128)(2,1)}, bf16[3072,768]{1,0:T(8,128)(2,1)}) custom-call(bf16[12,180,768]{2,1,0:T(8,128)(2,1)} %bitcast.19, bf16[8,12,24,768]{3,2,1,0:T(8,128)(2,1)} %get-tuple-element.49.back_ref, f32[12,180,768]{2,1,0:T(8,128)} %get-tuple-element.50.mg_ref, ...), custom_call_target="tpu_custom_call" | custom-call | tf_op jit(solution)/shard_map/leave/pallas_call | solution.py:1136
  509.1 9.0 %copy.37 = f32[1,12,180,768]{3,0,2,1:T(1,128)} copy(f32[1,12,180,768]{3,2,1,0:T(8,128)} %bitcast.20) | data formatting | bytes 13271040
  518.1 0.6 slice_reduce_fusion
  519.9 1.2 fusion.2
  521.1 0.7 reshape.87
  521.8 0.7 reshape.85
  522.5 2.8 fusion
  525.3 5.0 maximum_convert_fusion
  530.4 4.5 convert_element_type.23
  534.8 1.7 copy.48
  (20 shorter events, 1.8 us)
Async XLA Ops:
  509.0 9.0 %copy-start.2 = (f32[2,768]{1,0:T(2,128)S(1)}, f32[2,768]{1,0:T(2,128)}, u32[]{:S(2)}) copy-start(f32[2,768]{1,0:T(2,128)} %get-tuple-element.62) | copy-start | bytes 18436
  509.0 9.6 %copy-start.1 = (f32[3328,128]{1,0:T(8,128)S(1)}, f32[3328,128]{1,0:T(8,128)}, u32[]{:S(2)}) copy-start(f32[3328,128]{1,0:T(8,128)} %get-tuple-element.63) | copy-start | bytes 5111812
  522.5 7.9 %slice-start = ((s8[4718592]{0:T(1024)(128)(4,1)}), s8[4194304]{0:T(1024)(128)(4,1)S(1)}, s32[]{:S(2)}) async-start(s8[4718592]{0:T(1024)(128)(4,1)} %bitcast.21), calls=%async_computation | async-start | bytes 8388608
  525.3 5.0 slice-start.1
  530.4 4.5 copy-start

commit v4 on v3

--- a/solution.py
+++ b/solution.py
@@ -131,27 +131,6 @@
     return v_ref[row : row + 1, :]
 
 
-def enter_kernel(x_ref, flt_ref, v_ref, out_ref):
-    shards, _, slab, width = out_ref.shape
-    x = pad_rows(x_ref[0].astype(F32), COLS)
-    c, rs = center_scale(x)
-    first = (c * rs * vector(v_ref, NORM_G) + vector(v_ref, NORM_S)).astype(BF16)
-    out_ref[:, 0] = dot(flt_ref[...], first).astype(BF16).reshape(shards, slab, width)
-
-
-def enter(x, flt, vectors, shards, slab):
-    rows, lon, width = x.shape
-    return pl.pallas_call(
-        enter_kernel,
-        grid=(rows,),
-        in_specs=[pl.BlockSpec((1, lon, width), lambda r: (r, 0, 0)), full(flt), full(vectors)],
-        out_specs=pl.BlockSpec((shards, 1, slab, width), lambda r: (0, r, 0, 0)),
-        out_shape=sds((shards, rows, slab, width), BF16),
-        compiler_params=params(),
-        name="enter",
-    )(x, flt, vectors)
-
-
 def up8(n):
     return -(-n // 8) * 8
 
@@ -193,59 +172,6 @@
         src_ref=src, dst_ref=dst, send_sem=send_sem, recv_sem=recv_sem,
         device_id=(dp, peer), device_id_type=MESH,
     )
-
-
-def exchange_kernel(from_rows, modes, src_ref, out_ref, send_sem, recv_sem, own_sem):
-    shards, rows, slab, _ = src_ref.shape
-    me = lax.axis_index("lat")
-    dp = lax.axis_index("dp")
-    greet(shards, me, dp)
-    own = pltpu.make_async_copy(src_ref.at[me], out_ref.at[me], own_sem)
-    own.start()
-
-    def go(i, sender, receiver, act):
-        row_owner, mode_owner = (sender, receiver) if from_rows else (receiver, sender)
-
-        def piece(nr, ns):
-            part = (pl.ds(0, nr), pl.ds(0, ns))
-            copy = send(
-                src_ref.at[(receiver,) + part], out_ref.at[(sender,) + part],
-                send_sem.at[i], recv_sem.at[i], dp, receiver,
-            )
-            act(copy)
-
-        each_size(row_sizes(row_owner, rows), slab_sizes(mode_owner, modes, slab), piece)
-
-    def start(i, _):
-        go(i, me, lax.rem(me + i, shards), lambda copy: copy.start())
-        return 0
-
-    def finish(i, _):
-        go(i, me, lax.rem(me + i, shards), lambda copy: copy.wait_send())
-        go(i, lax.rem(me + shards - i, shards), me, lambda copy: copy.wait_recv())
-        return 0
-
-    lax.fori_loop(1, shards, start, 0)
-    own.wait()
-    lax.fori_loop(1, shards, finish, 0)
-
-
-def exchange(x, from_rows, modes, collective_id):
-    shards = x.shape[0]
-    return pl.pallas_call(
-        functools.partial(exchange_kernel, from_rows, modes),
-        in_specs=[pl.BlockSpec(memory_space=pl.ANY)],
-        out_specs=pl.BlockSpec(memory_space=pl.ANY),
-        out_shape=sds(x.shape, x.dtype),
-        scratch_shapes=[
-            pltpu.SemaphoreType.DMA((shards,)),
-            pltpu.SemaphoreType.DMA((shards,)),
-            pltpu.SemaphoreType.DMA,
-        ],
-        compiler_params=pltpu.CompilerParams(collective_id=collective_id, has_side_effects=True),
-        cost_estimate=pl.CostEstimate(flops=0, bytes_accessed=2 * x.size * 2, transcendentals=0),
-        name="exchange",
-    )(x)
 
 
 def halving_plan(groups, shards, n, turn):
@@ -282,14 +208,9 @@
     return offsets, bits, peers
 
 
-def sorted_peers(groups, shards, dp, me):
-    out = []
-    for axis, count in (("dp", groups), ("lat", shards)):
-        index = dp if axis == "dp" else me
-        for bit in range(count.bit_length() - 1):
-            other = index + 2**bit * (1 - 2 * lax.rem(index // 2**bit, 2))
-            out.append((other, me) if axis == "dp" else (dp, other))
-    return out
+def dp_halving_peers(groups, dp, me):
+    bits = range(groups.bit_length() - 1)
+    return [(dp + 2**bit * (1 - 2 * lax.rem(dp // 2**bit, 2)), me) for bit in bits]
 
 
 def rows_at(start, n, unit=8):
@@ -422,12 +343,10 @@
     lax.fori_loop(0, shards, one, 0)
 
 
-def each_mode(modes, fn, between=None):
+def each_mode(modes, fn):
     few = next(n for n in (3, 2, 1) if modes % n == 0)
 
     def some(j, _):
-        if between is not None:
-            between(j * few)
         for u in range(few):
             fn(j * few + u)
         return 0
@@ -453,18 +372,124 @@
             out_ref[p, b] = jnp.concatenate([block, jnp.zeros((n, lanes - n), F32)], 1)
 
 
+def peers(shards, fn):
+    def one(i, _):
+        fn(i)
+        return 0
+
+    lax.fori_loop(1, shards, one, 0)
+
+
+def emit_early(out_ref, early_s):
+    rows = early_s.shape[1]
+    for s in range(out_ref.shape[0]):
+        early_s[s] = out_ref[s, :rows]
+
+
+class Early:
+    def __init__(self, src, dst, sems, rows, modes, slab, dp, me):
+        self.src, self.dst, self.sems = src, dst, sems
+        self.rows, self.modes, self.slab = rows, modes, slab
+        self.dp, self.me, self.shards = dp, me, src.shape[0]
+
+    def move(self, i, sender, receiver, act):
+        count = self.src.shape[1]
+
+        def piece(nr, ns):
+            act(send(
+                self.src.at[receiver, pl.ds(0, nr), pl.ds(0, ns)], self.dst.at[sender, pl.ds(0, nr), pl.ds(0, ns)],
+                self.sems[0].at[i], self.sems[1].at[i], self.dp, receiver,
+            ))
+
+        live = row_sizes(receiver, count) if count == self.rows else [(receiver * self.rows < LAT, count)]
+        each_size(live, slab_sizes(sender, self.modes, self.slab), piece)
+
+    def own(self):
+        return pltpu.make_async_copy(self.src.at[self.me], self.dst.at[self.me], self.sems[0].at[0])
+
+    def start(self):
+        self.own().start()
+        peers(self.shards, lambda i: self.move(i, self.me, lax.rem(self.me + i, self.shards), lambda c: c.start()))
+
+    def finish(self):
+        self.own().wait()
+
+        def one(i):
+            self.move(i, self.me, lax.rem(self.me + i, self.shards), lambda c: c.wait_send())
+            self.move(i, lax.rem(self.me + self.shards - i, self.shards), self.me, lambda c: c.wait_recv())
+
+        peers(self.shards, one)
+
+
 def spectral_forward_kernel(
-    recv_ref, fa_ref, ia_ref, wi_ref, wo_ref, v_ref,
-    out_ref, freq_ref, hid_ref, gp_ref, t2_ref, wide_s, out_s, wi_s, wo_s,
+    hops, x_ref, flt_ref, fa_ref, ia_ref, wi_ref, wo_ref, all_ref, v_ref,
+    out_ref, freq_ref, hid_ref, gp_ref, t2_ref, early_ref,
+    stage_s, recv_s, early_s, wide_s, out_s, wi_s, wo_s, go_send, go_recv, go_own, early_send, early_recv,
 ):
-    slab, width = recv_ref.shape[2:]
+    g = pl.program_id(0)
+    rows, lon, _ = x_ref.shape
+    shards, _, slab, width = out_ref.shape
     modes = freq_ref.shape[0]
     h = LAT_PAD
-    widen(recv_ref, wide_s)
+    me = lax.axis_index("lat")
+    dp = lax.axis_index("dp")
+    early = Early(early_s, early_ref, (early_send, early_recv), rows, modes, slab, dp, me)
+
+    hop = rows // hops
+
+    def go(group, h, i, sender, receiver, act):
+        def piece(nr, ns):
+            part = (pl.ds(h * hop, nr), pl.ds(0, ns))
+            act(send(
+                stage_s.at[(group, receiver) + part], recv_s.at[(group, sender) + part],
+                go_send.at[group, h, i], go_recv.at[group, h, i], dp, receiver,
+            ))
+
+        each_size([(sender * rows + h * hop < LAT, hop)], slab_sizes(receiver, modes, slab), piece)
+
+    def own(group):
+        return pltpu.make_async_copy(stage_s.at[group, me], recv_s.at[group, me], go_own.at[group])
+
+    def to(i):
+        return lax.rem(me + i, shards)
+
+    def send_group(group, h):
+        peers(shards, lambda i: go(group, h, i, me, to(i), lambda c: c.start()))
+
+    @pl.when(g == 0)
+    def _():
+        def row(r, _):
+            c, rs = center_scale(pad_rows(x_ref[r].astype(F32), COLS))
+            first = (c * rs * vector(all_ref, NORM_G) + vector(all_ref, NORM_S)).astype(BF16)
+            spec = dot(flt_ref[...], first).astype(BF16)
+            for group in range(GROUPS):
+                part = spec[:, group * width : (group + 1) * width]
+                stage_s[group, :, r] = part.reshape(shards, slab, width)
+            return 0
+
+        for h in range(hops):
+            lax.fori_loop(h * hop, (h + 1) * hop, row, 0)
+            if h == 0:
+                greet(shards, me, dp)
+            send_group(0, h)
+        for group in range(GROUPS):
+            own(group).start()
+            if group:
+                for h in range(hops):
+                    send_group(group, h)
+
     spread_blocks(wi_ref, wi_s)
     spread_blocks(wo_ref, wo_s)
     if slab != 2 * modes:
         out_s[...] = jnp.zeros_like(out_s)
+    for group in range(GROUPS):
+
+        @pl.when(g == group)
+        def _():
+            own(group).wait()
+            for h in range(hops):
+                peers(shards, lambda i: go(group, h, i, lax.rem(me + shards - i, shards), me, lambda c: c.wait_recv()))
+            widen(recv_s.at[group], wide_s)
 
     def mix(v, w_ref, bias):
         a = dot(v, w_ref[...])
@@ -488,6 +513,18 @@
     each_mode(modes, one)
     emit_slabs(out_s, out_ref)
 
+    @pl.when(g == 0)
+    def _():
+        emit_early(out_ref, early_s)
+        early.start()
+
+    @pl.when(g == GROUPS - 1)
+    def _():
+        early.finish()
+        for group in range(GROUPS):
+            for h in range(hops):
+                peers(shards, lambda i: go(group, h, i, me, to(i), lambda c: c.wait_send()))
+
 
 def group_specs(shards, rows, slab, modes, part):
     n = 2 * LAT_PAD
@@ -502,39 +539,53 @@
     return pl.BlockSpec((2, blocks // GROUPS, n, lanes or n), lambda g: (0, g, 0, 0))
 
 
-def spectral_forward(recv, tb, wi, wo, vectors, modes):
-    shards, rows, slab, width = recv.shape
+def hops_of(rows):
+    return 2 if rows % 4 == 0 else 1
+
+
+def spectral_forward(x, tb, wi, wo, vectors, shards, slab, modes, collective_id):
+    rows, lon, width = x.shape
     part = width // GROUPS
     n = 2 * LAT_PAD
     slabs, spec, _ = group_specs(shards, rows, slab, modes, part)
     lines = pl.BlockSpec((vectors.shape[0], part), lambda g: (0, g))
+    hops = hops_of(rows)
+    dma = pltpu.SemaphoreType.DMA
+    early = (shards, rows // hops, slab, part)
     return pl.pallas_call(
-        spectral_forward_kernel,
+        functools.partial(spectral_forward_kernel, hops),
         grid=(GROUPS,),
-        in_specs=[slabs, full(tb["fa"]), full(tb["ia"]), weight_spec(wi), weight_spec(wo), lines],
-        out_specs=[slabs, spec, spec, spec, spec],
+        in_specs=[full(x), full(tb["flt"]), full(tb["fa"]), full(tb["ia"]), weight_spec(wi), weight_spec(wo)]
+        + [full(vectors), lines],
+        out_specs=[slabs, spec, spec, spec, spec, pl.BlockSpec(memory_space=pl.ANY)],
         out_shape=[
-            sds(recv.shape, BF16),
+            sds((shards, rows, slab, width), BF16),
             sds((modes, n, width), BF16),
             sds((modes, n, width), BF16),
             sds((modes, n, width), F32),
             sds((modes, n, width), F32),
+            sds(early, BF16),
         ],
         scratch_shapes=[
+            pltpu.VMEM((GROUPS, shards, rows, slab, part), BF16),
+            pltpu.VMEM((GROUPS, shards, rows, slab, part), BF16),
+            pltpu.VMEM(early, BF16),
             pltpu.VMEM((part // LANES, shards * rows * slab, LANES), F32),
             pltpu.VMEM((part // LANES, slab * LAT_PAD, LANES), F32),
             pltpu.VMEM((part, 2 * part), BF16),
             pltpu.VMEM((part, 2 * part), BF16),
+            dma((GROUPS, hops, shards)), dma((GROUPS, hops, shards)), dma((GROUPS,)), dma((shards,)), dma((shards,)),
         ],
-        compiler_params=params(),
+        compiler_params=params(collective_id=collective_id, has_side_effects=True),
         name="spectral_forward",
-    )(recv, tb["fa"], tb["ia"], wi, wo, vectors)
+    )(x, tb["flt"], tb["fa"], tb["ia"], wi, wo, vectors, vectors)
 
 
 def spectral_backward_kernel(
     groups, plans, recv_ref, iat_ref, fat_ref, wo_ref, wi_ref, freq_ref, hid_ref, gp_ref, t2_ref, dw1_ref, dw2_ref,
-    out_ref, dwo_ref, dbo_ref, dwi_ref, dbi_ref, part1_ref, part2_ref,
-    wide_s, out_s, wo_s, wi_s, dwo_s, dwi_s, acc1_s, acc2_s, recv1_s, recv2_s, load_sem, send_sems, recv_sems,
+    out_ref, dwo_ref, dbo_ref, dwi_ref, dbi_ref, part1_ref, part2_ref, early_ref,
+    wide_s, out_s, wo_s, wi_s, dwo_s, dwi_s, acc1_s, acc2_s, recv1_s, recv2_s, early_s,
+    load_sem, send_sems, recv_sems, early_send, early_recv,
 ):
     shards = recv_ref.shape[0]
     slab, width = recv_ref.shape[2:]
@@ -543,6 +594,7 @@
     g = pl.program_id(0)
     me = lax.axis_index("lat")
     dp = lax.axis_index("dp")
+    early = Early(early_s, early_ref, (early_send, early_recv), early_s.shape[1], modes, slab, dp, me)
     halving = Halving(plans, (acc1_s, acc2_s), (recv1_s, recv2_s), send_sems, recv_sems, dp, me)
     loads = [
         pltpu.make_async_copy(dw1_ref, acc1_s, load_sem.at[0]),
@@ -553,13 +605,14 @@
     def _():
         for copy in loads:
             copy.start()
-        signal_all(sorted_peers(groups, shards, dp, me))
+        lat_peers = [(dp, lax.rem(me + i, shards)) for i in range(1, shards)]
+        signal_all(lat_peers + [peer for peer in dp_halving_peers(groups, dp, me)])
         for copy in loads:
             copy.wait()
         halving.start(0)
 
     whole = GROUPS * modes
-    early = [whole * n // 8 // 3 * 3 for n in (1, 4, 6, 7)]
+    when_due = [whole * n // 8 // 3 * 3 for n in (1, 4, 6, 7)]
 
     widen(recv_ref, wide_s)
     spread_blocks(wo_ref, wo_s)
@@ -569,42 +622,59 @@
     for ref in (dwo_s, dbo_ref, dwi_s, dbi_ref):
         ref[...] = jnp.zeros_like(ref)
 
-    def grads(value, grad, dw_ref, db_ref):
-        re, im = grad[:h], grad[h:]
-        low_re, low_im = re.astype(BF16), im.astype(BF16)
-        low = jnp.concatenate([low_re, low_im], 0)
-        turned = jnp.concatenate([low_im, -low_re], 0)
-        dw_ref[...] += dot_tn(value, jnp.concatenate([low, turned], 1))
-        db_ref[0:1] += jnp.sum(low_re.astype(F32), 0, keepdims=True)
-        db_ref[1:2] += jnp.sum(low_im.astype(F32), 0, keepdims=True)
-        return low
+    def lowered(grad):
+        return grad[:h].astype(BF16), grad[h:].astype(BF16)
+
+    def grads(ref, first, lows, dw_ref, db_ref):
+        value = ref[pl.ds(first, len(lows))].reshape(len(lows) * 2 * h, width)
+        both = [jnp.concatenate(low, 0) for low in lows]
+        turned = [jnp.concatenate([im, -re], 0) for re, im in lows]
+        grad = jnp.concatenate([jnp.concatenate(both, 0), jnp.concatenate(turned, 0)], 1)
+        dw_ref[...] += dot_tn(value, grad)
+        for part in range(2):
+            total = sum(jnp.sum(low[part].astype(F32), 0, keepdims=True) for low in lows)
+            db_ref[part : part + 1] += total
+        return both
 
     def pull(v, w_ref):
         a = dot_nt(v, w_ref[:, :width])
         b = dot_nt(v, w_ref[:, width:])
         return jnp.concatenate([a[:h] + b[h:], a[h:] - b[:h]], 0)
 
-    def between(m):
-        for stage, when in enumerate(early):
-            pl.when(g * modes + m == when)(functools.partial(halving.tick, stage))
-
-    def one(m):
-        merged = dot(iat_ref[...], load_mode(wide_s, m, slab, modes))
-        og = grads(hid_ref[m], merged * t2_ref[m], dwo_s, dbo_ref)
-        ig = grads(freq_ref[m], pull(og, wo_s) * gp_ref[m], dwi_s, dbi_ref)
-        fg = pull(ig, wi_s).astype(BF16)
-        store_mode(out_s, m, dot(fat_ref[...], fg))
-
-    each_mode(modes, one, between)
+    few = next(n for n in (3, 2, 1) if modes % n == 0)
+
+    def some(j, _):
+        first = j * few
+        for stage, when in enumerate(when_due):
+            pl.when(g * modes + first == when)(functools.partial(halving.tick, stage))
+        lows = []
+        for u in range(few):
+            m = first + u
+            merged = dot(iat_ref[...], load_mode(wide_s, m, slab, modes))
+            lows.append(lowered(merged * t2_ref[m]))
+        outer_grads = grads(hid_ref, first, lows, dwo_s, dbo_ref)
+        lows = [lowered(pull(og, wo_s) * gp_ref[first + u]) for u, og in enumerate(outer_grads)]
+        inner_grads = grads(freq_ref, first, lows, dwi_s, dbi_ref)
+        for u, ig in enumerate(inner_grads):
+            store_mode(out_s, first + u, dot(fat_ref[...], pull(ig, wi_s).astype(BF16)))
+        return 0
+
+    lax.fori_loop(0, modes // few, some, 0)
     pick_blocks(dwo_s, dwo_ref)
     pick_blocks(dwi_s, dwi_ref)
     emit_slabs(out_s, out_ref)
 
+    @pl.when(g == 0)
+    def _():
+        emit_early(out_ref, early_s)
+        early.start()
+
     @pl.when(g == GROUPS - 1)
     def _():
-        for stage in range(len(early), halving.stages):
+        for stage in range(len(when_due), halving.stages):
             halving.tick(stage)
         halving.keep((part1_ref, part2_ref))
+        early.finish()
 
 
 def spectral_backward(recv, tb, wo, wi, freq, hid, gp, t2, dw1, dw2, groups, plans, collective_id):
@@ -625,10 +695,11 @@
         grid=(GROUPS,),
         in_specs=[slabs, full(tb["iat"]), full(tb["fat"]), weight_spec(wo), weight_spec(wi), spec, spec, spec, spec]
         + [any_, any_],
-        out_specs=[slabs, grad, pair, grad, pair, whole(n1, dw1.shape[1]), whole(n2, dw2.shape[1])],
+        out_specs=[slabs, grad, pair, grad, pair, whole(n1, dw1.shape[1]), whole(n2, dw2.shape[1]), any_],
         out_shape=[
             sds(recv.shape, BF16), dw, db, dw, db,
             sds((n1, dw1.shape[1]), BF16), sds((n2, dw2.shape[1]), BF16),
+            sds((shards, rows, slab, part), BF16),
         ],
         scratch_shapes=[
             pltpu.VMEM((part // LANES, shards * rows * slab, LANES), F32),
@@ -641,7 +712,8 @@
             pltpu.VMEM(dw2.shape, BF16),
             pltpu.VMEM((sum(received(p) for k, _, p, _ in plans if k == 0), dw1.shape[1]), BF16),
             pltpu.VMEM((sum(received(p) for k, _, p, _ in plans if k == 1), dw2.shape[1]), BF16),
-            dma((2,)), dma((len(plans), stages)), dma((len(plans), stages)),
+            pltpu.VMEM((shards, rows, slab, part), BF16),
+            dma((2,)), dma((len(plans), stages)), dma((len(plans), stages)), dma((shards,)), dma((shards,)),
         ],
         compiler_params=params(collective_id=collective_id, has_side_effects=True),
         name="spectral_backward",
@@ -663,10 +735,10 @@
 
 
 def feed_kernel(
-    per, chunk, hops, modes, scale_ref, x_ref, c_ref, back_ref, il_ref, ilt_ref, w1_ref, w2_ref, v_ref,
+    per, chunk, hops, modes, scale_ref, x_ref, c_ref, back_ref, early_ref, il_ref, ilt_ref, w1_ref, w2_ref, v_ref,
     lo_ref, mg_ref, out_ref, dw1_ref, dw2_ref, deb_ref, drb_ref, dpg_ref, dps_ref,
     slab_s, w1_s, w2_s, act_s, pre_s, sec_s, sect_s, up_s, mixed_s, xhat_s, rs_s, branch_s, grad_s,
-    w_sem, dw_sem, in_send, in_recv, in_own, out_send, out_recv, out_own,
+    w_sem, dw_sem, early_sem, in_send, in_recv, in_own, out_send, out_recv, out_own,
 ):
     g = pl.program_id(0)
     steps = pl.num_programs(0)
@@ -679,27 +751,40 @@
     me = lax.axis_index("lat")
     dp = lax.axis_index("dp")
 
-    def transfer(src, dst, sems, h, i, sender, receiver, row_owner, mode_owner, act):
+    def transfer(src, dst, sems, h, lanes, i, sender, receiver, row_owner, mode_owner, act):
         part = pl.ds(h * hop, hop)
 
         def piece(nr, ns):
             act(send(
-                src.at[receiver, part, pl.ds(0, ns)], dst.at[sender, part, pl.ds(0, ns)],
+                src.at[receiver, part, pl.ds(0, ns), lanes], dst.at[sender, part, pl.ds(0, ns), lanes],
                 sems[0].at[h, i], sems[1].at[h, i], dp, receiver,
             ))
 
         live = row_owner * rows + h * hop < LAT
         each_size([(live, hop)], slab_sizes(mode_owner, modes, slab), piece)
 
+    known = early_ref.shape[3]
+
+    def fresh(h):
+        return pl.ds(known, width - known) if h == 0 else pl.ds(0, width)
+
     def incoming(h, i, sender, receiver, act):
-        transfer(back_ref, slab_s, (in_send, in_recv), h, i, sender, receiver, receiver, sender, act)
+        transfer(
+            back_ref, slab_s, (in_send, in_recv), h, fresh(h), i, sender, receiver, receiver, sender, act
+        )
 
     def outgoing(h, i, sender, receiver, act):
-        transfer(slab_s, out_ref, (out_send, out_recv), h, i, sender, receiver, sender, receiver, act)
+        transfer(
+            slab_s, out_ref, (out_send, out_recv), h, pl.ds(0, width), i, sender, receiver, sender, receiver, act
+        )
 
     def own_in(h):
         part = pl.ds(h * hop, hop)
-        return pltpu.make_async_copy(back_ref.at[me, part], slab_s.at[me, part], in_own.at[h])
+        return pltpu.make_async_copy(
+            back_ref.at[me, part, :, fresh(h)], slab_s.at[me, part, :, fresh(h)], in_own.at[h]
+        )
+
+    early = pltpu.make_async_copy(early_ref, slab_s.at[:, pl.ds(0, hop), :, pl.ds(0, known)], early_sem)
 
     def own_out(h):
         part = pl.ds(h * hop, hop)
@@ -711,16 +796,9 @@
     def source(i):
         return lax.rem(me + shards - i, shards)
 
-    def peers(fn):
-        def one(i, _):
-            fn(i)
-            return 0
-
-        lax.fori_loop(1, shards, one, 0)
-
     def fetch(h):
         own_in(h).start()
-        peers(lambda i: incoming(h, i, me, to(i), lambda c: c.start()))
+        peers(shards, lambda i: incoming(h, i, me, to(i), lambda c: c.start()))
 
     weights = [
         pltpu.make_async_copy(w1_ref, w1_s, w_sem.at[0]),
@@ -731,20 +809,22 @@
     def _():
         for copy in weights:
             copy.start()
+        early.start()
         greet(shards, me, dp)
         fetch(0)
         for ref in (deb_ref, drb_ref, dpg_ref, dps_ref):
             ref[...] = jnp.zeros_like(ref)
 
-    @pl.when(lax.rem(g, every) == 0)
-    def _():
-        h = g // every
-        own_in(h).wait()
-        peers(lambda i: incoming(h, i, source(i), me, lambda c: c.wait_recv()))
-
-        @pl.when(h + 1 < hops)
+    for h in range(hops):
+
+        @pl.when(g == h * every)
         def _():
-            fetch(h + 1)
+            if h == 0:
+                early.wait()
+            own_in(h).wait()
+            peers(shards, lambda i: incoming(h, i, source(i), me, lambda c: c.wait_recv()))
+            if h + 1 < hops:
+                fetch(h + 1)
 
     at = pl.ds(0 if rows == per else pl.multiple_of(g * tall, tall), tall)
     for i in range(per):
@@ -800,7 +880,7 @@
     def _():
         h = g // every
         own_out(h).start()
-        peers(lambda i: outgoing(h, i, me, to(i), lambda c: c.start()))
+        peers(shards, lambda i: outgoing(h, i, me, to(i), lambda c: c.start()))
 
     for i in range(per):
         rows_i = pl.ds(i * COLS, COLS)
@@ -834,7 +914,7 @@
 
         lax.fori_loop(0, hidden // chunk, weight_chunk, 0)
 
-        def one(h, _):
+        for h in range(hops):
             own_out(h).wait()
 
             def wait_all(i):
@@ -842,10 +922,7 @@
                 outgoing(h, i, me, to(i), lambda c: c.wait_send())
                 outgoing(h, i, source(i), me, lambda c: c.wait_recv())
 
-            peers(wait_all)
-            return 0
-
-        lax.fori_loop(0, hops, one, 0)
+            peers(shards, wait_all)
 
         def finish(j, _):
             for copy in gradients(j):
@@ -855,13 +932,13 @@
         lax.fori_loop(0, hidden // chunk, finish, 0)
 
 
-def feed(scale, x, cot, back, tb, w1, w2, vectors, modes, collective_id):
+def feed(scale, x, cot, back, early, tb, w1, w2, vectors, modes, collective_id):
     rows, lon, width = x.shape
     hidden = w1.shape[1]
     shards, _, slab, _ = back.shape
     per = next(n for n in (2, 3, 1) if rows % n == 0)
     steps = rows // per
-    hops = 2 if steps % 2 == 0 else 1
+    hops = hops_of(rows)
     chunk = width
     row = pl.BlockSpec((per, lon, width), lambda g: (g, 0, 0))
     any_ = pl.BlockSpec(memory_space=pl.ANY)
@@ -873,7 +950,7 @@
         functools.partial(feed_kernel, per, chunk, hops, modes),
         grid=(steps,),
         in_specs=[
-            pl.BlockSpec(memory_space=pltpu.SMEM), row, row, any_, full(tb["il"]), full(tb["ilt"]), any_, any_,
+            pl.BlockSpec(memory_space=pltpu.SMEM), row, row, any_, any_, full(tb["il"]), full(tb["ilt"]), any_, any_,
             full(vectors),
         ],
         out_specs=[row, row, any_, any_, any_, vec(hidden // width), vec(1), vec(1), vec(1)],
@@ -902,7 +979,7 @@
             pltpu.VMEM((tall, LANES), F32),
             pltpu.VMEM((tall, width), F32),
             pltpu.VMEM((tall, width), F32),
-            dma((2,)), dma((2, hidden // chunk)),
+            dma((2,)), dma((2, hidden // chunk)), dma,
             dma((hops, shards)), dma((hops, shards)), dma((hops,)),
             dma((hops, shards)), dma((hops, shards)), dma((hops,)),
         ],
@@ -910,17 +987,17 @@
             vmem_limit_bytes=63 * 2**20, collective_id=collective_id, has_side_effects=True
         ),
         name="feed",
-    )(scale, x, cot, back, tb["il"], tb["ilt"], w1, w2, vectors)
+    )(scale, x, cot, back, early, tb["il"], tb["ilt"], w1, w2, vectors)
 
 
 def leave_kernel(
-    groups, hops, modes, plans, x_ref, back_ref, mg_ref, fl_ref, v_ref, *refs,
+    groups, hops, modes, plans, x_ref, back_ref, early_ref, mg_ref, fl_ref, v_ref, *refs,
 ):
     weight_refs, line_refs, refs = refs[:2], refs[2:8], refs[8:]
     (
         part1_ref, part2_ref, out_ref, sums_ref, norm_ref, dw1_ref, dw2_ref,
         slab_s, line_s, mine_s, from_dp, part_s, from_lat, all_s, norm_lat, norm_dp,
-        in_send, in_recv, in_own, wide_send, wide_recv, own_sem, small_sems,
+        in_send, in_recv, in_own, early_sem, wide_send, wide_recv, own_sem, small_sems,
     ) = refs
     g = pl.program_id(0)
     steps = pl.num_programs(0)
@@ -933,12 +1010,16 @@
     lat_peers = [lax.rem(me + i, shards) for i in range(1, shards)]
     dp_peers = [lax.rem(dp + i, groups) for i in range(1, groups)]
 
+    known = early_ref.shape[3]
+    fresh = pl.ds(known, slab_s.shape[3] - known)
+    early = pltpu.make_async_copy(early_ref, slab_s.at[:, :, :, pl.ds(0, known)], early_sem)
+
     def incoming(h, i, sender, receiver, act):
         part = pl.ds(h * hop, hop)
 
         def piece(nr, ns):
             act(send(
-                back_ref.at[receiver, part, pl.ds(0, ns)], slab_s.at[sender, part, pl.ds(0, ns)],
+                back_ref.at[receiver, part, pl.ds(0, ns), fresh], slab_s.at[sender, part, pl.ds(0, ns), fresh],
                 in_send.at[h, i], in_recv.at[h, i], dp, receiver,
             ))
 
@@ -947,22 +1028,15 @@
 
     def own_in(h):
         part = pl.ds(h * hop, hop)
-        return pltpu.make_async_copy(back_ref.at[me, part], slab_s.at[me, part], in_own.at[h])
-
-    def peers(fn):
-        def one(i, _):
-            fn(i)
-            return 0
-
-        lax.fori_loop(1, shards, one, 0)
+        return pltpu.make_async_copy(back_ref.at[me, part, :, fresh], slab_s.at[me, part, :, fresh], in_own.at[h])
 
     def fetch(h):
         own_in(h).start()
-        peers(lambda i: incoming(h, i, me, lax.rem(me + i, shards), lambda c: c.start()))
+        peers(shards, lambda i: incoming(h, i, me, lax.rem(me + i, shards), lambda c: c.start()))
 
     def arrived(h):
         own_in(h).wait()
-        peers(lambda i: incoming(h, i, lax.rem(me + shards - i, shards), me, lambda c: c.wait_recv()))
+        peers(shards, lambda i: incoming(h, i, lax.rem(me + shards - i, shards), me, lambda c: c.wait_recv()))
 
     walks = [halving_walk(first, plan, dp, me) for _, first, plan, _ in plans]
     outs = (dw1_ref, dw2_ref)
@@ -1018,19 +1092,19 @@
         return [(i, p, (p, me) if axis == "dp" else (dp, p)) for i, p in enumerate(peers_)]
 
     block = shards * n
-    mine = rows_at((dp * shards + me) * n, n)
-    mine_dp = rows_at(dp * block, block)
+    mine = low_rows_at((dp * shards + me) * n, n)
+    mine_dp = low_rows_at(dp * block, block)
     tiles = line_s.shape[1] // LANES
 
     def small(stage):
         if stage == 0:
             return [
-                remote(mine_s.at[rows_at(p * block, block)], from_dp.at[i], 0, i, to)
+                remote(mine_s.at[low_rows_at(p * block, block)], from_dp.at[i], 0, i, to)
                 for i, p, to in over(dp_peers, "dp")
             ]
         if stage == 1:
             return [
-                remote(part_s.at[rows_at(p * n, n)], from_lat.at[i], 1, i, to)
+                remote(part_s.at[low_rows_at(p * n, n)], from_lat.at[i], 1, i, to)
                 for i, p, to in over(lat_peers, "lat")
             ]
         if stage == 2:
@@ -1049,9 +1123,11 @@
         for copy in small(stage):
             copy.wait()
         if stage == 0:
-            part_s[...] = mine_s[mine_dp, :] + jnp.sum(from_dp[...], 0)
+            whole = mine_s[mine_dp, :].astype(F32) + jnp.sum(from_dp[...].astype(F32), 0)
+            part_s[...] = whole.astype(BF16)
         if stage == 1:
-            all_s[mine, :] = part_s[rows_at(me * n, n), :] + jnp.sum(from_lat[...], 0)
+            whole = part_s[low_rows_at(me * n, n), :].astype(F32) + jnp.sum(from_lat[...].astype(F32), 0)
+            all_s[mine, :] = whole.astype(BF16)
 
     def small_tick(stage):
         end(stage)
@@ -1062,15 +1138,18 @@
         at = 0
         for ref in weight_refs:
             value = ref[...].reshape(-1, LANES)
-            mine_s[at : at + value.shape[0], :] = value
+            mine_s[at : at + value.shape[0], :] = value.astype(BF16)
             at += value.shape[0]
-        mine_s[at:, :] = jnp.zeros((mine_s.shape[0] - at, LANES), F32)
-        for ref in line_refs:
-            for row in range(ref.shape[0]):
-                for t in range(tiles):
-                    mine_s[at : at + 1, :] = ref[row : row + 1, t * LANES : (t + 1) * LANES]
-                    at += 1
+        lines = [
+            ref[row : row + 1, t * LANES : (t + 1) * LANES]
+            for ref in line_refs
+            for row in range(ref.shape[0])
+            for t in range(tiles)
+        ]
+        lines.append(jnp.zeros((mine_s.shape[0] - at - len(lines), LANES), F32))
+        mine_s[at:, :] = jnp.concatenate(lines, 0).astype(BF16)
         signal_all([(dp, p) for p in lat_peers] + [(p, me) for p in dp_peers])
+        early.start()
         for j in range(count):
             own_part(j).start()
         spread_all(stages - 1, lambda c: c.start())
@@ -1079,6 +1158,7 @@
         line_s[...] = jnp.zeros_like(line_s)
         tick(0)
         small_tick(0)
+        early.wait()
         arrived(0)
         tick(1)
         small_tick(1)
@@ -1114,19 +1194,19 @@
         norm_dp[dp] = jnp.sum(norm_lat[...], 0)
         begin(5)
         end(3)
-        sums_ref[...] = all_s[...]
+        sums_ref[...] = all_s[...].astype(F32)
         for h in range(hops):
-            peers(lambda i: incoming(h, i, me, lax.rem(me + i, shards), lambda c: c.wait_send()))
+            peers(shards, lambda i: incoming(h, i, me, lax.rem(me + i, shards), lambda c: c.wait_send()))
         end(5)
         norm_ref[...] = jnp.sum(norm_dp[...], 0)
 
 
-def leave(x, back, mg, fl, vectors, small, part1, part2, shapes, groups, plans, modes, collective_id):
+def leave(x, back, early, mg, fl, vectors, small, part1, part2, shapes, groups, plans, modes, collective_id):
     rows, lon, width = x.shape
     shards, _, slab, _ = back.shape
-    hops = 2 if rows % 2 == 0 else 1
+    hops = hops_of(rows)
     stages = len(plans[0][2])
-    unit = 8 * groups * shards
+    unit = LOW_ROWS * groups * shards
     total = -(-sum(v.size // LANES for v in small) // unit) * unit
     n = total // (groups * shards)
     row = pl.BlockSpec((1, lon, width), lambda r: (r, 0, 0))
@@ -1136,27 +1216,27 @@
     return pl.pallas_call(
         functools.partial(leave_kernel, groups, hops, modes, plans),
         grid=(rows,),
-        in_specs=[row, any_, row, full(fl), full(vectors)] + [full(v) for v in small] + [any_, any_],
+        in_specs=[row, any_, any_, row, full(fl), full(vectors)] + [full(v) for v in small] + [any_, any_],
         out_specs=[row, whole(total, LANES), whole(2, width), any_, any_],
         out_shape=[sds((rows, lon, width), F32), sds((total, LANES), F32), sds((2, width), F32)]
         + [sds(shape, BF16) for shape in shapes],
         scratch_shapes=[
             pltpu.VMEM(back.shape, BF16),
             pltpu.VMEM((2, width), F32),
-            pltpu.VMEM((total, LANES), F32),
-            pltpu.VMEM((groups - 1, shards * n, LANES), F32),
-            pltpu.VMEM((shards * n, LANES), F32),
-            pltpu.VMEM((shards - 1, n, LANES), F32),
-            pltpu.VMEM((total, LANES), F32),
+            pltpu.VMEM((total, LANES), BF16),
+            pltpu.VMEM((groups - 1, shards * n, LANES), BF16),
+            pltpu.VMEM((shards * n, LANES), BF16),
+            pltpu.VMEM((shards - 1, n, LANES), BF16),
+            pltpu.VMEM((total, LANES), BF16),
             pltpu.VMEM((shards, 2, width), F32),
             pltpu.VMEM((groups, 2, width), F32),
-            dma((hops, shards)), dma((hops, shards)), dma((hops,)),
+            dma((hops, shards)), dma((hops, shards)), dma((hops,)), dma,
             dma((len(plans), stages)), dma((len(plans), stages)), dma((len(plans),)),
             dma((6, 2, max(groups, shards) - 1)),
         ],
         compiler_params=params(collective_id=collective_id, has_side_effects=True),
         name="leave",
-    )(x, back, mg, fl, vectors, *small, part1, part2)
+    )(x, back, early, mg, fl, vectors, *small, part1, part2)
 
 
 def shards_fn(
@@ -1177,18 +1257,19 @@
         inner_bias.reshape(-1), outer_bias.reshape(-1), expand_bias,
     ]).reshape(-1, width)
 
-    spec = exchange(enter(x, tb["flt"], vectors, shards, slab), True, modes, 0)
-    back, freq, hid, gp, t2 = spectral_forward(spec, tb, inner_weight, outer_weight, vectors, modes)
+    back, freq, hid, gp, t2, early = spectral_forward(
+        x, tb, inner_weight, outer_weight, vectors, shards, slab, modes, 0
+    )
     (layer_out, mixed_grad, mode_grad, dw1, dw2, deb, drb, dpg, dps) = feed(
-        scale, x, cot, back, tb, expand_weight, reduce_weight, vectors, modes, 1
+        scale, x, cot, back, early, tb, expand_weight, reduce_weight, vectors, modes, 1
     )
     plans = halving_plans(groups, shards, (dw1.shape[0], dw2.shape[0]))
-    slab_grad, dwo, dbo, dwi, dbi, part1, part2 = spectral_backward(
+    slab_grad, dwo, dbo, dwi, dbi, part1, part2, early = spectral_backward(
         mode_grad, tb, outer_weight, inner_weight, freq, hid, gp, t2, dw1, dw2, groups, plans, 2
     )
     small = (dwi, dwo, dbi, dbo, dpg, dps, deb, drb)
     input_grad, sums, norm, dw1, dw2 = leave(
-        x, slab_grad, mixed_grad, tb["fl"], vectors, small, part1, part2,
+        x, slab_grad, early, mixed_grad, tb["fl"], vectors, small, part1, part2,
         (dw1.shape, dw2.shape), groups, plans, modes, 3
     )
     dw1 = jnp.concatenate([dw1[:width], dw1[width:]], 1).astype(F32)

time: 538 us -> 489 us (0.909)
  Pallas kernels: 501 us -> 452 us
    pallas_call x1, Pallas kernels: 169 us -> 134 us  [feed(): pl.pallas_call(functools.partial(feed_kernel, per, chunk, hops, modes), g...]
    pallas_call x1, Pallas kernels: 135 us -> 99.5 us  [leave(): pl.pallas_call(functools.partial(leave_kernel, groups, hops, modes, plans...]
    pallas_call x1, Pallas kernels: 91 us -> 108 us  [spectral_backward(): pl.pallas_call(functools.partial(spectral_backward_kernel, groups, plans)...]
    pallas_call x3 -> x1, Pallas kernels: 106 us -> 111 us  [spectral_forward(): pl.pallas_call(functools.partial(spectral_forward_kernel, hops), grid=(GR...]
where the time goes in v4:
time: 489 us; the launch traced here: 488 us
  Pallas kernels  452 us (92%)
  local copies, waits for them, and re-layouts  24.4 us (5%)
  other arithmetic  10.1 us (2%)
    pallas_call x1, Pallas kernels, feed(): pl.pallas_call(functools.partial(feed_kernel, per, chunk, hops, modes), g...  134 us
    pallas_call x1, Pallas kernels, spectral_forward(): pl.pallas_call(functools.partial(spectral_forward_kernel, hops), grid=(GR...  111 us
    pallas_call x1, Pallas kernels, spectral_backward(): pl.pallas_call(functools.partial(spectral_backward_kernel, groups, plans)...  108 us
    pallas_call x1, Pallas kernels, leave(): pl.pallas_call(functools.partial(leave_kernel, groups, hops, modes, plans...  99.5 us
    unnamed x19, local copies, waits for them, and re-layouts  14.3 us

profile of v4, /device:TPU:0, one launch (start us, length us, event | category | flops | bytes accessed | tf_op | source)
XLA Modules:
  0.0 488.0 jit_solution(1613292336028184595)
XLA Ops:
  1.9 0.8 reshape.81
  2.7 0.8 reshape.82
  3.4 0.7 constant_dynamic-update-slice_fusion.7
  4.1 0.7 constant_dynamic-update-slice_fusion.6
  4.8 0.7 constant_dynamic-update-slice_fusion.5
  5.5 0.7 constant_dynamic-update-slice_fusion.4
  6.2 0.7 constant_dynamic-update-slice_fusion.3
  6.9 0.7 constant_dynamic-update-slice_fusion
  7.6 0.6 reshape.83.all_ref.v_ref
  8.3 110.6 %spectral_forward.1 = (bf16[8,12,24,768]{3,2,1,0:T(8,128)(2,1)}, bf16[12,192,768]{2,1,0:T(8,128)(2,1)}, bf16[12,192,768]{2,1,0:T(8,128)(2,1)}, f32[12,192,768]{2...) custom-call(bf16[12,180,768]{2,1,0:T(8,128)(2,1)} %bitcast.17, ...), custom_call_target="tpu_custom_call" | custom-call | tf_op jit(solution)/shard_map/spectral_forward/pallas_call | solution.py:555
  118.8 133.8 %feed.1 = (bf16[12,180,768]{2,1,0:T(8,128)(2,1)}, f32[12,180,768]{2,1,0:T(8,128)}, bf16[8,12,24,768]{3,2,1,0:T(8,128)(2,1)}, bf16[1536,1536]{1,0:T(8,128)(2,1)},...) custom-call(f32[2,12]{1,0:T(2,128)} %pad_maximum_fusion.scale_ref, ...), custom_call_target="tpu_custom_call" | custom-call | tf_op jit(solution)/shard_map/feed/pallas_call | solution.py:949
  252.7 108.2 %spectral_backward.1 = (bf16[8,12,24,768]{3,2,1,0:T(8,128)(2,1)}, f32[2,8,96,128]{3,2,1,0:T(8,128)}, f32[2,768]{1,0:T(2,128)}, f32[2,8,96,128]{3,2,1,0:T(8,128)}...) custom-call(bf16[8,12,24,768]{3,2,1,0:T(8,128)(2,1)} %get-tuple-eleme, ...), custom_call_target="tpu_custom_call" | custom-call | tf_op jit(solution)/shard_map/spectral_backward/pallas_call | solution.py:693
  360.9 99.5 %leave.1 = (f32[12,180,768]{2,1,0:T(8,128)}, f32[3584,128]{1,0:T(8,128)}, f32[2,768]{1,0:T(2,128)}, bf16[1536,1536]{1,0:T(8,128)(2,1)}, bf16[3072,768]{1,0:T(8,128)(2,1)}) custom-call(bf16[12,180,768]{2,1,0:T(8,128)(2,1)} %bitcast.19, bf16[8,12,24,768]{3,2,1,0:T(8,128)(2,1)} %get-tuple-element.52.back_ref, ...), custom_call_target="tpu_custom_call" | custom-call | tf_op jit(solution)/shard_map/leave/pallas_call | solution.py:1216
  460.4 9.0 %copy.37 = f32[1,12,180,768]{3,0,2,1:T(1,128)} copy(f32[1,12,180,768]{3,2,1,0:T(8,128)} %bitcast.20) | data formatting | bytes 13271040
  469.4 0.6 slice_reduce_fusion
  470.0 0.6 slice_bitcast_fusion
  470.6 0.6 slice_bitcast_fusion.1
  471.3 1.2 fusion.2
  472.5 0.7 reshape.87
  473.2 0.7 reshape.85
  473.8 2.8 fusion
  476.7 5.0 %maximum_convert_fusion = f32[768,3072]{1,0:T(8,128)} fusion(bf16[768,1536]{1,0:T(8,128)(2,1)S(1)} %get-tuple-element.87, bf16[768,1536]{1,0:T(8,128)(2,1)S(1)} %get-tuple-element.86), kind=kLoop, calls=%fused_computation | loop fusion | flops 9437184 | bytes 14155776 | tf_op jit(solution)/shard_map/convert_element_type | solution.py:1275
  481.7 4.5 convert_element_type.23
  486.2 1.7 copy.48
  (18 shorter events, 0.6 us)
Async XLA Ops:
  460.4 9.0 %copy-start.2 = (f32[2,768]{1,0:T(2,128)S(1)}, f32[2,768]{1,0:T(2,128)}, u32[]{:S(2)}) copy-start(f32[2,768]{1,0:T(2,128)} %get-tuple-element.66) | copy-start | bytes 18436
  460.4 9.6 %copy-start.1 = (f32[3584,128]{1,0:T(8,128)S(1)}, f32[3584,128]{1,0:T(8,128)}, u32[]{:S(2)}) copy-start(f32[3584,128]{1,0:T(8,128)} %get-tuple-element.67) | copy-start | bytes 5505028
  473.8 7.9 %slice-start = ((s8[4718592]{0:T(1024)(128)(4,1)}), s8[4194304]{0:T(1024)(128)(4,1)S(1)}, s32[]{:S(2)}) async-start(s8[4718592]{0:T(1024)(128)(4,1)} %bitcast.21), calls=%async_computation | async-start | bytes 8388608
  476.7 5.0 %slice-start.1 = ((s8[4718592]{0:T(1024)(128)(4,1)}), s8[524288]{0:T(1024)(128)(4,1)S(1)}, s32[]{:S(2)}) async-start(s8[4718592]{0:T(1024)(128)(4,1)} %bitcast.21), calls=%async_computation.1 | async-start | bytes 1048576
  481.7 4.5 copy-start

commit v5 on v4

--- a/solution.py
+++ b/solution.py
@@ -131,6 +131,21 @@
     return v_ref[row : row + 1, :]
 
 
+VECTOR_ROWS = 16
+
+
+def put_vectors(v_s, flat, blocked):
+    width = v_s.shape[1]
+    for row, ref in flat:
+        for i in range(ref.shape[0] // width):
+            v_s[row + i : row + i + 1, :] = ref[i * width : (i + 1) * width].reshape(1, width)
+    for row, ref in blocked:
+        _, blocks, n = ref.shape
+        for p in range(2):
+            for b in range(blocks):
+                v_s[row + p : row + p + 1, b * n : (b + 1) * n] = ref[p, b : b + 1, :]
+
+
 def up8(n):
     return -(-n // 8) * 8
 
@@ -422,9 +437,9 @@
 
 
 def spectral_forward_kernel(
-    hops, x_ref, flt_ref, fa_ref, ia_ref, wi_ref, wo_ref, all_ref, v_ref,
+    hops, x_ref, flt_ref, fa_ref, ia_ref, wi_ref, wo_ref, ng_ref, ns_ref, bi_ref, bo_ref,
     out_ref, freq_ref, hid_ref, gp_ref, t2_ref, early_ref,
-    stage_s, recv_s, early_s, wide_s, out_s, wi_s, wo_s, go_send, go_recv, go_own, early_send, early_recv,
+    v_s, stage_s, recv_s, early_s, wide_s, out_s, wi_s, wo_s, go_send, go_recv, go_own, early_send, early_recv,
 ):
     g = pl.program_id(0)
     rows, lon, _ = x_ref.shape
@@ -460,13 +475,14 @@
     def _():
         def row(r, _):
             c, rs = center_scale(pad_rows(x_ref[r].astype(F32), COLS))
-            first = (c * rs * vector(all_ref, NORM_G) + vector(all_ref, NORM_S)).astype(BF16)
+            first = (c * rs * vector(v_s, NORM_G) + vector(v_s, NORM_S)).astype(BF16)
             spec = dot(flt_ref[...], first).astype(BF16)
             for group in range(GROUPS):
                 part = spec[:, group * width : (group + 1) * width]
                 stage_s[group, :, r] = part.reshape(shards, slab, width)
             return 0
 
+        put_vectors(v_s, ((NORM_G, ng_ref), (NORM_S, ns_ref)), ((INNER_B, bi_ref), (OUTER_B, bo_ref)))
         for h in range(hops):
             lax.fori_loop(h * hop, (h + 1) * hop, row, 0)
             if h == 0:
@@ -493,8 +509,9 @@
 
     def mix(v, w_ref, bias):
         a = dot(v, w_ref[...])
-        re = a[:h, :width] - a[h:, width:] + vector(v_ref, bias)
-        im = a[h:, :width] + a[:h, width:] + vector(v_ref, bias + 1)
+        lanes = pl.ds(pl.multiple_of(g * width, LANES), width)
+        re = a[:h, :width] - a[h:, width:] + v_s[bias : bias + 1, lanes]
+        im = a[h:, :width] + a[:h, width:] + v_s[bias + 1 : bias + 2, lanes]
         return jnp.concatenate([re, im], 0)
 
     def one(m):
@@ -548,7 +565,6 @@
     part = width // GROUPS
     n = 2 * LAT_PAD
     slabs, spec, _ = group_specs(shards, rows, slab, modes, part)
-    lines = pl.BlockSpec((vectors.shape[0], part), lambda g: (0, g))
     hops = hops_of(rows)
     dma = pltpu.SemaphoreType.DMA
     early = (shards, rows // hops, slab, part)
@@ -556,7 +572,7 @@
         functools.partial(spectral_forward_kernel, hops),
         grid=(GROUPS,),
         in_specs=[full(x), full(tb["flt"]), full(tb["fa"]), full(tb["ia"]), weight_spec(wi), weight_spec(wo)]
-        + [full(vectors), lines],
+        + [full(v) for v in vectors],
         out_specs=[slabs, spec, spec, spec, spec, pl.BlockSpec(memory_space=pl.ANY)],
         out_shape=[
             sds((shards, rows, slab, width), BF16),
@@ -567,6 +583,7 @@
             sds(early, BF16),
         ],
         scratch_shapes=[
+            pltpu.VMEM((VECTOR_ROWS, width), F32),
             pltpu.VMEM((GROUPS, shards, rows, slab, part), BF16),
             pltpu.VMEM((GROUPS, shards, rows, slab, part), BF16),
             pltpu.VMEM(early, BF16),
@@ -578,7 +595,7 @@
         ],
         compiler_params=params(collective_id=collective_id, has_side_effects=True),
         name="spectral_forward",
-    )(x, tb["flt"], tb["fa"], tb["ia"], wi, wo, vectors, vectors)
+    )(x, tb["flt"], tb["fa"], tb["ia"], wi, wo, *vectors)
 
 
 def spectral_backward_kernel(
@@ -735,9 +752,10 @@
 
 
 def feed_kernel(
-    per, chunk, hops, modes, scale_ref, x_ref, c_ref, back_ref, early_ref, il_ref, ilt_ref, w1_ref, w2_ref, v_ref,
+    per, chunk, hops, modes, scale_ref, x_ref, c_ref, back_ref, early_ref, il_ref, ilt_ref, w1_ref, w2_ref,
+    ng_ref, ns_ref, pg_ref, ps_ref, rb_ref, eb_ref,
     lo_ref, mg_ref, out_ref, dw1_ref, dw2_ref, deb_ref, drb_ref, dpg_ref, dps_ref,
-    slab_s, w1_s, w2_s, act_s, pre_s, sec_s, sect_s, up_s, mixed_s, xhat_s, rs_s, branch_s, grad_s,
+    v_ref, slab_s, w1_s, w2_s, act_s, pre_s, sec_s, sect_s, up_s, mixed_s, xhat_s, rs_s, branch_s, grad_s,
     w_sem, dw_sem, early_sem, in_send, in_recv, in_own, out_send, out_recv, out_own,
 ):
     g = pl.program_id(0)
@@ -812,6 +830,14 @@
         early.start()
         greet(shards, me, dp)
         fetch(0)
+        put_vectors(
+            v_ref,
+            (
+                (NORM_G, ng_ref), (NORM_S, ns_ref), (POST_G, pg_ref), (POST_S, ps_ref), (REDUCE_B, rb_ref),
+                (EXPAND_B, eb_ref),
+            ),
+            (),
+        )
         for ref in (deb_ref, drb_ref, dpg_ref, dps_ref):
             ref[...] = jnp.zeros_like(ref)
 
@@ -951,8 +977,8 @@
         grid=(steps,),
         in_specs=[
             pl.BlockSpec(memory_space=pltpu.SMEM), row, row, any_, any_, full(tb["il"]), full(tb["ilt"]), any_, any_,
-            full(vectors),
-        ],
+        ]
+        + [full(v) for v in vectors],
         out_specs=[row, row, any_, any_, any_, vec(hidden // width), vec(1), vec(1), vec(1)],
         out_shape=[
             sds((rows, lon, width), BF16),
@@ -966,6 +992,7 @@
             sds((1, width), F32),
         ],
         scratch_shapes=[
+            pltpu.VMEM((VECTOR_ROWS, width), F32),
             pltpu.VMEM(back.shape, BF16),
             pltpu.VMEM(w1.shape, BF16),
             pltpu.VMEM(w2.shape, BF16),
@@ -987,16 +1014,16 @@
             vmem_limit_bytes=63 * 2**20, collective_id=collective_id, has_side_effects=True
         ),
         name="feed",
-    )(scale, x, cot, back, early, tb["il"], tb["ilt"], w1, w2, vectors)
+    )(scale, x, cot, back, early, tb["il"], tb["ilt"], w1, w2, *vectors)
 
 
 def leave_kernel(
-    groups, hops, modes, plans, x_ref, back_ref, early_ref, mg_ref, fl_ref, v_ref, *refs,
+    groups, hops, modes, plans, x_ref, back_ref, early_ref, mg_ref, fl_ref, ng_ref, *refs,
 ):
     weight_refs, line_refs, refs = refs[:2], refs[2:8], refs[8:]
     (
         part1_ref, part2_ref, out_ref, sums_ref, norm_ref, dw1_ref, dw2_ref,
-        slab_s, line_s, mine_s, from_dp, part_s, from_lat, all_s, norm_lat, norm_dp,
+        v_ref, slab_s, line_s, mine_s, from_dp, part_s, from_lat, all_s, norm_lat, norm_dp,
         in_send, in_recv, in_own, early_sem, wide_send, wide_recv, own_sem, small_sems,
     ) = refs
     g = pl.program_id(0)
@@ -1135,6 +1162,13 @@
 
     @pl.when(g == 0)
     def _():
+        early.start()
+        for j in range(count):
+            own_part(j).start()
+        signal_all([(dp, p) for p in lat_peers] + [(p, me) for p in dp_peers])
+        spread_all(stages - 1, lambda c: c.start())
+        fetch(0)
+        put_vectors(v_ref, ((NORM_G, ng_ref),), ())
         at = 0
         for ref in weight_refs:
             value = ref[...].reshape(-1, LANES)
@@ -1148,13 +1182,7 @@
         ]
         lines.append(jnp.zeros((mine_s.shape[0] - at - len(lines), LANES), F32))
         mine_s[at:, :] = jnp.concatenate(lines, 0).astype(BF16)
-        signal_all([(dp, p) for p in lat_peers] + [(p, me) for p in dp_peers])
-        early.start()
-        for j in range(count):
-            own_part(j).start()
-        spread_all(stages - 1, lambda c: c.start())
         begin(0)
-        fetch(0)
         line_s[...] = jnp.zeros_like(line_s)
         tick(0)
         small_tick(0)
@@ -1177,7 +1205,7 @@
     grad = jnp.where(live, spectrum, jnp.zeros_like(spectrum)) + mg
     line_s[0:1] += jnp.sum(grad * xhat, 0, keepdims=True)
     line_s[1:2] += jnp.sum(grad, 0, keepdims=True)
-    out_ref[0] = (mg + norm_back(grad, xhat, rs, vector(v_ref, NORM_G)))[:lon]
+    out_ref[...] = (mg + norm_back(grad, xhat, rs, vector(v_ref, NORM_G)))[:lon].reshape(out_ref.shape)
 
     @pl.when(g == hop - 1)
     def _():
@@ -1201,7 +1229,7 @@
         norm_ref[...] = jnp.sum(norm_dp[...], 0)
 
 
-def leave(x, back, early, mg, fl, vectors, small, part1, part2, shapes, groups, plans, modes, collective_id):
+def leave(x, back, early, mg, fl, gain, small, part1, part2, shapes, groups, plans, modes, collective_id):
     rows, lon, width = x.shape
     shards, _, slab, _ = back.shape
     hops = hops_of(rows)
@@ -1216,11 +1244,12 @@
     return pl.pallas_call(
         functools.partial(leave_kernel, groups, hops, modes, plans),
         grid=(rows,),
-        in_specs=[row, any_, any_, row, full(fl), full(vectors)] + [full(v) for v in small] + [any_, any_],
-        out_specs=[row, whole(total, LANES), whole(2, width), any_, any_],
-        out_shape=[sds((rows, lon, width), F32), sds((total, LANES), F32), sds((2, width), F32)]
+        in_specs=[row, any_, any_, row, full(fl), full(gain)] + [full(v) for v in small] + [any_, any_],
+        out_specs=[pl.BlockSpec((lon, 1, width), lambda r: (r, 0, 0)), whole(total, LANES), whole(2, width), any_, any_],
+        out_shape=[sds((rows * lon, 1, width), F32), sds((total, LANES), F32), sds((2, width), F32)]
         + [sds(shape, BF16) for shape in shapes],
         scratch_shapes=[
+            pltpu.VMEM((VECTOR_ROWS, width), F32),
             pltpu.VMEM(back.shape, BF16),
             pltpu.VMEM((2, width), F32),
             pltpu.VMEM((total, LANES), BF16),
@@ -1236,7 +1265,7 @@
         ],
         compiler_params=params(collective_id=collective_id, has_side_effects=True),
         name="leave",
-    )(x, back, early, mg, fl, vectors, *small, part1, part2)
+    )(x, back, early, mg, fl, gain, *small, part1, part2)
 
 
 def shards_fn(
@@ -1252,16 +1281,12 @@
     scale = jnp.stack([keep * (storm_weight[0].astype(F32) / 64.0), keep])
     x = inputs[0]
     cot = cotangent[0]
-    vectors = jnp.concatenate([
-        norm_gain, norm_shift, post_gain, post_shift, reduce_bias,
-        inner_bias.reshape(-1), outer_bias.reshape(-1), expand_bias,
-    ]).reshape(-1, width)
-
     back, freq, hid, gp, t2, early = spectral_forward(
-        x, tb, inner_weight, outer_weight, vectors, shards, slab, modes, 0
+        x, tb, inner_weight, outer_weight, (norm_gain, norm_shift, inner_bias, outer_bias), shards, slab, modes, 0
     )
     (layer_out, mixed_grad, mode_grad, dw1, dw2, deb, drb, dpg, dps) = feed(
-        scale, x, cot, back, early, tb, expand_weight, reduce_weight, vectors, modes, 1
+        scale, x, cot, back, early, tb, expand_weight, reduce_weight,
+        (norm_gain, norm_shift, post_gain, post_shift, reduce_bias, expand_bias), modes, 1
     )
     plans = halving_plans(groups, shards, (dw1.shape[0], dw2.shape[0]))
     slab_grad, dwo, dbo, dwi, dbi, part1, part2, early = spectral_backward(
@@ -1269,7 +1294,7 @@
     )
     small = (dwi, dwo, dbi, dbo, dpg, dps, deb, drb)
     input_grad, sums, norm, dw1, dw2 = leave(
-        x, slab_grad, early, mixed_grad, tb["fl"], vectors, small, part1, part2,
+        x, slab_grad, early, mixed_grad, tb["fl"], norm_gain, small, part1, part2,
         (dw1.shape, dw2.shape), groups, plans, modes, 3
     )
     dw1 = jnp.concatenate([dw1[:width], dw1[width:]], 1).astype(F32)
@@ -1282,7 +1307,7 @@
     weight = lambda v: v.reshape(inner_weight.shape[:3] + (LANES,))[..., :block]
     line = lambda v: v.reshape(-1)
     return (
-        layer_out[None], input_grad[None], norm[0], norm[1],
+        layer_out[None], input_grad.reshape(1, rows, lon, width), norm[0], norm[1],
         weight(dwi), dbi.reshape(inner_bias.shape), weight(dwo), dbo.reshape(outer_bias.shape),
         line(dpg), line(dps), dw1, line(deb), dw2, line(drb),
     )

time: 489 us -> 482 us (0.986)
  local copies, waits for them, and re-layouts: 24.4 us -> 16.2 us
    unnamed x19 -> x12, local copies, waits for them, and re-layouts: 14.3 us -> 4.58 us
where the time goes in v5:
time: 482 us; the launch traced here: 481 us
  Pallas kernels  452 us (94%)
  local copies, waits for them, and re-layouts  16.2 us (3%)
  other arithmetic  11.1 us (2%)
    pallas_call x1, Pallas kernels, feed(): pl.pallas_call(functools.partial(feed_kernel, per, chunk, hops, modes), g...  134 us
    pallas_call x1, Pallas kernels, spectral_forward(): pl.pallas_call(functools.partial(spectral_forward_kernel, hops), grid=(GR...  111 us
    pallas_call x1, Pallas kernels, spectral_backward(): pl.pallas_call(functools.partial(spectral_backward_kernel, groups, plans)...  108 us
    pallas_call x1, Pallas kernels, leave(): pl.pallas_call(functools.partial(leave_kernel, groups, hops, modes, plans...  99.3 us

profile of v5, /device:TPU:0, one launch (start us, length us, event | category | flops | bytes accessed | tf_op | source)
XLA Modules:
  0.0 480.9 jit_solution(16993991524968504976)
XLA Ops:
  1.3 0.6 pad_maximum_fusion.scale_ref
  1.9 110.7 %spectral_forward.1 = (bf16[8,12,24,768]{3,2,1,0:T(8,128)(2,1)}, bf16[12,192,768]{2,1,0:T(8,128)(2,1)}, bf16[12,192,768]{2,1,0:T(8,128)(2,1)}, f32[12,192,768]{2...) custom-call(bf16[12,180,768]{2,1,0:T(8,128)(2,1)} %bitcast.17, ...), custom_call_target="tpu_custom_call" | custom-call | tf_op jit(solution)/shard_map/spectral_forward/pallas_call | solution.py:571
  112.6 133.9 %feed.1 = (bf16[12,180,768]{2,1,0:T(8,128)(2,1)}, f32[12,180,768]{2,1,0:T(8,128)}, bf16[8,12,24,768]{3,2,1,0:T(8,128)(2,1)}, bf16[1536,1536]{1,0:T(8,128)(2,1)},...) custom-call(f32[2,12]{1,0:T(2,128)} %pad_maximum_fusion.scale_ref, ...), custom_call_target="tpu_custom_call" | custom-call | tf_op jit(solution)/shard_map/feed/pallas_call | solution.py:975
  246.5 108.2 %spectral_backward.1 = (bf16[8,12,24,768]{3,2,1,0:T(8,128)(2,1)}, f32[2,8,96,128]{3,2,1,0:T(8,128)}, f32[2,768]{1,0:T(2,128)}, f32[2,8,96,128]{3,2,1,0:T(8,128)}...) custom-call(bf16[8,12,24,768]{3,2,1,0:T(8,128)(2,1)} %get-tuple-eleme, ...), custom_call_target="tpu_custom_call" | custom-call | tf_op jit(solution)/shard_map/spectral_backward/pallas_call | solution.py:710
  354.7 99.3 %leave.1 = (f32[2160,1,768]{2,1,0:T(1,128)}, f32[3584,128]{1,0:T(8,128)}, f32[2,768]{1,0:T(2,128)}, bf16[1536,1536]{1,0:T(8,128)(2,1)}, bf16[3072,768]{1,0:T(8,128)(2,1)}) custom-call(bf16[12,180,768]{2,1,0:T(8,128)(2,1)} %bitcast.19, bf16[8,12,24,768]{3,2,1,0:T(8,128)(2,1)} %get-tuple-element.52.back_ref, ...), custom_call_target="tpu_custom_call" | custom-call | tf_op jit(solution)/shard_map/leave/pallas_call | solution.py:1244
  454.1 1.4 slice_reduce_fusion
  455.4 1.3 slice_bitcast_fusion
  456.8 1.4 slice_bitcast_fusion.1
  458.1 0.8 fusion.1
  458.9 2.6 fusion.2
  461.5 0.7 reshape.79
  462.2 0.7 reshape.77
  462.9 2.8 fusion
  465.7 0.0 slice-start.3
  465.7 0.0 slice-start
  465.7 5.0 %maximum_convert_fusion = f32[768,3072]{1,0:T(8,128)} fusion(bf16[768,1536]{1,0:T(8,128)(2,1)S(1)} %get-tuple-element.73, bf16[768,1536]{1,0:T(8,128)(2,1)S(1)} %get-tuple-element.72), kind=kLoop, calls=%fused_computation | loop fusion | flops 9437184 | bytes 14155776 | tf_op jit(solution)/shard_map/convert_element_type | solution.py:1300
  470.8 0.0 slice-done.2
  470.8 0.0 slice-done.3
  470.8 0.0 slice-start.1
  470.8 5.5 %convert_element_type.23 = f32[3072,768]{1,0:T(8,128)} convert(bf16[3072,768]{1,0:T(8,128)(2,1)S(1)} %bitcast.24) | non-fusion elementwise | flops 2359296 | bytes 14155776 | tf_op jit(solution)/shard_map/convert_element_type | solution.py:1301
  476.3 0.0 copy-done
  476.3 1.7 copy.40
  478.0 0.0 slice-done
  478.1 2.8 copy.41
  (7 shorter events, 0.0 us)
Async XLA Ops:
  462.9 7.9 %slice-start.2 = ((s8[4718592]{0:T(1024)(128)(4,1)}), s8[4194304]{0:T(1024)(128)(4,1)S(1)}, s32[]{:S(2)}) async-start(s8[4718592]{0:T(1024)(128)(4,1)} %bitcast.23), calls=%async_computation.2 | async-start | bytes 8388608
  465.7 5.1 %slice-start.3 = ((s8[4718592]{0:T(1024)(128)(4,1)}), s8[524288]{0:T(1024)(128)(4,1)S(1)}, s32[]{:S(2)}) async-start(s8[4718592]{0:T(1024)(128)(4,1)} %bitcast.23), calls=%async_computation.3 | async-start | bytes 1048576
  465.7 12.3 %slice-start = ((s8[6635520]{0:T(1024)(128)(4,1)}), s8[2441216]{0:T(1024)(128)(4,1)S(1)}, s32[]{:S(2)}) async-start(s8[6635520]{0:T(1024)(128)(4,1)} %bitcast.20), calls=%async_computation | async-start | bytes 4882432
  470.8 5.5 %copy-start = (bf16[12,180,768]{2,1,0:T(8,128)(2,1)S(1)}, bf16[12,180,768]{2,1,0:T(8,128)(2,1)}, u32[]{:S(2)}) copy-start(bf16[12,180,768]{2,1,0:T(8,128)(2,1)} %get-tuple-element.44) | copy-start | bytes 9953284
  470.8 7.3 %slice-start.1 = ((s8[6635520]{0:T(1024)(128)(4,1)}), s8[4194304]{0:T(1024)(128)(4,1)S(1)}, s32[]{:S(2)}) async-start(s8[6635520]{0:T(1024)(128)(4,1)} %bitcast.20), calls=%async_computation.1 | async-start | bytes 8388608

commit v6 on v5

--- a/solution.py
+++ b/solution.py
@@ -1022,7 +1022,7 @@
 ):
     weight_refs, line_refs, refs = refs[:2], refs[2:8], refs[8:]
     (
-        part1_ref, part2_ref, out_ref, sums_ref, norm_ref, dw1_ref, dw2_ref,
+        part1_ref, part2_ref, out_ref, sum1_ref, sum2_ref, sums_ref, norm_ref, dw1_ref, dw2_ref,
         v_ref, slab_s, line_s, mine_s, from_dp, part_s, from_lat, all_s, norm_lat, norm_dp,
         in_send, in_recv, in_own, early_sem, wide_send, wide_recv, own_sem, small_sems,
     ) = refs
@@ -1222,14 +1222,20 @@
         norm_dp[dp] = jnp.sum(norm_lat[...], 0)
         begin(5)
         end(3)
-        sums_ref[...] = all_s[...].astype(F32)
+        at = 0
+        for ref in (sum1_ref, sum2_ref):
+            size = ref.shape[0] * ref.shape[1] * ref.shape[2]
+            value = all_s[at : at + size, :].astype(F32)
+            ref[...] = value.reshape(ref.shape[:3] + (LANES,))[..., : ref.shape[3]]
+            at += size
+        sums_ref[...] = all_s[at : at + sums_ref.shape[0], :].astype(F32)
         for h in range(hops):
             peers(shards, lambda i: incoming(h, i, me, lax.rem(me + i, shards), lambda c: c.wait_send()))
         end(5)
         norm_ref[...] = jnp.sum(norm_dp[...], 0)
 
 
-def leave(x, back, early, mg, fl, gain, small, part1, part2, shapes, groups, plans, modes, collective_id):
+def leave(x, back, early, mg, fl, gain, small, part1, part2, shapes, block, groups, plans, modes, collective_id):
     rows, lon, width = x.shape
     shards, _, slab, _ = back.shape
     hops = hops_of(rows)
@@ -1237,6 +1243,7 @@
     unit = LOW_ROWS * groups * shards
     total = -(-sum(v.size // LANES for v in small) // unit) * unit
     n = total // (groups * shards)
+    lines = up8(sum(v.size // LANES for v in small[2:]))
     row = pl.BlockSpec((1, lon, width), lambda r: (r, 0, 0))
     any_ = pl.BlockSpec(memory_space=pl.ANY)
     whole = lambda *shape: pl.BlockSpec(shape, lambda r: (0,) * len(shape))
@@ -1245,8 +1252,9 @@
         functools.partial(leave_kernel, groups, hops, modes, plans),
         grid=(rows,),
         in_specs=[row, any_, any_, row, full(fl), full(gain)] + [full(v) for v in small] + [any_, any_],
-        out_specs=[pl.BlockSpec((lon, 1, width), lambda r: (r, 0, 0)), whole(total, LANES), whole(2, width), any_, any_],
-        out_shape=[sds((rows * lon, 1, width), F32), sds((total, LANES), F32), sds((2, width), F32)]
+        out_specs=[pl.BlockSpec((lon, 1, width), lambda r: (r, 0, 0)), whole(*block), whole(*block), whole(lines, LANES), whole(2, width), any_, any_],
+        out_shape=[sds((rows * lon, 1, width), F32), sds(block, F32), sds(block, F32)]
+        + [sds((lines, LANES), F32), sds((2, width), F32)]
         + [sds(shape, BF16) for shape in shapes],
         scratch_shapes=[
             pltpu.VMEM((VECTOR_ROWS, width), F32),
@@ -1293,22 +1301,19 @@
         mode_grad, tb, outer_weight, inner_weight, freq, hid, gp, t2, dw1, dw2, groups, plans, 2
     )
     small = (dwi, dwo, dbi, dbo, dpg, dps, deb, drb)
-    input_grad, sums, norm, dw1, dw2 = leave(
+    input_grad, dwi, dwo, sums, norm, dw1, dw2 = leave(
         x, slab_grad, early, mixed_grad, tb["fl"], norm_gain, small, part1, part2,
-        (dw1.shape, dw2.shape), groups, plans, modes, 3
+        (dw1.shape, dw2.shape), inner_weight.shape, groups, plans, modes, 3
     )
     dw1 = jnp.concatenate([dw1[:width], dw1[width:]], 1).astype(F32)
     dw2 = dw2.astype(F32)
+    small = small[2:]
     ends = np.cumsum([v.size // LANES for v in small])
-    dwi, dwo, dbi, dbo, dpg, dps, deb, drb = [
-        sums[e - v.size // LANES : e] for v, e in zip(small, ends)
-    ]
-    block = inner_weight.shape[-1]
-    weight = lambda v: v.reshape(inner_weight.shape[:3] + (LANES,))[..., :block]
+    dbi, dbo, dpg, dps, deb, drb = [sums[e - v.size // LANES : e] for v, e in zip(small, ends)]
     line = lambda v: v.reshape(-1)
     return (
         layer_out[None], input_grad.reshape(1, rows, lon, width), norm[0], norm[1],
-        weight(dwi), dbi.reshape(inner_bias.shape), weight(dwo), dbo.reshape(outer_bias.shape),
+        dwi, dbi.reshape(inner_bias.shape), dwo, dbo.reshape(outer_bias.shape),
         line(dpg), line(dps), dw1, line(deb), dw2, line(drb),
     )
 

time: 482 us -> 481 us (level)
  no operation moved by 1% of the time
where the time goes in v6:
time: 481 us; the launch traced here: 480 us
  Pallas kernels  452 us (94%)
  local copies, waits for them, and re-layouts  15.4 us (3%)
  other arithmetic  11.1 us (2%)
    pallas_call x1, Pallas kernels, feed(): pl.pallas_call(functools.partial(feed_kernel, per, chunk, hops, modes), g...  134 us
    pallas_call x1, Pallas kernels, spectral_forward(): pl.pallas_call(functools.partial(spectral_forward_kernel, hops), grid=(GR...  111 us
    pallas_call x1, Pallas kernels, spectral_backward(): pl.pallas_call(functools.partial(spectral_backward_kernel, groups, plans)...  108 us
    pallas_call x1, Pallas kernels, leave(): pl.pallas_call(functools.partial(leave_kernel, groups, hops, modes, plans...  99.2 us

profile of v6, /device:TPU:0, one launch (start us, length us, event | category | flops | bytes accessed | tf_op | source)
XLA Modules:
  0.0 480.0 jit_solution(17365119959153916907)
XLA Ops:
  1.3 0.6 pad_maximum_fusion.scale_ref
  1.9 110.8 %spectral_forward.1 = (bf16[8,12,24,768]{3,2,1,0:T(8,128)(2,1)}, bf16[12,192,768]{2,1,0:T(8,128)(2,1)}, bf16[12,192,768]{2,1,0:T(8,128)(2,1)}, f32[12,192,768]{2...) custom-call(bf16[12,180,768]{2,1,0:T(8,128)(2,1)} %bitcast.13, ...), custom_call_target="tpu_custom_call" | custom-call | tf_op jit(solution)/shard_map/spectral_forward/pallas_call | solution.py:571
  112.7 133.9 %feed.1 = (bf16[12,180,768]{2,1,0:T(8,128)(2,1)}, f32[12,180,768]{2,1,0:T(8,128)}, bf16[8,12,24,768]{3,2,1,0:T(8,128)(2,1)}, bf16[1536,1536]{1,0:T(8,128)(2,1)},...) custom-call(f32[2,12]{1,0:T(2,128)} %pad_maximum_fusion.scale_ref, ...), custom_call_target="tpu_custom_call" | custom-call | tf_op jit(solution)/shard_map/feed/pallas_call | solution.py:975
  246.6 108.2 %spectral_backward.1 = (bf16[8,12,24,768]{3,2,1,0:T(8,128)(2,1)}, f32[2,8,96,128]{3,2,1,0:T(8,128)}, f32[2,768]{1,0:T(2,128)}, f32[2,8,96,128]{3,2,1,0:T(8,128)}...) custom-call(bf16[8,12,24,768]{3,2,1,0:T(8,128)(2,1)} %get-tuple-eleme, ...), custom_call_target="tpu_custom_call" | custom-call | tf_op jit(solution)/shard_map/spectral_backward/pallas_call | solution.py:710
  354.8 99.2 %leave.1 = (f32[2160,1,768]{2,1,0:T(1,128)}, f32[2,8,96,96]{3,2,1,0:T(8,128)}, f32[2,8,96,96]{3,2,1,0:T(8,128)}, f32[72,128]{1,0:T(8,128)}, f32[2,768]{1,0:T(2,1...) custom-call(bf16[12,180,768]{2,1,0:T(8,128)(2,1)} %bitcast.15, ...), custom_call_target="tpu_custom_call" | custom-call | tf_op jit(solution)/shard_map/leave/pallas_call | solution.py:1251
  454.0 1.4 slice_reduce_fusion
  455.4 1.3 slice_bitcast_fusion
  456.7 1.4 slice_bitcast_fusion.1
  458.1 0.8 fusion.1
  458.9 0.7 reshape.71
  459.6 0.7 reshape.70
  460.2 2.8 fusion
  463.1 0.0 slice-start.3
  463.1 0.0 slice-start
  463.1 5.0 %maximum_convert_fusion = f32[768,3072]{1,0:T(8,128)} fusion(bf16[768,1536]{1,0:T(8,128)(2,1)S(1)} %get-tuple-element.77, bf16[768,1536]{1,0:T(8,128)(2,1)S(1)} %get-tuple-element.76), kind=kLoop, calls=%fused_computation | loop fusion | flops 9437184 | bytes 14155776 | tf_op jit(solution)/shard_map/convert_element_type | solution.py:1308
  468.1 0.0 slice-done.2
  468.1 0.0 slice-start.1
  468.1 5.5 %convert_element_type.23 = f32[3072,768]{1,0:T(8,128)} convert(bf16[3072,768]{1,0:T(8,128)(2,1)S(1)} %bitcast.20) | non-fusion elementwise | flops 2359296 | bytes 14155776 | tf_op jit(solution)/shard_map/convert_element_type | solution.py:1309
  473.7 1.7 copy.42
  475.4 0.0 slice-done.1
  475.4 0.0 copy-start.1
  475.4 2.8 copy.43
  478.3 0.9 copy.44
  479.1 0.9 copy.45
  (12 shorter events, 0.0 us)
Async XLA Ops:
  460.2 7.9 %slice-start.2 = ((s8[4718592]{0:T(1024)(128)(4,1)}), s8[4194304]{0:T(1024)(128)(4,1)S(1)}, s32[]{:S(2)}) async-start(s8[4718592]{0:T(1024)(128)(4,1)} %bitcast.19), calls=%async_computation.2 | async-start | bytes 8388608
  463.1 5.1 %slice-start.3 = ((s8[4718592]{0:T(1024)(128)(4,1)}), s8[524288]{0:T(1024)(128)(4,1)S(1)}, s32[]{:S(2)}) async-start(s8[4718592]{0:T(1024)(128)(4,1)} %bitcast.19), calls=%async_computation.3 | async-start | bytes 1048576
  463.1 12.3 %slice-start = ((s8[6635520]{0:T(1024)(128)(4,1)}), s8[2441216]{0:T(1024)(128)(4,1)S(1)}, s32[]{:S(2)}) async-start(s8[6635520]{0:T(1024)(128)(4,1)} %bitcast.16), calls=%async_computation | async-start | bytes 4882432
  468.1 5.5 %copy-start = (bf16[12,180,768]{2,1,0:T(8,128)(2,1)S(1)}, bf16[12,180,768]{2,1,0:T(8,128)(2,1)}, u32[]{:S(2)}) copy-start(bf16[12,180,768]{2,1,0:T(8,128)(2,1)} %get-tuple-element.46) | copy-start | bytes 9953284
  468.1 7.3 %slice-start.1 = ((s8[6635520]{0:T(1024)(128)(4,1)}), s8[4194304]{0:T(1024)(128)(4,1)S(1)}, s32[]{:S(2)}) async-start(s8[6635520]{0:T(1024)(128)(4,1)} %bitcast.16), calls=%async_computation.1 | async-start | bytes 8388608
  475.4 2.8 copy-start.2
  475.4 3.7 copy-start.1
